TPU v7x, 32 devices: a whole 2x2x4 slice. The times are simulated.
32 devices in a mesh: wide: 16 (over z, y, core), narrow: 2 (over x).
Axes of the slice: x: 2, y: 2, z: 4, core: 2. Of those that a mesh axis runs over, the one named last changes fastest.
Arguments:
- spin: float32 [3, 32, 32, 256], P(None, None, 'wide', 'narrow'), may hold values from -1 to 1, as said below
- region: int32 [32, 32, 256], P(None, 'wide', 'narrow'), may hold values 0 or 1
- material: int32 [32, 32, 256], P(None, 'wide', 'narrow'), may hold values from 0 to 3
- saturation: float32 [4], replicated, may hold values from 0.5 to 2
- anisotropy: float32 [4], replicated, may hold values from 0.2 to 1
- damping: float32 [4], replicated, may hold values from 0.05 to 0.5
- applied: float32 [3], replicated, may hold values from -3 to 3
- demag_spectrum: bfloat16 [6, 64, 64, 512], P(None, 'wide', 'narrow'), may hold values from -2.5 to 2.5, as said below
Outputs:
- rate: float32 [3, 32, 32, 256], P(None, None, 'wide', 'narrow')
- demag_field: float32 [3, 32, 32, 256], P(None, None, 'wide', 'narrow')
Inputs may be any that keep to these rules, and one draw needn't show every extreme that they name: `spin`: every cell's three components form a unit vector. `demag_spectrum`: every component is unchanged when all three wave numbers are replaced by their negatives modulo 64, 64, 512.
All inputs are finite; a program needn't handle non-finite values. No bound on the sum of `region` on one device may be relied on, other than what follows from the above.
Results may differ from a plain program's by a relative error of at most 0.0003.
Values sent between devices are 32-bit elements; how exact they have to be, the bound alone decides.
No kernel may reach another device: no remote copies, remote signals or barrier semaphores. Data moves between devices by JAX's collectives and lax.ppermute only.
A program may use at most 64 MiB of HBM per device.

v0:
```python
from functools import partial
import math

import jax
import jax.numpy as jnp
import numpy as np
from jax import lax
from jax.experimental import pallas as pl
from jax.experimental.pallas import tpu as pltpu
from jax.sharding import PartitionSpec as P

exchange_coef = 0.3
highest = lax.Precision.HIGHEST


def extended(x, sides, width):
    for axis, dim in sides:
        peers, length = (lax.axis_size(axis), x.shape[dim])
        up = [(i, (i + 1) % peers) for i in range(peers - 1)]
        down = [(j, i) for i, j in up]
        last = lax.slice_in_dim(x, length - width, length, axis=dim)
        leading = lax.slice_in_dim(x, 0, width, axis=dim)
        before = lax.ppermute(last, axis, up)
        after = lax.ppermute(leading, axis, down)
        x = jnp.concatenate([before, x, after], axis=dim)
    return x


def phase_table(rows_count, cols_count, length, sign):
    left_index = lax.broadcasted_iota(jnp.int32, (rows_count, cols_count), 0)
    right_index = lax.broadcasted_iota(jnp.int32, (rows_count, cols_count), 1)
    angle = (left_index * right_index % length).astype(jnp.float32) * (2.0 * math.pi / length)
    return (jnp.cos(angle), sign * jnp.sin(angle))


def contract(pattern, phases, values):
    phase_re, phase_im = phases
    value_re, value_im = values
    product = partial(jnp.einsum, pattern, precision=highest)
    if value_im is None:
        return (product(phase_re, value_re), product(phase_im, value_re))
    return (
        product(phase_re, value_re) - product(phase_im, value_im),
        product(phase_re, value_im) + product(phase_im, value_re),
    )


def factors(half_size, at_end):
    if at_end:
        inner_size = math.gcd(half_size, 128)
    else:
        inner_size = max(
            (
                divisor
                for divisor in range(1, half_size + 1)
                if half_size % divisor == 0 and divisor * divisor <= 2 * half_size
            )
        )
    return (inner_size, 2 * half_size // inner_size)


def forward(values, at_end, natural):
    value_re, value_im = values
    extent = value_re.shape
    half_size = extent[1]
    length = 2 * half_size
    inner_size, outer_size = factors(half_size, at_end)
    tail_index = "" if at_end else "b"
    blocked = (extent[0], outer_size // 2, inner_size) + extent[2:]
    value_re = value_re.reshape(blocked)
    value_im = None if value_im is None else value_im.reshape(blocked)
    phases = phase_table(outer_size, outer_size // 2, outer_size, -1.0)
    work_re, work_im = contract(
        "kn,anp" + tail_index + "->akp" + tail_index, phases, (value_re, value_im)
    )
    twist_re, twist_im = phase_table(outer_size, inner_size, length, -1.0)
    if not at_end:
        twist_re, twist_im = (twist_re[:, :, None], twist_im[:, :, None])
    work_re, work_im = (
        work_re * twist_re - work_im * twist_im,
        work_re * twist_im + work_im * twist_re,
    )
    target = "ajk" if natural else "akj"
    phases = phase_table(inner_size, inner_size, inner_size, -1.0)
    out_re, out_im = contract(
        "jp,akp" + tail_index + "->" + target + tail_index, phases, (work_re, work_im)
    )
    merged = (extent[0], length) + extent[2:]
    return (out_re.reshape(merged), out_im.reshape(merged))


def inverse(values, at_end, natural, real_only):
    value_re, value_im = values
    extent = value_re.shape
    length = extent[1]
    half_size = length // 2
    inner_size, outer_size = factors(half_size, at_end)
    tail_index = "" if at_end else "b"
    if natural:
        blocked = (extent[0], inner_size, outer_size) + extent[2:]
        source = "ajk"
    else:
        blocked = (extent[0], outer_size, inner_size) + extent[2:]
        source = "akj"
    phases = phase_table(inner_size, inner_size, inner_size, 1.0)
    work_re, work_im = contract(
        "pj," + source + tail_index + "->akp" + tail_index,
        phases,
        (value_re.reshape(blocked), value_im.reshape(blocked)),
    )
    twist_re, twist_im = phase_table(outer_size, inner_size, length, 1.0)
    if not at_end:
        twist_re, twist_im = (twist_re[:, :, None], twist_im[:, :, None])
    work_re, work_im = (
        work_re * twist_re - work_im * twist_im,
        work_re * twist_im + work_im * twist_re,
    )
    phases = phase_table(outer_size // 2, outer_size, outer_size, 1.0)
    pattern = "nk,akp" + tail_index + "->anp" + tail_index
    scale = 1.0 / length
    merged = (extent[0], half_size) + extent[2:]
    if real_only:
        product = partial(jnp.einsum, pattern, precision=highest)
        result = product(phases[0], work_re) - product(phases[1], work_im)
        return result.reshape(merged) * scale
    out_re, out_im = contract(pattern, phases, (work_re, work_im))
    return (out_re.reshape(merged) * scale, out_im.reshape(merged) * scale)


def along_x(pieces):
    piece_re, piece_im = pieces
    members, planes, cells_x, cells_y = piece_re.shape
    extent = (members * planes, cells_x, cells_y)
    out_re, out_im = forward((piece_re.reshape(extent), piece_im.reshape(extent)), False, True)
    merged = (members, planes, 2 * cells_x, cells_y)
    return (out_re.reshape(merged), out_im.reshape(merged))


def along_y(pieces):
    piece_re, piece_im = pieces
    members, planes, rows_x, cells_y = piece_re.shape
    extent = (members * planes * rows_x, cells_y)
    out_re, out_im = forward((piece_re.reshape(extent), piece_im.reshape(extent)), True, False)
    merged = (members, planes, rows_x, 2 * cells_y)
    return (out_re.reshape(merged), out_im.reshape(merged))


def back_to_bricks(field_re, field_im):
    members, planes, rows_x, length_y = field_re.shape
    flattened = (members * planes * rows_x, length_y)
    grid_re, grid_im = inverse(
        (field_re.reshape(flattened), field_im.reshape(flattened)), True, False, False
    )
    merged = (members, planes, rows_x, length_y // 2)
    piece_re = lax.all_to_all(
        grid_re.reshape(merged), "narrow", split_axis=3, concat_axis=2, tiled=True
    )
    piece_im = lax.all_to_all(
        grid_im.reshape(merged), "narrow", split_axis=3, concat_axis=2, tiled=True
    )
    members, planes, length_x, cells_y = piece_re.shape
    extent = (members * planes, length_x, cells_y)
    out_re, out_im = inverse(
        (piece_re.reshape(extent), piece_im.reshape(extent)), False, True, False
    )
    invert_merged = (members, planes, length_x // 2, cells_y)
    columns = (out_re.reshape(invert_merged), out_im.reshape(invert_merged))
    piece_re, piece_im = lax.all_to_all(columns, "wide", split_axis=2, concat_axis=1, tiled=True)
    members, planes, cells_x, cells_y = piece_re.shape
    extent = (members, planes, cells_x * cells_y)
    result = inverse((piece_re.reshape(extent), piece_im.reshape(extent)), False, True, True)
    merged = (members, planes // 2, cells_x, cells_y)
    return result.reshape(merged)


def couple(kernel, values, picks):
    return -(
        kernel[picks[0]] * values[0] + kernel[picks[1]] * values[1] + kernel[picks[2]] * values[2]
    )


def cross(left, right):
    return jnp.stack(
        [
            left[1] * right[2] - left[2] * right[1],
            left[2] * right[0] - left[0] * right[2],
            left[0] * right[1] - left[1] * right[0],
        ]
    )


def general_shards(spin, region, material, saturation, anisotropy, damping, applied, demag_spectrum):
    magnet = region.astype(jnp.float32)
    direction = spin * magnet[None]
    species = saturation.shape[0]
    chosen = (
        material[None] == lax.broadcasted_iota(jnp.int32, (species,) + material.shape, 0)
    ).astype(jnp.float32)

    def lookup(entries):
        return jnp.sum(chosen * entries[:, None, None, None], axis=0)

    sat_cell = lookup(saturation)
    anis_cell = lookup(anisotropy)
    damp_cell = lookup(damping)
    moment = direction * sat_cell[None]
    components, layers, width_x, width_y = spin.shape
    flattened = moment.reshape(components, layers, width_x * width_y)
    spec_re, spec_im = forward((flattened, None), False, True)
    stacked = (components, 2 * layers, width_x, width_y)
    spectra = along_x(
        (
            lax.all_to_all(
                spec_re.reshape(stacked), "wide", split_axis=1, concat_axis=2, tiled=True
            ),
            lax.all_to_all(
                spec_im.reshape(stacked), "wide", split_axis=1, concat_axis=2, tiled=True
            ),
        )
    )
    spec_re, spec_im = along_y(
        lax.all_to_all(spectra, "narrow", split_axis=2, concat_axis=3, tiled=True)
    )
    parts, planes, rows_x, length_y = demag_spectrum.shape
    inner_size, outer_size = factors(length_y // 2, True)
    kernel = demag_spectrum.reshape(parts, planes, rows_x, inner_size, outer_size)
    kernel = (
        kernel.transpose(0, 1, 2, 4, 3).reshape(parts, planes, rows_x, length_y).astype(jnp.float32)
    )
    couplings = ((0, 3, 4), (3, 1, 5), (4, 5, 2))
    field_re = [couple(kernel, spec_re, picks) for picks in couplings]
    field_im = [couple(kernel, spec_im, picks) for picks in couplings]
    demag = back_to_bricks(jnp.stack(field_re), jnp.stack(field_im))
    framed = extended(direction, (("wide", 2), ("narrow", 3)), 1)
    framed = jnp.pad(framed, ((0, 0), (1, 1), (0, 0), (0, 0)))
    weight = jnp.sum(framed * framed, axis=0)
    neighbours = (
        framed[:, 2:, 1:-1, 1:-1]
        + framed[:, :-2, 1:-1, 1:-1]
        + framed[:, 1:-1, 2:, 1:-1]
        + framed[:, 1:-1, :-2, 1:-1]
        + framed[:, 1:-1, 1:-1, 2:]
        + framed[:, 1:-1, 1:-1, :-2]
    )
    present = (
        weight[2:, 1:-1, 1:-1]
        + weight[:-2, 1:-1, 1:-1]
        + weight[1:-1, 2:, 1:-1]
        + weight[1:-1, :-2, 1:-1]
        + weight[1:-1, 1:-1, 2:]
        + weight[1:-1, 1:-1, :-2]
    )
    laplace = neighbours - present[None] * direction
    zeros = jnp.zeros_like(sat_cell)
    uniaxial = jnp.stack([zeros, zeros, 2.0 * anis_cell / sat_cell * direction[2]])
    field = (
        exchange_coef * laplace / sat_cell[None] + demag + applied[:, None, None, None] + uniaxial
    )
    torque = cross(direction, field)
    rate = (
        -(torque + damp_cell[None] * cross(direction, torque)) / (1.0 + damp_cell * damp_cell)[None]
    )
    return (rate, demag)


def split_table(table):
    high = jnp.asarray(np.asarray(table, np.float32)).astype(jnp.bfloat16)
    high64 = np.asarray(np.asarray(table, np.float32).astype(high.dtype), np.float64)
    low = (table - high64).astype(np.float32).astype(high.dtype)
    return np.asarray(high64.astype(high.dtype)), low


class Plan:
    def __init__(self, wide, narrow, layers, width_x, width_y, planes, rows_x, length_y):
        self.wide, self.narrow = wide, narrow
        self.layers, self.width_x, self.width_y = layers, width_x, width_y
        self.planes, self.rows_x = planes, rows_x
        self.length_z, self.length_x, self.length_y = planes * wide, rows_x * narrow, length_y
        self.cells_x, self.cells_y = width_x * wide, width_y * narrow
        self.devices = wide * narrow
        self.special = self.narrow * (wide // 2) + 1

    def fits(self):
        return (
            self.narrow == 2
            and self.planes == 4
            and self.wide % 16 == 0
            and self.devices * 2 == self.length_z
            and self.length_z == 2 * self.layers
            and self.length_x == 2 * self.cells_x
            and self.length_y == 2 * self.cells_y
            and self.width_x == 2
            and self.width_y % 128 == 0
            and self.rows_x % 16 == 0
            and (self.layers * self.width_x) % 8 == 0
            and 6 * self.rows_x == 3 * self.layers * self.width_x
        )

    def wave(self):
        w, n = np.divmod(np.arange(self.devices), self.narrow)
        return self.planes * w + np.where(w < self.wide // 2, 1 + n, 1 - n)

    def thickness_tables(self):
        wave = self.wave()
        z = np.arange(self.layers)
        angle = 2.0 * np.pi * ((wave[:, None] * z[None]) % self.length_z) / self.length_z
        ahead = np.stack([np.cos(angle), -np.sin(angle)], 1)
        back = np.stack([2.0 * np.cos(angle), -2.0 * np.sin(angle)], 1)
        ahead[self.special, 1] = 1.0
        back[self.special, 0] = np.cos(angle[self.special])
        back[self.special, 1] = 1.0
        back *= -1.0 / (self.length_z * self.length_x * self.length_y)
        n = np.arange(self.devices) % self.narrow
        x = np.arange(self.width_x)
        sign = 1.0 - 2.0 * ((n[:, None] * x[None]) % 2)
        unit_c, unit_x = np.eye(3), np.eye(self.width_x)
        ahead = np.einsum("drz,dx,cb,xv->dcrxbzv", ahead, sign, unit_c, unit_x)
        back = np.einsum("drz,dx,cb,xv->bzvdcrx", back, sign, unit_c, unit_x)
        count = self.devices * 6 * self.width_x
        cells = 3 * self.layers * self.width_x
        return ahead.reshape(count, cells), back.reshape(cells, count)

    def lateral_tables(self):
        half = self.cells_y
        y, k = np.arange(half), np.arange(half)
        angle = 2.0 * np.pi * ((y[:, None] * k[None]) % self.length_y) / self.length_y
        cosine, sine = np.cos(angle), np.sin(angle)
        sine[:, 0] = 1.0 - 2.0 * (y % 2)
        ahead_y = np.concatenate([cosine, sine], 1)
        back_y = np.ascontiguousarray(ahead_y.T)
        x = (np.arange(self.wide)[None] * self.width_x + np.arange(self.width_x)[:, None]).reshape(-1)
        kx = np.arange(self.length_x)
        angle = 2.0 * np.pi * ((kx[:, None] * x[None]) % self.length_x) / self.length_x
        cosine, sine = np.cos(angle), np.sin(angle)
        ahead_x = np.concatenate([cosine, sine], 0)
        back_x = np.block([[cosine.T, -sine.T], [sine.T, cosine.T]])
        flip = np.zeros((half, half))
        flip[(half - k) % half, k] = 1.0
        return ahead_y, back_y, ahead_x, back_x, flip


def halves(value):
    high = value.astype(jnp.bfloat16)
    return high, (value - high.astype(jnp.float32)).astype(jnp.bfloat16)


def mul(left, right):
    return jnp.dot(left, right, preferred_element_type=jnp.float32)


def pick(material, entries, species):
    value = jnp.zeros(material.shape, jnp.float32)
    for s in range(species):
        value = jnp.where(material == s, entries[s], value)
    return value


def rows_of(plan):
    w, n = lax.axis_index("wide"), lax.axis_index("narrow")
    low = w < plan.wide // 2
    own = jnp.where(low, 1 + n, 1 - n)
    other = jnp.where(low, 2 - n, n)
    return w, n, own, other


def first_kernel(plan, species, spin, region, material, saturation, t_high, t_low, tensor,
                 out, up, down, swap, zero, turned, held, held0, sems):
    w, n, own, other = rows_of(plan)
    fetch = pltpu.make_async_copy(tensor.at[:, other], held, sems.at[0])
    fetch.start()
    fetch0 = pltpu.make_async_copy(tensor.at[:, 0], held0, sems.at[1])
    fetch0.start()
    cells = plan.layers * plan.width_x
    magnet = region[...].astype(jnp.float32)
    sat = pick(material[...], saturation, species)
    high, low = [], []
    for c in range(3):
        direction = spin[c * cells : (c + 1) * cells, :] * magnet
        turned[c * cells : (c + 1) * cells, :] = direction
        a, b = halves(direction * sat)
        high.append(a)
        low.append(b)
    high, low = jnp.concatenate(high, 0), jnp.concatenate(low, 0)
    out[...] = mul(t_high[...], high) + (mul(t_low[...], high) + mul(t_high[...], low))
    count = 3 * plan.layers
    up[...] = turned[pl.ds(1, count, stride=2), :]
    down[...] = turned[pl.ds(0, count, stride=2), :]
    swap[:, plan.length_y :] = turned[...]
    fetch.wait()
    fetch0.wait()
    for t in range(6):
        rows = slice(t * plan.rows_x, (t + 1) * plan.rows_x)
        swap[rows, : plan.length_y] = held[t].astype(jnp.float32)
    @pl.when(w == 0)
    def _():
        for t in range(6):
            rows = slice(t * plan.rows_x, (t + 1) * plan.rows_x)
            zero[rows, :] = held0[t].astype(jnp.float32)


def tensor_kernel(plan, swapped, zero_a, zero_b, flip, tensor, full, held, sems):
    w, n, own, other = rows_of(plan)
    fetch = pltpu.make_async_copy(tensor.at[:, own], held, sems.at[0])
    fetch.start()
    half, count = plan.cells_y, plan.rows_x
    special = jnp.logical_and(w == plan.wide // 2, n == 1)

    def place(slot, part, t, values):
        rows = slice(part * count, (part + 1) * count)
        full[slot, t, rows, :half] = values[:, :half].astype(jnp.float32)
        full[slot, t, rows, half:] = mul(values[:, half:].astype(jnp.bfloat16), flip[...])

    for t in range(6):
        place(0, 1, t, swapped[t * count : (t + 1) * count, : plan.length_y])
    @pl.when(special)
    def _():
        for t in range(6):
            place(1, 0, t, zero_b[t * count : (t + 1) * count, :])
            place(1, 1, t, zero_a[t * count : (t + 1) * count, :])
    fetch.wait()
    for t in range(6):
        place(0, 0, t, held[t])


COUPLINGS = ((0, 3, 4), (3, 1, 5), (4, 5, 2))


def plane_kernel(plan, got, y_high, y_low, x_ahead, xb_pair, xb_low, yb_high, yb_low, full,
                 out, mixed, packed, spread):
    w, n, own, other = rows_of(plan)
    special = jnp.logical_and(w == plan.wide // 2, n == 1)
    slot = special.astype(jnp.int32)
    lanes, half, wide = plan.width_y, plan.cells_y, plan.wide
    cells_x, length_x = plan.cells_x, plan.length_x
    block = 6 * plan.width_x
    per_c = 2 * cells_x
    narrow = plan.narrow
    lines = []
    for c in range(3):
        for j in range(2 * plan.width_x):
            row = c * 2 * plan.width_x + j
            lines.append(jnp.concatenate(
                [got[pl.ds(m * block + row, wide, stride=narrow * block), :] for m in range(narrow)], 1))
    lines = jnp.concatenate(lines, 0)
    high, low = halves(lines)
    waves = mul(high, y_high[...]) + (mul(low, y_high[...]) + mul(high, y_low[...]))
    for g in range(6):
        a, b = halves(waves[g * cells_x : (g + 1) * cells_x, :])
        mixed[g] = mul(x_ahead[...], jnp.concatenate([a, b, a], 0))
    step = 16
    for lane in range(0, half, 128):
        for row in range(0, length_x, step):
            left = slice(lane, lane + 128)
            right = slice(half + lane, half + lane + 128)
            cr, sr = slice(row, row + step), slice(length_x + row, length_x + row + step)
            fields = []
            for g in range(6):
                cp, sp = mixed[g, cr, left], mixed[g, sr, left]
                cq, sq = mixed[g, cr, right], mixed[g, sr, right]
                if lane == 0:
                    edge = lax.broadcasted_iota(jnp.int32, cp.shape, 1) == 0
                    cq0, sq0 = jnp.where(edge, 0.0, cq), jnp.where(edge, 0.0, sq)
                    fields.append((cp - sq0, -(sp + cq0),
                                   jnp.where(edge, cq, cp + sq), jnp.where(edge, -sq, cq - sp)))
                else:
                    fields.append((cp - sq, -(sp + cq), cp + sq, cq - sp))
            for i in range(3):
                sums = []
                for s, lanes_at in ((0, left), (2, right)):
                    real = imag = None
                    for j in range(3):
                        t = COUPLINGS[i][j]
                        ka = full[0, t, cr, lanes_at]
                        kb = full[slot, t, cr, lanes_at]
                        a, b = fields[2 * j], fields[2 * j + 1]
                        re = ka * a[s] - kb * b[s + 1]
                        im = ka * a[s + 1] + kb * b[s]
                        real = re if real is None else real + re
                        imag = im if imag is None else imag + im
                    sums.append((real, imag))
                (pr, pi), (mr, mi) = sums
                even_re, even_im, odd_re, odd_im = pr + mr, pi + mi, mi - pi, pr - mr
                if lane == 0:
                    even_re, even_im = jnp.where(edge, pr, even_re), jnp.where(edge, pi, even_im)
                    odd_re, odd_im = jnp.where(edge, mr, odd_re), jnp.where(edge, mi, odd_im)
                for value, at, lanes_at in (
                    (even_re, 0, left), (even_im, length_x, left),
                    (odd_re, 0, right), (odd_im, length_x, right),
                ):
                    a, b = halves(value)
                    packed[i, at + row : at + row + step, lanes_at] = a
                    packed[i, 2 * length_x + at + row : 2 * length_x + at + row + step, lanes_at] = b
    back = []
    for i in range(3):
        back.append(mul(xb_pair[...], packed[i]) + mul(xb_low[...], packed[i, : 2 * length_x, :]))
    high, low = halves(jnp.concatenate(back, 0))
    result = mul(high, yb_high[...]) + (mul(low, yb_high[...]) + mul(high, yb_low[...]))
    for c in range(3):
        for j in range(2 * plan.width_x):
            row = c * 2 * plan.width_x + j
            for m in range(narrow):
                out[pl.ds(m * block + row, wide, stride=narrow * block), :] = result[
                    row * wide : (row + 1) * wide, m * lanes : (m + 1) * lanes]


def local_kernel(plan, species, turned, side, before, after, material, saturation, anisotropy,
                 applied, out, woven):
    n = lax.axis_index("narrow")
    cells, layers = plan.layers * plan.width_x, plan.layers
    row = lax.broadcasted_iota(jnp.int32, (cells, plan.width_y), 0)
    col = lax.broadcasted_iota(jnp.int32, (cells, plan.width_y), 1)
    first, last = col == 0, col == plan.width_y - 1
    even = row % 2 == 0
    ahead = jnp.where(n == 0, 1.0, 0.0)
    sat = pick(material[...], saturation, species)
    anis = pick(material[...], anisotropy, species)
    sums, present, own = [], jnp.zeros((cells, plan.width_y), jnp.float32), []
    for c in range(3):
        d = turned[c * cells : (c + 1) * cells, :]
        s = side[c * cells : (c + 1) * cells, :]
        woven[pl.ds(0, layers, stride=2), :] = before[c * layers : (c + 1) * layers, :]
        woven[pl.ds(1, layers, stride=2), :] = after[c * layers : (c + 1) * layers, :]
        near = (
            jnp.where(row >= 2, pltpu.roll(d, 2, 0), 0.0),
            jnp.where(row < cells - 2, pltpu.roll(d, cells - 2, 0), 0.0),
            woven[...],
            jnp.where(even, pltpu.roll(d, cells - 1, 0), pltpu.roll(d, 1, 0)),
            pltpu.roll(jnp.where(first, s * ahead, d), plan.width_y - 1, 1),
            pltpu.roll(jnp.where(last, s * (1.0 - ahead), d), 1, 1),
        )
        total = near[0]
        present = present + near[0] * near[0]
        for v in near[1:]:
            total = total + v
            present = present + v * v
        sums.append(total)
        own.append(d)
    for c in range(3):
        field = exchange_coef * (sums[c] - present * own[c]) / sat + applied[c]
        if c == 2:
            field = field + 2.0 * anis / sat * own[2]
        out[c * cells : (c + 1) * cells, :] = field


def last_kernel(plan, species, got, t_high, t_low, base, turned, material, damping, rate, demag):
    cells = plan.layers * plan.width_x
    high, low = halves(got[...])
    demag[...] = mul(t_high[...], high) + (mul(t_low[...], high) + mul(t_high[...], low))
    damp = pick(material[...], damping, species)
    d = [turned[c * cells : (c + 1) * cells, :] for c in range(3)]
    f = [demag[c * cells : (c + 1) * cells, :] + base[c * cells : (c + 1) * cells, :] for c in range(3)]

    def turn(u, v):
        return [u[1] * v[2] - u[2] * v[1], u[2] * v[0] - u[0] * v[2], u[0] * v[1] - u[1] * v[0]]

    torque = turn(d, f)
    again = turn(d, torque)
    scale = -1.0 / (1.0 + damp * damp)
    for c in range(3):
        rate[c * cells : (c + 1) * cells, :] = (torque[c] + damp * again[c]) * scale


VMEM = pl.BlockSpec(memory_space=pltpu.VMEM)
SMEM = pl.BlockSpec(memory_space=pltpu.SMEM)
ANY = pl.BlockSpec(memory_space=pl.ANY)


def plane_shards(plan, spin, region, material, saturation, anisotropy, damping, applied, demag_spectrum):
    f32, bf16 = jnp.float32, jnp.bfloat16
    cells, lanes = plan.layers * plan.width_x, plan.width_y
    count, length_y, length_x = plan.devices * 6 * plan.width_x, plan.length_y, plan.length_x
    species = saturation.shape[0]
    shape = jax.ShapeDtypeStruct
    spin2 = spin.reshape(3 * cells, lanes)
    region2, material2 = region.reshape(cells, lanes), material.reshape(cells, lanes)
    ahead_z, back_z = plan.thickness_tables()
    ahead_y, back_y, ahead_x, back_x, flip = plan.lateral_tables()
    az, bz, ay, by = (split_table(t) for t in (ahead_z, back_z, ahead_y, back_y))
    ax, bx = split_table(ahead_x), split_table(back_x)
    x_ahead = np.concatenate([ax[0], ax[0], ax[1]], 1)
    xb_pair = np.concatenate([bx[0], bx[0]], 1)

    def call(body, out_shape, in_specs, out_specs, scratch, flops, limit=24 << 20):
        return pl.pallas_call(
            body, out_shape=out_shape, in_specs=in_specs, out_specs=out_specs, scratch_shapes=scratch,
            compiler_params=pltpu.CompilerParams(vmem_limit_bytes=limit),
            cost_estimate=pl.CostEstimate(flops=flops, bytes_accessed=1 << 20, transcendentals=0),
        )

    rows6 = 6 * plan.rows_x
    out, up, down, swap, zero, turned = call(
        partial(first_kernel, plan, species),
        (shape((count, lanes), f32), shape((3 * plan.layers, lanes), f32), shape((3 * plan.layers, lanes), f32),
         shape((rows6, length_y + lanes), f32), shape((rows6, length_y), f32), shape((3 * cells, lanes), f32)),
        [VMEM, VMEM, VMEM, SMEM, VMEM, VMEM, ANY],
        (VMEM,) * 6,
        [pltpu.VMEM((6, plan.rows_x, length_y), bf16), pltpu.VMEM((6, plan.rows_x, length_y), bf16),
         pltpu.SemaphoreType.DMA((2,))],
        1 << 28,
    )(spin2, region2, material2, saturation, jnp.asarray(az[0]), jnp.asarray(az[1]), demag_spectrum)

    both = ("wide", "narrow")
    swapped = lax.ppermute(swap, "narrow", [(0, 1), (1, 0)])
    zero_a = lax.ppermute(zero, both, [(0, plan.special)])
    zero_b = lax.ppermute(zero, both, [(1, plan.special)])
    blocks = (plan.devices, 3, 2 * plan.width_x, lanes)
    got = lax.all_to_all(out.reshape(blocks), both, 0, 0, tiled=True).reshape(count, lanes)

    full = call(
        partial(tensor_kernel, plan),
        shape((2, 6, length_x, length_y), f32),
        [VMEM, VMEM, VMEM, VMEM, ANY], VMEM,
        [pltpu.VMEM((6, plan.rows_x, length_y), bf16), pltpu.SemaphoreType.DMA((1,))],
        1 << 27,
    )(swapped, zero_a, zero_b, jnp.asarray(flip.astype(az[0].dtype)), demag_spectrum)

    sent = call(
        partial(plane_kernel, plan),
        shape((count, lanes), f32),
        [VMEM] * 9, VMEM,
        [pltpu.VMEM((6, 2 * length_x, length_y), f32), pltpu.VMEM((3, 4 * length_x, length_y), bf16),
         pltpu.VMEM((8, 128), f32)],
        1 << 29,
    )(got, jnp.asarray(ay[0]), jnp.asarray(ay[1]), jnp.asarray(x_ahead), jnp.asarray(xb_pair),
      jnp.asarray(bx[1]), jnp.asarray(by[0]), jnp.asarray(by[1]), full)

    back = lax.all_to_all(sent.reshape(blocks), both, 0, 0, tiled=True).reshape(count, lanes)
    rise = [(i, i + 1) for i in range(plan.wide - 1)]
    before = lax.ppermute(up, "wide", rise)
    after = lax.ppermute(down, "wide", [(j, i) for i, j in rise])
    base = pl.pallas_call(
        partial(local_kernel, plan, species),
        grid=(1,),
        out_shape=shape((3 * cells, lanes), f32),
        in_specs=[pl.BlockSpec((3 * cells, lanes), lambda i: (0, 0)),
                  pl.BlockSpec((3 * cells, lanes), lambda i: (0, length_y // lanes)),
                  pl.BlockSpec((3 * plan.layers, lanes), lambda i: (0, 0)),
                  pl.BlockSpec((3 * plan.layers, lanes), lambda i: (0, 0)),
                  pl.BlockSpec((cells, lanes), lambda i: (0, 0)), SMEM, SMEM, SMEM],
        out_specs=pl.BlockSpec((3 * cells, lanes), lambda i: (0, 0)),
        scratch_shapes=[pltpu.VMEM((cells, lanes), f32)],
        compiler_params=pltpu.CompilerParams(vmem_limit_bytes=16 << 20),
        cost_estimate=pl.CostEstimate(flops=1 << 22, bytes_accessed=1 << 19, transcendentals=0),
    )(turned, swapped, before, after, material2, saturation, anisotropy, applied)

    rate, demag = call(
        partial(last_kernel, plan, species),
        (shape((3 * cells, lanes), f32), shape((3 * cells, lanes), f32)),
        [VMEM] * 6 + [SMEM], (VMEM, VMEM), [], 1 << 28,
    )(back, jnp.asarray(bz[0]), jnp.asarray(bz[1]), base, turned, material2, damping)
    return rate.reshape(spin.shape), demag.reshape(spin.shape)


def shards(*args):
    spin, demag_spectrum = args[0], args[-1]
    components, layers, width_x, width_y = spin.shape
    parts, planes, rows_x, length_y = demag_spectrum.shape
    plan = Plan(lax.axis_size("wide"), lax.axis_size("narrow"), layers, width_x, width_y,
                planes, rows_x, length_y)
    if plan.fits():
        return plane_shards(plan, *args)
    return general_shards(*args)


def solution(mesh):
    placed = (
        P(None, None, "wide", "narrow"),
        P(None, "wide", "narrow"),
        P(None, "wide", "narrow"),
        P(),
        P(),
        P(),
        P(),
        P(None, "wide", "narrow", None),
    )
    return jax.shard_map(
        shards,
        mesh=mesh,
        in_specs=placed,
        out_specs=(P(None, None, "wide", "narrow"), P(None, None, "wide", "narrow")),
        check_vma=False,
    )
```

profile of v0, /device:TPU:1, one launch (start us, length us, event | category | flops | bytes accessed | tf_op | source)
XLA Modules:
  0.0 55.2 jit_solution(8397841990013817427)
XLA Ops:
  0.6 1.1 %copy-done = bf16[6,4,32,512]{3,2,1,0:T(8,128)(2,1)S(1)} copy-done((bf16[6,4,32,512]{3,2,1,0:T(8,128)(2,1)S(1)}, bf16[6,4,32,512]{3,2,1,0:T(8,128)(2,1)}, u32[]{:S(2)}) %copy-start) | copy-done | bytes 786456
  1.8 0.9 %copy-done.8 = bf16[384,192]{1,0:T(8,128)(2,1)S(1)} copy-done((bf16[384,192]{1,0:T(8,128)(2,1)S(1)}, bf16[384,192]{1,0:T(8,128)(2,1)}, u32[]{:S(2)}) %copy-start.8) | copy-done | bytes 147480
  2.7 0.9 %copy-done.9 = bf16[384,192]{1,0:T(8,128)(2,1)S(1)} copy-done((bf16[384,192]{1,0:T(8,128)(2,1)S(1)}, bf16[384,192]{1,0:T(8,128)(2,1)}, u32[]{:S(2)}) %copy-start.9) | copy-done | bytes 147480
  3.6 0.8 %copy-done.11 = s32[32,2,128]{2,1,0:T(2,128)S(1)} copy-done((s32[32,2,128]{2,1,0:T(2,128)S(1)}, s32[32,2,128]{2,1,0:T(2,128)}, u32[]{:S(2)}) %copy-start.11) | copy-done | bytes 32792
  4.4 0.9 %copy-done.13 = f32[3,32,2,128]{3,2,1,0:T(2,128)S(1)} copy-done((f32[3,32,2,128]{3,2,1,0:T(2,128)S(1)}, f32[3,32,2,128]{3,2,1,0:T(2,128)}, u32[]{:S(2)}) %copy-start.13) | copy-done | bytes 98328
  5.3 0.8 %copy-done.16 = s32[32,2,128]{2,1,0:T(2,128)S(1)} copy-done((s32[32,2,128]{2,1,0:T(2,128)S(1)}, s32[32,2,128]{2,1,0:T(2,128)}, u32[]{:S(2)}) %copy-start.16) | copy-done | bytes 32792
  6.0 0.7 %copy-done.18 = f32[4]{0:T(128)S(1)} copy-done((f32[4]{0:T(128)S(1)}, f32[4]{0:T(128)}, u32[]{:S(2)}) %copy-start.18) | copy-done | bytes 40
  6.7 1.7 %shard_map.203 = (f32[384,128]{1,0:T(8,128)}, f32[96,128]{1,0:T(8,128)S(1)}, f32[96,128]{1,0:T(8,128)S(1)}, f32[192,640]{1,0:T(8,128)S(1)}, f32[192,512]{1,0:T(8,128)S(1)}, /*index=5*/f32[192,128]{1,0:T(8,128)S(1)}) custom-call(f32[192,128]{1,0:T(8,128)S(1)} %bitcast.14, s32[64,128]{1,0:T(8,128)S(1)} %bitcast.15, s32[64,128]{1,0:T(8,128)S(1)} %bitcast.11, ...), custom_call_target="tpu_custom_call" | custom-call | flops 268435456 | bytes 1048576 | tf_op jit(solution)/shard_map/pallas_call | solution.py:591
  8.4 2.1 %collective-permute-start = (f32[192,640]{1,0:T(8,128)S(1)}, f32[192,640]{1,0:T(8,128)S(1)}, u32[]{:S(2)}, u32[]{:S(2)}) collective-permute-start(f32[192,640]{1,0:T(8,128)S(1)} %get-tuple-element.11), channel_id=1, source_target_pairs={{0,1},{1,0},{2,3},{3,2},{4,5},{5,4},{6,7},{7,6},{8,9},{9,8},{10,11... | collective-permute-start | bytes 1474568 | tf_op jit(solution)/shard_map/ppermute | solution.py:603
  10.5 0.7 %collective-permute-start.2 = (f32[192,512]{1,0:T(8,128)S(1)}, f32[192,512]{1,0:T(8,128)S(1)}, u32[]{:S(2)}, u32[]{:S(2)}) collective-permute-start(f32[192,512]{1,0:T(8,128)S(1)} %get-tuple-element.12), channel_id=1, source_target_pairs={{1,17}} | collective-permute-start | bytes 1179656 | tf_op jit(solution)/shard_map/ppermute | solution.py:605
  11.2 0.7 %collective-permute-start.1 = (f32[192,512]{1,0:T(8,128)S(1)}, f32[192,512]{1,0:T(8,128)S(1)}, u32[]{:S(2)}, u32[]{:S(2)}) collective-permute-start(f32[192,512]{1,0:T(8,128)S(1)} %get-tuple-element.12), channel_id=1, source_target_pairs={{0,17}} | collective-permute-start | bytes 1179656 | tf_op jit(solution)/shard_map/ppermute | solution.py:604
  11.9 0.0 copy-start.17
  11.9 7.6 %all-to-all-start = ((f32[32,3,4,128]{3,2,1,0:T(4,128)}), f32[32,3,4,128]{3,2,1,0:T(4,128)S(1)}, u32[]{:S(2)}, u32[]{:S(2)}) async-start(f32[32,3,4,128]{3,2,1,0:T(4,128)} %bitcast.3), calls=%async_computation | async-start | bytes 393216 | tf_op jit(solution)/shard_map/all_to_all | solution.py:607
  19.5 0.7 %copy-done.2 = f32[192,512]{1,0:T(8,128)} copy-done((f32[192,512]{1,0:T(8,128)}, f32[192,512]{1,0:T(8,128)S(1)}, u32[]{:S(2)}) %copy-start.2) | copy-done | bytes 393240
  20.3 1.1 %collective-permute-done.swapped.side = f32[192,640]{1,0:T(8,128)S(1)} collective-permute-done((f32[192,640]{1,0:T(8,128)S(1)}, f32[192,640]{1,0:T(8,128)S(1)}, u32[]{:S(2)}, u32[]{:S(2)}) %collective-permute-start) | collective-permute-done | bytes 491552 | tf_op jit(solution)/shard_map/ppermute | solution.py:603
  21.4 1.0 %copy-done.3 = f32[192,512]{1,0:T(8,128)S(1)} copy-done((f32[192,512]{1,0:T(8,128)S(1)}, f32[192,512]{1,0:T(8,128)}, u32[]{:S(2)}) %copy-start.3) | copy-done | bytes 393240
  22.4 0.9 %copy-done.10 = bf16[256,256]{1,0:T(8,128)(2,1)S(1)} copy-done((bf16[256,256]{1,0:T(8,128)(2,1)S(1)}, bf16[256,256]{1,0:T(8,128)(2,1)}, u32[]{:S(2)}) %copy-start.10) | copy-done | bytes 131096
  23.3 0.5 shard_map.204.full
  23.9 5.0 %all-to-all-done = f32[32,3,4,128]{3,2,1,0:T(4,128)S(1)} async-done(((f32[32,3,4,128]{3,2,1,0:T(4,128)}), f32[32,3,4,128]{3,2,1,0:T(4,128)S(1)}, u32[]{:S(2)}, u32[]{:S(2)}) %all-to-all-start) | async-done | bytes 196640 | tf_op jit(solution)/shard_map/all_to_all | solution.py:607
  28.9 0.9 %copy-done.4 = bf16[512,256]{1,0:T(8,128)(2,1)S(1)} copy-done((bf16[512,256]{1,0:T(8,128)(2,1)S(1)}, bf16[512,256]{1,0:T(8,128)(2,1)}, u32[]{:S(2)}) %copy-start.4) | copy-done | bytes 262168
  29.8 0.9 %copy-done.5 = bf16[512,256]{1,0:T(8,128)(2,1)S(1)} copy-done((bf16[512,256]{1,0:T(8,128)(2,1)S(1)}, bf16[512,256]{1,0:T(8,128)(2,1)}, u32[]{:S(2)}) %copy-start.5) | copy-done | bytes 262168
  30.8 0.9 %copy-done.6 = bf16[256,512]{1,0:T(8,128)(2,1)S(1)} copy-done((bf16[256,512]{1,0:T(8,128)(2,1)S(1)}, bf16[256,512]{1,0:T(8,128)(2,1)}, u32[]{:S(2)}) %copy-start.6) | copy-done | bytes 262168
  31.7 0.9 %copy-done.7 = bf16[256,512]{1,0:T(8,128)(2,1)S(1)} copy-done((bf16[256,512]{1,0:T(8,128)(2,1)S(1)}, bf16[256,512]{1,0:T(8,128)(2,1)}, u32[]{:S(2)}) %copy-start.7) | copy-done | bytes 262168
  32.7 0.8 %copy-done.14 = bf16[64,256]{1,0:T(8,128)(2,1)S(1)} copy-done((bf16[64,256]{1,0:T(8,128)(2,1)S(1)}, bf16[64,256]{1,0:T(8,128)(2,1)}, u32[]{:S(2)}) %copy-start.14) | copy-done | bytes 32792
  33.4 0.8 %copy-done.15 = bf16[128,96]{1,0:T(8,128)(2,1)S(1)} copy-done((bf16[128,96]{1,0:T(8,128)(2,1)S(1)}, bf16[128,96]{1,0:T(8,128)(2,1)}, u32[]{:S(2)}) %copy-start.15) | copy-done | bytes 24600
  34.3 2.6 %shard_map.205 = f32[384,128]{1,0:T(8,128)} custom-call(f32[384,128]{1,0:T(8,128)S(1)} %bitcast.9, bf16[256,512]{1,0:T(8,128)(2,1)S(1)} %copy-done.7, bf16[256,512]{1,0:T(8,128)(2,1)S(1)} %copy-done.6, bf16[128,96]{1,0:T(8,128)(2,1)S(1)} %copy-done.15, bf16[64,256]{1,0:T(8,128)(2,1)S(1)} %copy-done.14, bf16[64,128]{1,0:T(8,128)(2,1)S(1)} %copy-done.17, ...), custom_call_target="tpu_custom_call" | custom-call | flops 536870912 | bytes 1048576 | tf_op jit(solution)/shard_map/pallas_call | solution.py:617
  36.9 6.6 %all-to-all-start.1 = ((f32[32,3,4,128]{3,2,1,0:T(4,128)}), f32[32,3,4,128]{3,2,1,0:T(4,128)S(1)}, u32[]{:S(2)}, u32[]{:S(2)}) async-start(f32[32,3,4,128]{3,2,1,0:T(4,128)} %bitcast.5), calls=%async_computation.1 | async-start | bytes 393216 | tf_op jit(solution)/shard_map/all_to_all | solution.py:627
  43.5 3.5 %collective-permute-start.3 = (f32[96,128]{1,0:T(8,128)S(1)}, f32[96,128]{1,0:T(8,128)S(1)}, u32[]{:S(2)}, u32[]{:S(2)}) collective-permute-start(f32[96,128]{1,0:T(8,128)S(1)} %copy-done.25), channel_id=1, source_target_pairs={{0,2},{2,4},{4,6},{6,8},{8,10},{10,12},{12,14},{14,16},{16,18},{18... | collective-permute-start | bytes 147464 | tf_op jit(solution)/shard_map/ppermute | solution.py:629
  47.0 1.9 %collective-permute-start.4 = (f32[96,128]{1,0:T(8,128)S(1)}, f32[96,128]{1,0:T(8,128)S(1)}, u32[]{:S(2)}, u32[]{:S(2)}) collective-permute-start(f32[96,128]{1,0:T(8,128)S(1)} %copy-done.23), channel_id=1, source_target_pairs={{2,0},{4,2},{6,4},{8,6},{10,8},{12,10},{14,12},{16,14},{18,16},{20... | collective-permute-start | bytes 147464 | tf_op jit(solution)/shard_map/ppermute | solution.py:630
  48.9 4.0 %collective-permute-done.4.after = f32[96,128]{1,0:T(8,128)S(1)} collective-permute-done((f32[96,128]{1,0:T(8,128)S(1)}, f32[96,128]{1,0:T(8,128)S(1)}, u32[]{:S(2)}, u32[]{:S(2)}) %collective-permute-start.4) | collective-permute-done | bytes 49184 | tf_op jit(solution)/shard_map/ppermute | solution.py:630
  53.0 0.7 %shard_map.206.base = f32[192,128]{1,0:T(8,128)S(1)} custom-call(f32[192,128]{1,0:T(8,128)S(1)} %get-tuple-element.13.turned, f32[192,640]{1,0:T(8,128)S(1)} %collective-permute-done.swapped.side, f32[96,128]{1,0:T(8,128)S(1)} %collective-permute-done.3.before, f32[96,128]{1,0:T(8,128)S(1)} %collective-permute-done.4.after, s32[64,128]{1,0:T(8,128)S(1)} %bitcast.12, ...), custom_call_target="tpu_custom_call" | custom-call | flops 4194304 | bytes 524288 | tf_op jit(solution)/shard_map/pallas_call | solution.py:631
  53.7 1.5 %shard_map.207 = (f32[192,128]{1,0:T(8,128)}, f32[192,128]{1,0:T(8,128)}) custom-call(f32[384,128]{1,0:T(8,128)S(1)} %bitcast.10, bf16[192,384]{1,0:T(8,128)(2,1)S(1)} %copy-done.28, bf16[192,384]{1,0:T(8,128)(2,1)S(1)} %copy-done.27, f32[192,128]{1,0:T(8,128)S(1)} %shard_map.206.base, f32[192,128]{1,0:T(8,128)S(1)} %get-tuple-element.13.turned, ...), custom_call_target="tpu_custom_call" | custom-call | flops 268435456 | bytes 1048576 | tf_op jit(solution)/shard_map/pallas_call | solution.py:646
  (45 shorter events, 0.1 us)
Async XLA Ops:
  0.6 1.1 %copy-start = (bf16[6,4,32,512]{3,2,1,0:T(8,128)(2,1)S(1)}, bf16[6,4,32,512]{3,2,1,0:T(8,128)(2,1)}, u32[]{:S(2)}) copy-start(bf16[6,4,32,512]{3,2,1,0:T(8,128)(2,1)} %tensor.3) | copy-start | bytes 2359300
  1.8 0.9 %copy-start.8 = (bf16[384,192]{1,0:T(8,128)(2,1)S(1)}, bf16[384,192]{1,0:T(8,128)(2,1)}, u32[]{:S(2)}) copy-start(bf16[384,192]{1,0:T(8,128)(2,1)} %constant.25.clone.t_low) | copy-start | bytes 442372
  2.7 0.9 %copy-start.9 = (bf16[384,192]{1,0:T(8,128)(2,1)S(1)}, bf16[384,192]{1,0:T(8,128)(2,1)}, u32[]{:S(2)}) copy-start(bf16[384,192]{1,0:T(8,128)(2,1)} %constant.24.clone.t_high) | copy-start | bytes 442372
  3.6 0.8 %copy-start.11 = (s32[32,2,128]{2,1,0:T(2,128)S(1)}, s32[32,2,128]{2,1,0:T(2,128)}, u32[]{:S(2)}) copy-start(s32[32,2,128]{2,1,0:T(2,128)} %param.22) | copy-start | bytes 98308
  4.4 0.9 %copy-start.13 = (f32[3,32,2,128]{3,2,1,0:T(2,128)S(1)}, f32[3,32,2,128]{3,2,1,0:T(2,128)}, u32[]{:S(2)}) copy-start(f32[3,32,2,128]{3,2,1,0:T(2,128)} %param.20) | copy-start | bytes 294916
  5.3 0.8 %copy-start.16 = (s32[32,2,128]{2,1,0:T(2,128)S(1)}, s32[32,2,128]{2,1,0:T(2,128)}, u32[]{:S(2)}) copy-start(s32[32,2,128]{2,1,0:T(2,128)} %param.21) | copy-start | bytes 98308
  6.7 14.7 %copy-start.1 = (bf16[6,4,32,512]{3,2,1,0:T(8,128)(2,1)S(1)}, bf16[6,4,32,512]{3,2,1,0:T(8,128)(2,1)}, u32[]{:S(2)}) copy-start(bf16[6,4,32,512]{3,2,1,0:T(8,128)(2,1)} %tensor.3) | copy-start | bytes 2359300
  8.4 11.1 %copy-start.22 = (f32[96,128]{1,0:T(8,128)}, f32[96,128]{1,0:T(8,128)S(1)}, u32[]{:S(2)}) copy-start(f32[96,128]{1,0:T(8,128)S(1)} %get-tuple-element.15) | copy-start | bytes 147460
  8.4 11.1 %copy-start.24 = (f32[96,128]{1,0:T(8,128)}, f32[96,128]{1,0:T(8,128)S(1)}, u32[]{:S(2)}) copy-start(f32[96,128]{1,0:T(8,128)S(1)} %get-tuple-element.14) | copy-start | bytes 147460
  8.4 13.0 %collective-permute-start = (f32[192,640]{1,0:T(8,128)S(1)}, f32[192,640]{1,0:T(8,128)S(1)}, u32[]{:S(2)}, u32[]{:S(2)}) collective-permute-start(f32[192,640]{1,0:T(8,128)S(1)} %get-tuple-element.11), channel_id=1, source_target_pairs={{0,1},{1,0},{2,3},{3,2},{4,5},{5,4},{6,7},{7,6},{8,9},{9,8},{10,11... | collective-permute-start | bytes 1474568 | tf_op jit(solution)/shard_map/ppermute | solution.py:603
  10.5 9.0 %collective-permute-start.2 = (f32[192,512]{1,0:T(8,128)S(1)}, f32[192,512]{1,0:T(8,128)S(1)}, u32[]{:S(2)}, u32[]{:S(2)}) collective-permute-start(f32[192,512]{1,0:T(8,128)S(1)} %get-tuple-element.12), channel_id=1, source_target_pairs={{1,17}} | collective-permute-start | bytes 1179656 | tf_op jit(solution)/shard_map/ppermute | solution.py:605
  11.2 8.3 %collective-permute-start.1 = (f32[192,512]{1,0:T(8,128)S(1)}, f32[192,512]{1,0:T(8,128)S(1)}, u32[]{:S(2)}, u32[]{:S(2)}) collective-permute-start(f32[192,512]{1,0:T(8,128)S(1)} %get-tuple-element.12), channel_id=1, source_target_pairs={{0,17}} | collective-permute-start | bytes 1179656 | tf_op jit(solution)/shard_map/ppermute | solution.py:604
  11.9 17.0 %copy-start.17 = (bf16[64,128]{1,0:T(8,128)(2,1)S(1)}, bf16[64,128]{1,0:T(8,128)(2,1)}, u32[]{:S(2)}) copy-start(bf16[64,128]{1,0:T(8,128)(2,1)} %constant.31.clone.xb_low) | copy-start | bytes 49156
  11.9 17.0 %all-to-all-start = ((f32[32,3,4,128]{3,2,1,0:T(4,128)}), f32[32,3,4,128]{3,2,1,0:T(4,128)S(1)}, u32[]{:S(2)}, u32[]{:S(2)}) async-start(f32[32,3,4,128]{3,2,1,0:T(4,128)} %bitcast.3), calls=%async_computation | async-start | bytes 393216 | tf_op jit(solution)/shard_map/all_to_all | solution.py:607
  21.4 1.0 %copy-start.3 = (f32[192,512]{1,0:T(8,128)S(1)}, f32[192,512]{1,0:T(8,128)}, u32[]{:S(2)}) copy-start(f32[192,512]{1,0:T(8,128)} %copy-done.2) | copy-start | bytes 1179652
  22.4 0.9 %copy-start.10 = (bf16[256,256]{1,0:T(8,128)(2,1)S(1)}, bf16[256,256]{1,0:T(8,128)(2,1)}, u32[]{:S(2)}) copy-start(bf16[256,256]{1,0:T(8,128)(2,1)} %constant.26.clone.flip) | copy-start | bytes 393220
  28.9 1.0 %copy-start.4 = (bf16[512,256]{1,0:T(8,128)(2,1)S(1)}, bf16[512,256]{1,0:T(8,128)(2,1)}, u32[]{:S(2)}) copy-start(bf16[512,256]{1,0:T(8,128)(2,1)} %constant.33.clone.yb_low) | copy-start | bytes 786436
  29.8 0.9 %copy-start.5 = (bf16[512,256]{1,0:T(8,128)(2,1)S(1)}, bf16[512,256]{1,0:T(8,128)(2,1)}, u32[]{:S(2)}) copy-start(bf16[512,256]{1,0:T(8,128)(2,1)} %constant.32.clone.yb_high) | copy-start | bytes 786436
  30.8 0.9 %copy-start.6 = (bf16[256,512]{1,0:T(8,128)(2,1)S(1)}, bf16[256,512]{1,0:T(8,128)(2,1)}, u32[]{:S(2)}) copy-start(bf16[256,512]{1,0:T(8,128)(2,1)} %constant.28.clone.y_low) | copy-start | bytes 786436
  31.7 0.9 %copy-start.7 = (bf16[256,512]{1,0:T(8,128)(2,1)S(1)}, bf16[256,512]{1,0:T(8,128)(2,1)}, u32[]{:S(2)}) copy-start(bf16[256,512]{1,0:T(8,128)(2,1)} %constant.27.clone.y_high) | copy-start | bytes 786436
  34.2 9.3 %copy-start.25 = (f32[96,128]{1,0:T(8,128)S(1)}, f32[96,128]{1,0:T(8,128)}, u32[]{:S(2)}) copy-start(f32[96,128]{1,0:T(8,128)} %copy-done.24) | copy-start | bytes 147460
  34.2 12.8 %copy-start.23 = (f32[96,128]{1,0:T(8,128)S(1)}, f32[96,128]{1,0:T(8,128)}, u32[]{:S(2)}) copy-start(f32[96,128]{1,0:T(8,128)} %copy-done.22) | copy-start | bytes 147460
  34.2 18.7 %copy-start.12 = (s32[32,2,128]{2,1,0:T(2,128)S(1)}, s32[32,2,128]{2,1,0:T(2,128)}, u32[]{:S(2)}) copy-start(s32[32,2,128]{2,1,0:T(2,128)} %param.22) | copy-start | bytes 98308
  34.2 18.7 %copy-start.19 = (f32[4]{0:T(128)S(1)}, f32[4]{0:T(128)}, u32[]{:S(2)}) copy-start(f32[4]{0:T(128)} %saturation.3) | copy-start | bytes 52
  34.2 18.7 %copy-start.20 = (f32[4]{0:T(128)S(1)}, f32[4]{0:T(128)}, u32[]{:S(2)}) copy-start(f32[4]{0:T(128)} %anisotropy.1) | copy-start | bytes 52
  34.2 18.7 %copy-start.21 = (f32[3]{0:T(128)S(1)}, f32[3]{0:T(128)}, u32[]{:S(2)}) copy-start(f32[3]{0:T(128)} %applied.1) | copy-start | bytes 40
  34.2 19.5 %copy-start.26 = (f32[4]{0:T(128)S(1)}, f32[4]{0:T(128)}, u32[]{:S(2)}) copy-start(f32[4]{0:T(128)} %damping.1) | copy-start | bytes 52
  34.2 19.5 %copy-start.27 = (bf16[192,384]{1,0:T(8,128)(2,1)S(1)}, bf16[192,384]{1,0:T(8,128)(2,1)}, u32[]{:S(2)}) copy-start(bf16[192,384]{1,0:T(8,128)(2,1)} %constant.35.clone.t_low) | copy-start | bytes 442372
  34.2 19.5 %copy-start.28 = (bf16[192,384]{1,0:T(8,128)(2,1)S(1)}, bf16[192,384]{1,0:T(8,128)(2,1)}, u32[]{:S(2)}) copy-start(bf16[192,384]{1,0:T(8,128)(2,1)} %constant.34.clone.t_high) | copy-start | bytes 442372
  36.9 16.8 %all-to-all-start.1 = ((f32[32,3,4,128]{3,2,1,0:T(4,128)}), f32[32,3,4,128]{3,2,1,0:T(4,128)S(1)}, u32[]{:S(2)}, u32[]{:S(2)}) async-start(f32[32,3,4,128]{3,2,1,0:T(4,128)} %bitcast.5), calls=%async_computation.1 | async-start | bytes 393216 | tf_op jit(solution)/shard_map/all_to_all | solution.py:627
  43.5 5.5 %collective-permute-start.3 = (f32[96,128]{1,0:T(8,128)S(1)}, f32[96,128]{1,0:T(8,128)S(1)}, u32[]{:S(2)}, u32[]{:S(2)}) collective-permute-start(f32[96,128]{1,0:T(8,128)S(1)} %copy-done.25), channel_id=1, source_target_pairs={{0,2},{2,4},{4,6},{6,8},{8,10},{10,12},{12,14},{14,16},{16,18},{18... | collective-permute-start | bytes 147464 | tf_op jit(solution)/shard_map/ppermute | solution.py:629
  47.0 5.9 %collective-permute-start.4 = (f32[96,128]{1,0:T(8,128)S(1)}, f32[96,128]{1,0:T(8,128)S(1)}, u32[]{:S(2)}, u32[]{:S(2)}) collective-permute-start(f32[96,128]{1,0:T(8,128)S(1)} %copy-done.23), channel_id=1, source_target_pairs={{2,0},{4,2},{6,4},{8,6},{10,8},{12,10},{14,12},{16,14},{18,16},{20... | collective-permute-start | bytes 147464 | tf_op jit(solution)/shard_map/ppermute | solution.py:630
  (4 other events, 2.9 us)
where the time goes:
time: 56.1 us; the launch traced here: 55.2 us
  starting transfers between devices  23.1 us (41%)
  local copies, waits for them, and re-layouts  14.1 us (25%)
  waiting for transfers between devices  10.1 us (18%)
  Pallas kernels  7.06 us (13%)
  between operations  0.9 us (2%)
    unnamed x58, local copies, waits for them, and re-layouts  14.1 us
    all_to_all x1, starting transfers between devices, plane_shards(): lax.all_to_all(out.reshape(blocks), both, 0, 0, tiled=True)  7.56 us
    all_to_all x1, starting transfers between devices, plane_shards(): lax.all_to_all(sent.reshape(blocks), both, 0, 0, tiled=True)  6.58 us
    all_to_all x1, waiting for transfers between devices, plane_shards(): lax.all_to_all(out.reshape(blocks), both, 0, 0, tiled=True)  5 us
    ppermute x1, waiting for transfers between devices, plane_shards(): after = lax.ppermute(down, 'wide', [(j, i) for i, j in rise])  3.99 us
    ppermute x1, starting transfers between devices, plane_shards(): before = lax.ppermute(up, 'wide', rise)  3.54 us
    pallas_call x1, Pallas kernels, plane_shards(): call(partial(plane_kernel, plan), shape((count, lanes), f32), [VMEM] * 9,...  2.6 us
    ppermute x1, starting transfers between devices, plane_shards(): swapped = lax.ppermute(swap, 'narrow', [(0, 1), (1, 0)])  2.09 us
  transfers between devices with their start and end apart: 7, of which 3 were waited for; matrix products, arithmetic and copies ran while one was open for 0% of the time, Pallas kernels for 2%

commit v1 on v0

--- a/solution.py
+++ b/solution.py
@@ -8,6 +8,7 @@
 from jax.experimental import pallas as pl
 from jax.experimental.pallas import tpu as pltpu
 from jax.sharding import PartitionSpec as P
+
 
 exchange_coef = 0.3
 highest = lax.Precision.HIGHEST
@@ -334,9 +335,7 @@
         cosine, sine = np.cos(angle), np.sin(angle)
         ahead_x = np.concatenate([cosine, sine], 0)
         back_x = np.block([[cosine.T, -sine.T], [sine.T, cosine.T]])
-        flip = np.zeros((half, half))
-        flip[(half - k) % half, k] = 1.0
-        return ahead_y, back_y, ahead_x, back_x, flip
+        return ahead_y, back_y, ahead_x, back_x
 
 
 def halves(value):
@@ -363,13 +362,37 @@
     return w, n, own, other
 
 
-def first_kernel(plan, species, spin, region, material, saturation, t_high, t_low, tensor,
-                 out, up, down, swap, zero, turned, held, held0, sems):
-    w, n, own, other = rows_of(plan)
-    fetch = pltpu.make_async_copy(tensor.at[:, other], held, sems.at[0])
-    fetch.start()
-    fetch0 = pltpu.make_async_copy(tensor.at[:, 0], held0, sems.at[1])
-    fetch0.start()
+def first_kernel(plan, species, spin_at, region_at, material_at, saturation_at, table_at, tensor,
+                 out_at, near_at, next_at, swap_at, zero_at, edge_at, turned_at,
+                 spin, region, material, saturation, table, held, held0,
+                 out, near, next_, swap, zero, edge, turned, sems, done):
+    w, _, _, other = rows_of(plan)
+    count = plan.rows_x
+    moves = [
+        pltpu.make_async_copy(source, target, sems.at[k])
+        for k, (source, target) in enumerate((
+            (saturation_at, saturation), (material_at, material), (region_at, region), (spin_at, spin),
+            (table_at, table), (tensor.at[:, other], held),
+        ))
+    ]
+    for move in moves:
+        move.start()
+    fetch0 = pltpu.make_async_copy(tensor.at[:, 0], held0, sems.at[6])
+    send0 = pltpu.make_async_copy(zero, zero_at, sems.at[7])
+
+    @pl.when(w == 0)
+    def _():
+        fetch0.start()
+
+    sent = []
+
+    def send(source, target):
+        move = pltpu.make_async_copy(source, target, done.at[len(sent)])
+        move.start()
+        sent.append(move)
+
+    for move in moves[:4]:
+        move.wait()
     cells = plan.layers * plan.width_x
     magnet = region[...].astype(jnp.float32)
     sat = pick(material[...], saturation, species)
@@ -377,59 +400,104 @@
     for c in range(3):
         direction = spin[c * cells : (c + 1) * cells, :] * magnet
         turned[c * cells : (c + 1) * cells, :] = direction
+        swap[c * cells : (c + 1) * cells, plan.length_y :] = direction
         a, b = halves(direction * sat)
         high.append(a)
         low.append(b)
     high, low = jnp.concatenate(high, 0), jnp.concatenate(low, 0)
-    out[...] = mul(t_high[...], high) + (mul(t_low[...], high) + mul(t_high[...], low))
-    count = 3 * plan.layers
-    up[...] = turned[pl.ds(1, count, stride=2), :]
-    down[...] = turned[pl.ds(0, count, stride=2), :]
-    swap[:, plan.length_y :] = turned[...]
-    fetch.wait()
-    fetch0.wait()
+    send(turned, turned_at)
+    moves[5].wait()
     for t in range(6):
-        rows = slice(t * plan.rows_x, (t + 1) * plan.rows_x)
+        rows = slice(t * count, (t + 1) * count)
         swap[rows, : plan.length_y] = held[t].astype(jnp.float32)
+    send(swap, swap_at)
+    moves[4].wait()
+    lines = out.shape[0]
+    t_high, t_low = table[:lines, :], table[lines:, :]
+    out[...] = mul(t_high, high) + (mul(t_low, high) + mul(t_high, low))
+    send(out, out_at)
+    layers3 = 3 * plan.layers
+    up, down = turned[pl.ds(1, layers3, stride=2), :], turned[pl.ds(0, layers3, stride=2), :]
+    near[...] = jnp.where(w % 2 == 0, up, down)
+    next_[...] = jnp.where(w % 2 == 0, down, up)
+    send(near, near_at)
+    send(next_, next_at)
+
     @pl.when(w == 0)
     def _():
+        fetch0.wait()
         for t in range(6):
-            rows = slice(t * plan.rows_x, (t + 1) * plan.rows_x)
-            zero[rows, :] = held0[t].astype(jnp.float32)
-
-
-def tensor_kernel(plan, swapped, zero_a, zero_b, flip, tensor, full, held, sems):
-    w, n, own, other = rows_of(plan)
+            zero[t * count : (t + 1) * count, :] = held0[t].astype(jnp.float32)
+            edge[t : t + 1, :] = held0[t, 0:1, :].astype(jnp.float32)
+        edge[6:8, :] = jnp.zeros((2, plan.length_y), jnp.float32)
+        send0.start()
+        last = pltpu.make_async_copy(edge, edge_at, sems.at[8])
+        last.start()
+        last.wait()
+        send0.wait()
+
+    for move in sent:
+        move.wait()
+
+
+def flip_of(half):
+    sum_of = lax.broadcasted_iota(jnp.int32, (half, half), 0) + lax.broadcasted_iota(jnp.int32, (half, half), 1)
+    return jnp.where((sum_of == half) | (sum_of == 0), 1.0, 0.0).astype(jnp.bfloat16)
+
+
+def own_kernel(plan, tensor, table, full, held, sems):
+    _, _, own, _ = rows_of(plan)
     fetch = pltpu.make_async_copy(tensor.at[:, own], held, sems.at[0])
     fetch.start()
-    half, count = plan.cells_y, plan.rows_x
-    special = jnp.logical_and(w == plan.wide // 2, n == 1)
-
-    def place(slot, part, t, values):
-        rows = slice(part * count, (part + 1) * count)
-        full[slot, t, rows, :half] = values[:, :half].astype(jnp.float32)
-        full[slot, t, rows, half:] = mul(values[:, half:].astype(jnp.bfloat16), flip[...])
-
-    for t in range(6):
-        place(0, 1, t, swapped[t * count : (t + 1) * count, : plan.length_y])
-    @pl.when(special)
-    def _():
-        for t in range(6):
-            place(1, 0, t, zero_b[t * count : (t + 1) * count, :])
-            place(1, 1, t, zero_a[t * count : (t + 1) * count, :])
+    half = plan.cells_y
+    flip = flip_of(half)
     fetch.wait()
     for t in range(6):
-        place(0, 0, t, held[t])
+        values = held[t]
+        full[t, :, :half] = values[:, :half].astype(jnp.float32)
+        full[t, :, half:] = mul(values[:, half:], flip)
+
+
+def far_kernel(plan, swapped, zero_at, edge_at, full, second, zero, edge, sems):
+    w, n, _, _ = rows_of(plan)
+    half, count = plan.cells_y, plan.rows_x
+    flip = flip_of(half)
+    for t in range(6):
+        rows = slice(t * count, (t + 1) * count)
+        full[t, :, :half] = swapped[rows, :half]
+        full[t, :, half:] = mul(swapped[rows, half : 2 * half].astype(jnp.bfloat16), flip)
+
+    @pl.when(jnp.logical_and(w == plan.wide // 2, n == 1))
+    def _():
+        moves = [pltpu.make_async_copy(zero_at, zero, sems.at[0]), pltpu.make_async_copy(edge_at, edge, sems.at[1])]
+        for move in moves:
+            move.start()
+        for move in moves:
+            move.wait()
+        row = lax.broadcasted_iota(jnp.int32, (count, count), 0)
+        col = lax.broadcasted_iota(jnp.int32, (count, count), 1)
+        turn = jnp.where(row + col == count, 1.0, 0.0).astype(jnp.bfloat16)
+        first = lax.broadcasted_iota(jnp.int32, (count, half), 0) == 0
+        lane0 = lax.broadcasted_iota(jnp.int32, (count, half), 1) == 0
+        edge_low = edge[:, :half]
+        edge_high = mul(edge[:, half:].astype(jnp.bfloat16), flip)
+        for t in range(6):
+            rows = slice(t * count, (t + 1) * count)
+            plus = zero[rows, :half]
+            minus = mul(zero[rows, half:].astype(jnp.bfloat16), flip)
+            second[t, :count, :half] = plus
+            second[t, :count, half:] = minus
+            swap_plus = mul(turn, jnp.where(lane0, plus, minus).astype(jnp.bfloat16))
+            swap_minus = mul(turn, jnp.where(lane0, minus, plus).astype(jnp.bfloat16))
+            second[t, count:, :half] = jnp.where(first, edge_low[t : t + 1, :], swap_plus)
+            second[t, count:, half:] = jnp.where(first, edge_high[t : t + 1, :], swap_minus)
 
 
 COUPLINGS = ((0, 3, 4), (3, 1, 5), (4, 5, 2))
 
 
-def plane_kernel(plan, got, y_high, y_low, x_ahead, xb_pair, xb_low, yb_high, yb_low, full,
-                 out, mixed, packed, spread):
-    w, n, own, other = rows_of(plan)
-    special = jnp.logical_and(w == plan.wide // 2, n == 1)
-    slot = special.astype(jnp.int32)
+def plane_kernel(plan, got, table, own_part, far_part, second, out, mixed, packed):
+    w, n, _, _ = rows_of(plan)
     lanes, half, wide = plan.width_y, plan.cells_y, plan.wide
     cells_x, length_x = plan.cells_x, plan.length_x
     block = 6 * plan.width_x
@@ -443,58 +511,84 @@
                 [got[pl.ds(m * block + row, wide, stride=narrow * block), :] for m in range(narrow)], 1))
     lines = jnp.concatenate(lines, 0)
     high, low = halves(lines)
-    waves = mul(high, y_high[...]) + (mul(low, y_high[...]) + mul(high, y_low[...]))
+    y_high, y_low = table[:half, :], table[half : 2 * half, :]
+    base = 4 * half
+    x_ahead = table[base : base + 2 * length_x, : 3 * cells_x]
+    xb_pair = table[base : base + per_c, half : half + 4 * length_x]
+    xb_low = table[base + per_c : base + 2 * per_c, half : half + 2 * length_x]
+    waves = mul(high, y_high) + (mul(low, y_high) + mul(high, y_low))
     for g in range(6):
         a, b = halves(waves[g * cells_x : (g + 1) * cells_x, :])
-        mixed[g] = mul(x_ahead[...], jnp.concatenate([a, b, a], 0))
+        mixed[g] = mul(x_ahead, jnp.concatenate([a, b, a], 0))
     step = 16
-    for lane in range(0, half, 128):
-        for row in range(0, length_x, step):
-            left = slice(lane, lane + 128)
-            right = slice(half + lane, half + lane + 128)
-            cr, sr = slice(row, row + step), slice(length_x + row, length_x + row + step)
-            fields = []
-            for g in range(6):
-                cp, sp = mixed[g, cr, left], mixed[g, sr, left]
-                cq, sq = mixed[g, cr, right], mixed[g, sr, right]
-                if lane == 0:
-                    edge = lax.broadcasted_iota(jnp.int32, cp.shape, 1) == 0
-                    cq0, sq0 = jnp.where(edge, 0.0, cq), jnp.where(edge, 0.0, sq)
-                    fields.append((cp - sq0, -(sp + cq0),
-                                   jnp.where(edge, cq, cp + sq), jnp.where(edge, -sq, cq - sp)))
-                else:
-                    fields.append((cp - sq, -(sp + cq), cp + sq, cq - sp))
-            for i in range(3):
-                sums = []
-                for s, lanes_at in ((0, left), (2, right)):
-                    real = imag = None
-                    for j in range(3):
-                        t = COUPLINGS[i][j]
-                        ka = full[0, t, cr, lanes_at]
-                        kb = full[slot, t, cr, lanes_at]
-                        a, b = fields[2 * j], fields[2 * j + 1]
-                        re = ka * a[s] - kb * b[s + 1]
-                        im = ka * a[s + 1] + kb * b[s]
-                        real = re if real is None else real + re
-                        imag = im if imag is None else imag + im
-                    sums.append((real, imag))
-                (pr, pi), (mr, mi) = sums
-                even_re, even_im, odd_re, odd_im = pr + mr, pi + mi, mi - pi, pr - mr
-                if lane == 0:
-                    even_re, even_im = jnp.where(edge, pr, even_re), jnp.where(edge, pi, even_im)
-                    odd_re, odd_im = jnp.where(edge, mr, odd_re), jnp.where(edge, mi, odd_im)
-                for value, at, lanes_at in (
-                    (even_re, 0, left), (even_im, length_x, left),
-                    (odd_re, 0, right), (odd_im, length_x, right),
-                ):
-                    a, b = halves(value)
-                    packed[i, at + row : at + row + step, lanes_at] = a
-                    packed[i, 2 * length_x + at + row : 2 * length_x + at + row + step, lanes_at] = b
+
+    def couple(paired):
+        for lane in range(0, half, 128):
+            for row in range(0, length_x, step):
+                left = slice(lane, lane + 128)
+                right = slice(half + lane, half + lane + 128)
+                cr, sr = slice(row, row + step), slice(length_x + row, length_x + row + step)
+                part = own_part if row < plan.rows_x else far_part
+                at = slice(row % plan.rows_x, row % plan.rows_x + step)
+                fields = []
+                for g in range(6):
+                    cp, sp = mixed[g, cr, left], mixed[g, sr, left]
+                    cq, sq = mixed[g, cr, right], mixed[g, sr, right]
+                    if lane == 0:
+                        edge = lax.broadcasted_iota(jnp.int32, cp.shape, 1) == 0
+                        cq0, sq0 = jnp.where(edge, 0.0, cq), jnp.where(edge, 0.0, sq)
+                        fields.append((cp - sq0, -(sp + cq0),
+                                       jnp.where(edge, cq, cp + sq), jnp.where(edge, -sq, cq - sp)))
+                    else:
+                        fields.append((cp - sq, -(sp + cq), cp + sq, cq - sp))
+                if not paired:
+                    fields = [
+                        (a[0] - b[1], a[1] + b[0], a[2] - b[3], a[3] + b[2])
+                        for a, b in zip(fields[0::2], fields[1::2])
+                    ]
+                for i in range(3):
+                    sums = []
+                    for s, lanes_at in ((0, left), (2, right)):
+                        real = imag = None
+                        for j in range(3):
+                            t = COUPLINGS[i][j]
+                            ka = part[t, at, lanes_at]
+                            if paired:
+                                kb = second[t, cr, lanes_at]
+                                a, b = fields[2 * j], fields[2 * j + 1]
+                                re = ka * a[s] - kb * b[s + 1]
+                                im = ka * a[s + 1] + kb * b[s]
+                            else:
+                                re, im = ka * fields[j][s], ka * fields[j][s + 1]
+                            real = re if real is None else real + re
+                            imag = im if imag is None else imag + im
+                        sums.append((real, imag))
+                    (pr, pi), (mr, mi) = sums
+                    even_re, even_im, odd_re, odd_im = pr + mr, pi + mi, mi - pi, pr - mr
+                    if lane == 0:
+                        even_re, even_im = jnp.where(edge, pr, even_re), jnp.where(edge, pi, even_im)
+                        odd_re, odd_im = jnp.where(edge, mr, odd_re), jnp.where(edge, mi, odd_im)
+                    for value, base_at, lanes_at in (
+                        (even_re, 0, left), (even_im, length_x, left),
+                        (odd_re, 0, right), (odd_im, length_x, right),
+                    ):
+                        a, b = halves(value)
+                        high_at, low_at = base_at + row, 2 * length_x + base_at + row
+                        packed[i, high_at : high_at + step, lanes_at] = a
+                        packed[i, low_at : low_at + step, lanes_at] = b
+
+    special = jnp.logical_and(w == plan.wide // 2, n == 1)
+    pl.when(special)(lambda: couple(True))
+    pl.when(jnp.logical_not(special))(lambda: couple(False))
     back = []
     for i in range(3):
-        back.append(mul(xb_pair[...], packed[i]) + mul(xb_low[...], packed[i, : 2 * length_x, :]))
+        back.append(mul(xb_pair, packed[i]) + mul(xb_low, packed[i, : 2 * length_x, :]))
     high, low = halves(jnp.concatenate(back, 0))
-    result = mul(high, yb_high[...]) + (mul(low, yb_high[...]) + mul(high, yb_low[...]))
+    result = None
+    for k in (slice(0, half), slice(half, 2 * half)):
+        yb_high, yb_low = table[2 * half : 3 * half, k], table[3 * half : 4 * half, k]
+        part = mul(high[:, k], yb_high) + (mul(low[:, k], yb_high) + mul(high[:, k], yb_low))
+        result = part if result is None else result + part
     for c in range(3):
         for j in range(2 * plan.width_x):
             row = c * 2 * plan.width_x + j
@@ -503,9 +597,9 @@
                     row * wide : (row + 1) * wide, m * lanes : (m + 1) * lanes]
 
 
-def local_kernel(plan, species, turned, side, before, after, material, saturation, anisotropy,
-                 applied, out, woven):
-    n = lax.axis_index("narrow")
+def local_kernel(plan, species, turned, side, near, next_, material, saturation, anisotropy,
+                 applied, table, out, woven):
+    w, n = lax.axis_index("wide"), lax.axis_index("narrow")
     cells, layers = plan.layers * plan.width_x, plan.layers
     row = lax.broadcasted_iota(jnp.int32, (cells, plan.width_y), 0)
     col = lax.broadcasted_iota(jnp.int32, (cells, plan.width_y), 1)
@@ -518,9 +612,10 @@
     for c in range(3):
         d = turned[c * cells : (c + 1) * cells, :]
         s = side[c * cells : (c + 1) * cells, :]
-        woven[pl.ds(0, layers, stride=2), :] = before[c * layers : (c + 1) * layers, :]
-        woven[pl.ds(1, layers, stride=2), :] = after[c * layers : (c + 1) * layers, :]
-        near = (
+        a, b = near[c * layers : (c + 1) * layers, :], next_[c * layers : (c + 1) * layers, :]
+        woven[pl.ds(0, layers, stride=2), :] = jnp.where(w % 2 == 0, b, a)
+        woven[pl.ds(1, layers, stride=2), :] = jnp.where(w % 2 == 0, a, b)
+        beside = (
             jnp.where(row >= 2, pltpu.roll(d, 2, 0), 0.0),
             jnp.where(row < cells - 2, pltpu.roll(d, cells - 2, 0), 0.0),
             woven[...],
@@ -528,9 +623,9 @@
             pltpu.roll(jnp.where(first, s * ahead, d), plan.width_y - 1, 1),
             pltpu.roll(jnp.where(last, s * (1.0 - ahead), d), 1, 1),
         )
-        total = near[0]
-        present = present + near[0] * near[0]
-        for v in near[1:]:
+        total = beside[0]
+        present = present + beside[0] * beside[0]
+        for v in beside[1:]:
             total = total + v
             present = present + v * v
         sums.append(total)
@@ -542,10 +637,11 @@
         out[c * cells : (c + 1) * cells, :] = field
 
 
-def last_kernel(plan, species, got, t_high, t_low, base, turned, material, damping, rate, demag):
+def last_kernel(plan, species, got, table, base, turned, material, damping, rate, demag):
     cells = plan.layers * plan.width_x
+    t_high, t_low = table[: 3 * cells, :], table[3 * cells :, :]
     high, low = halves(got[...])
-    demag[...] = mul(t_high[...], high) + (mul(t_low[...], high) + mul(t_high[...], low))
+    demag[...] = mul(t_high, high) + (mul(t_low, high) + mul(t_high, low))
     damp = pick(material[...], damping, species)
     d = [turned[c * cells : (c + 1) * cells, :] for c in range(3)]
     f = [demag[c * cells : (c + 1) * cells, :] + base[c * cells : (c + 1) * cells, :] for c in range(3)]
@@ -560,9 +656,10 @@
         rate[c * cells : (c + 1) * cells, :] = (torque[c] + damp * again[c]) * scale
 
 
+LIMITS = (67043328, 24 << 20, 24 << 20, 16 << 20, 24 << 20)
 VMEM = pl.BlockSpec(memory_space=pltpu.VMEM)
 SMEM = pl.BlockSpec(memory_space=pltpu.SMEM)
-ANY = pl.BlockSpec(memory_space=pl.ANY)
+HBM = pl.BlockSpec(memory_space=pltpu.HBM)
 
 
 def plane_shards(plan, spin, region, material, saturation, anisotropy, damping, applied, demag_spectrum):
@@ -574,7 +671,7 @@
     spin2 = spin.reshape(3 * cells, lanes)
     region2, material2 = region.reshape(cells, lanes), material.reshape(cells, lanes)
     ahead_z, back_z = plan.thickness_tables()
-    ahead_y, back_y, ahead_x, back_x, flip = plan.lateral_tables()
+    ahead_y, back_y, ahead_x, back_x = plan.lateral_tables()
     az, bz, ay, by = (split_table(t) for t in (ahead_z, back_z, ahead_y, back_y))
     ax, bx = split_table(ahead_x), split_table(back_x)
     x_ahead = np.concatenate([ax[0], ax[0], ax[1]], 1)
@@ -588,46 +685,61 @@
         )
 
     rows6 = 6 * plan.rows_x
-    out, up, down, swap, zero, turned = call(
+    table_in, table_out = jnp.asarray(np.concatenate(az, 0)), jnp.asarray(np.concatenate(bz, 0))
+    outs = ((count, lanes), (3 * plan.layers, lanes), (3 * plan.layers, lanes), (rows6, length_y + lanes),
+            (rows6, length_y), (8, length_y), (3 * cells, lanes))
+    out, near, next_, swap, zero, edge, turned = call(
         partial(first_kernel, plan, species),
-        (shape((count, lanes), f32), shape((3 * plan.layers, lanes), f32), shape((3 * plan.layers, lanes), f32),
-         shape((rows6, length_y + lanes), f32), shape((rows6, length_y), f32), shape((3 * cells, lanes), f32)),
-        [VMEM, VMEM, VMEM, SMEM, VMEM, VMEM, ANY],
-        (VMEM,) * 6,
-        [pltpu.VMEM((6, plan.rows_x, length_y), bf16), pltpu.VMEM((6, plan.rows_x, length_y), bf16),
-         pltpu.SemaphoreType.DMA((2,))],
-        1 << 28,
-    )(spin2, region2, material2, saturation, jnp.asarray(az[0]), jnp.asarray(az[1]), demag_spectrum)
+        tuple(shape(o, f32) for o in outs), [HBM] * 6, (HBM,) * len(outs),
+        [pltpu.VMEM((3 * cells, lanes), f32), pltpu.VMEM((cells, lanes), jnp.int32),
+         pltpu.VMEM((cells, lanes), jnp.int32), pltpu.SMEM((species,), f32),
+         pltpu.VMEM(table_in.shape, bf16),
+         pltpu.VMEM((6, plan.rows_x, length_y), bf16), pltpu.VMEM((6, plan.rows_x, length_y), bf16)]
+        + [pltpu.VMEM(o, f32) for o in outs]
+        + [pltpu.SemaphoreType.DMA((9,)), pltpu.SemaphoreType.DMA((5,))],
+        1 << 28, LIMITS[0],
+    )(spin2, region2, material2, saturation, table_in, demag_spectrum)
 
     both = ("wide", "narrow")
     swapped = lax.ppermute(swap, "narrow", [(0, 1), (1, 0)])
-    zero_a = lax.ppermute(zero, both, [(0, plan.special)])
-    zero_b = lax.ppermute(zero, both, [(1, plan.special)])
     blocks = (plan.devices, 3, 2 * plan.width_x, lanes)
     got = lax.all_to_all(out.reshape(blocks), both, 0, 0, tiled=True).reshape(count, lanes)
-
-    full = call(
-        partial(tensor_kernel, plan),
-        shape((2, 6, length_x, length_y), f32),
-        [VMEM, VMEM, VMEM, VMEM, ANY], VMEM,
-        [pltpu.VMEM((6, plan.rows_x, length_y), bf16), pltpu.SemaphoreType.DMA((1,))],
-        1 << 27,
-    )(swapped, zero_a, zero_b, jnp.asarray(flip.astype(az[0].dtype)), demag_spectrum)
+    edge_a = lax.ppermute(edge, both, [(0, plan.special)])
+    zero_b = lax.ppermute(zero, both, [(1, plan.special)])
+    pairs = [(i ^ 1, i) for i in range(plan.wide)]
+    near = lax.ppermute(near, "wide", pairs)
+    pairs = [(i, j) for i in range(1, plan.wide - 1, 2) for i, j in ((i, i + 1), (i + 1, i))]
+    next_ = lax.ppermute(next_, "wide", pairs)
+
+    half = plan.cells_y
+    folded = [np.concatenate([t[:half], t[half:]], 1) for t in by]
+    small = np.zeros((2 * length_x, 2 * half), az[0].dtype)
+    small[:, : 3 * plan.cells_x] = x_ahead
+    small[: 2 * plan.cells_x, half : half + 4 * length_x] = xb_pair
+    small[2 * plan.cells_x : 4 * plan.cells_x, half : half + 2 * length_x] = bx[1]
+    table = jnp.asarray(np.concatenate([ay[0], ay[1], *folded, small], 0))
+
+    own_part = call(
+        partial(own_kernel, plan), shape((6, plan.rows_x, length_y), f32), [HBM, VMEM], VMEM,
+        [pltpu.VMEM((6, plan.rows_x, length_y), bf16), pltpu.SemaphoreType.DMA((1,))], 1 << 26, LIMITS[1],
+    )(demag_spectrum, table)
+    far_part, second = call(
+        partial(far_kernel, plan),
+        (shape((6, plan.rows_x, length_y), f32), shape((6, length_x, length_y), f32)),
+        [VMEM, HBM, HBM], (VMEM, VMEM),
+        [pltpu.VMEM((rows6, length_y), f32), pltpu.VMEM((8, length_y), f32), pltpu.SemaphoreType.DMA((2,))],
+        1 << 26, LIMITS[1],
+    )(swapped, zero_b, edge_a)
 
     sent = call(
         partial(plane_kernel, plan),
         shape((count, lanes), f32),
-        [VMEM] * 9, VMEM,
-        [pltpu.VMEM((6, 2 * length_x, length_y), f32), pltpu.VMEM((3, 4 * length_x, length_y), bf16),
-         pltpu.VMEM((8, 128), f32)],
-        1 << 29,
-    )(got, jnp.asarray(ay[0]), jnp.asarray(ay[1]), jnp.asarray(x_ahead), jnp.asarray(xb_pair),
-      jnp.asarray(bx[1]), jnp.asarray(by[0]), jnp.asarray(by[1]), full)
+        [VMEM] * 5, VMEM,
+        [pltpu.VMEM((6, 2 * length_x, length_y), f32), pltpu.VMEM((3, 4 * length_x, length_y), bf16)],
+        1 << 29, LIMITS[2],
+    )(got, table, own_part, far_part, second)
 
     back = lax.all_to_all(sent.reshape(blocks), both, 0, 0, tiled=True).reshape(count, lanes)
-    rise = [(i, i + 1) for i in range(plan.wide - 1)]
-    before = lax.ppermute(up, "wide", rise)
-    after = lax.ppermute(down, "wide", [(j, i) for i, j in rise])
     base = pl.pallas_call(
         partial(local_kernel, plan, species),
         grid=(1,),
@@ -636,25 +748,25 @@
                   pl.BlockSpec((3 * cells, lanes), lambda i: (0, length_y // lanes)),
                   pl.BlockSpec((3 * plan.layers, lanes), lambda i: (0, 0)),
                   pl.BlockSpec((3 * plan.layers, lanes), lambda i: (0, 0)),
-                  pl.BlockSpec((cells, lanes), lambda i: (0, 0)), SMEM, SMEM, SMEM],
+                  pl.BlockSpec((cells, lanes), lambda i: (0, 0)), SMEM, SMEM, SMEM, VMEM],
         out_specs=pl.BlockSpec((3 * cells, lanes), lambda i: (0, 0)),
         scratch_shapes=[pltpu.VMEM((cells, lanes), f32)],
-        compiler_params=pltpu.CompilerParams(vmem_limit_bytes=16 << 20),
+        compiler_params=pltpu.CompilerParams(vmem_limit_bytes=LIMITS[3]),
         cost_estimate=pl.CostEstimate(flops=1 << 22, bytes_accessed=1 << 19, transcendentals=0),
-    )(turned, swapped, before, after, material2, saturation, anisotropy, applied)
+    )(turned, swapped, near, next_, material2, saturation, anisotropy, applied, table_out)
 
     rate, demag = call(
         partial(last_kernel, plan, species),
         (shape((3 * cells, lanes), f32), shape((3 * cells, lanes), f32)),
-        [VMEM] * 6 + [SMEM], (VMEM, VMEM), [], 1 << 28,
-    )(back, jnp.asarray(bz[0]), jnp.asarray(bz[1]), base, turned, material2, damping)
+        [VMEM] * 5 + [SMEM], (VMEM, VMEM), [], 1 << 28, LIMITS[4],
+    )(back, table_out, base, turned, material2, damping)
     return rate.reshape(spin.shape), demag.reshape(spin.shape)
 
 
 def shards(*args):
     spin, demag_spectrum = args[0], args[-1]
-    components, layers, width_x, width_y = spin.shape
-    parts, planes, rows_x, length_y = demag_spectrum.shape
+    _, layers, width_x, width_y = spin.shape
+    _, planes, rows_x, length_y = demag_spectrum.shape
     plan = Plan(lax.axis_size("wide"), lax.axis_size("narrow"), layers, width_x, width_y,
                 planes, rows_x, length_y)
     if plan.fits():

time: 56.1 us -> 41.5 us (0.74)
  the two profiles are of different devices: /device:TPU:1 before, /device:TPU:0 now
where the time goes in v1:
time: 41.5 us; the launch traced here: 41.1 us
  starting transfers between devices  20.1 us (48%)
  waiting for transfers between devices  8.27 us (20%)
  Pallas kernels  7.76 us (19%)
  local copies, waits for them, and re-layouts  4.18 us (10%)
  between operations  0.81 us (2%)
    all_to_all x1, waiting for transfers between devices, plane_shards(): lax.all_to_all(sent.reshape(blocks), both, 0, 0, tiled=True)  7.36 us
    ppermute x1, starting transfers between devices, plane_shards(): edge_a = lax.ppermute(edge, both, [(0, plan.special)])  5.48 us
    all_to_all x1, starting transfers between devices, plane_shards(): lax.all_to_all(sent.reshape(blocks), both, 0, 0, tiled=True)  5.15 us
    all_to_all x1, starting transfers between devices, plane_shards(): lax.all_to_all(out.reshape(blocks), both, 0, 0, tiled=True)  4.76 us
    unnamed x26, local copies, waits for them, and re-layouts  4.18 us
    ppermute x1, starting transfers between devices, plane_shards(): swapped = lax.ppermute(swap, 'narrow', [(0, 1), (1, 0)])  3.03 us
    pallas_call x1, Pallas kernels, plane_shards(): call(partial(plane_kernel, plan), shape((count, lanes), f32), [VMEM] * 5,...  2.51 us
    pallas_call x1, Pallas kernels, plane_shards(): call(partial(first_kernel, plan, species), tuple((shape(o, f32) for o in...  2.46 us
  transfers between devices with their start and end apart: 7, of which 3 were waited for; matrix products, arithmetic and copies ran while one was open for 0% of the time, Pallas kernels for 3%

profile of v1, /device:TPU:0, one launch (start us, length us, event | category | flops | bytes accessed | tf_op | source)
XLA Modules:
  0.0 41.1 jit_solution(3860685271043211995)
XLA Ops:
  0.6 2.5 %shard_map.122 = (f32[384,128]{1,0:T(8,128)}, f32[96,128]{1,0:T(8,128)}, f32[96,128]{1,0:T(8,128)}, f32[192,640]{1,0:T(8,128)}, f32[192,512]{1,0:T(8,128)}, /*index=5*/f32[8,512]{1,0:T(8,128)}, f32[192,128]{1,0:T(8,128)}) custom-call(f32[192,128]{1,0:T(8,128)} %bitcast.15, s32[64,128]{1,0:T(8,128)} %bitcast.16, s32[64,128]{1,0:T(8,128)} %bitcast.11, ...), custom_call_target="tpu_custom_call" | custom-call | flops 268435456 | bytes 1048576 | tf_op jit(solution)/shard_map/pallas_call | solution.py:691
  3.1 3.0 %collective-permute-start = (f32[192,640]{1,0:T(8,128)}, f32[192,640]{1,0:T(8,128)S(1)}, u32[]{:S(2)}, u32[]{:S(2)}) collective-permute-start(f32[192,640]{1,0:T(8,128)} %get-tuple-element.14), channel_id=1, source_target_pairs={{0,1},{1,0},{2,3},{3,2},{4,5},{5,4},{6,7},{7,6},{8,9},{9,8},{10,11... | collective-permute-start | bytes 1474568 | tf_op jit(solution)/shard_map/ppermute | solution.py:704
  6.1 0.7 %collective-permute-start.1 = (f32[192,512]{1,0:T(8,128)}, f32[192,512]{1,0:T(8,128)S(1)}, u32[]{:S(2)}, u32[]{:S(2)}) collective-permute-start(f32[192,512]{1,0:T(8,128)} %get-tuple-element.15), channel_id=1, source_target_pairs={{1,17}} | collective-permute-start | bytes 1179656 | tf_op jit(solution)/shard_map/ppermute | solution.py:708
  6.8 4.8 %all-to-all-start = ((f32[32,3,4,128]{3,2,1,0:T(4,128)}), f32[32,3,4,128]{3,2,1,0:T(4,128)S(1)}, u32[]{:S(2)}, u32[]{:S(2)}) async-start(f32[32,3,4,128]{3,2,1,0:T(4,128)} %bitcast.14), calls=%async_computation | async-start | bytes 393216 | tf_op jit(solution)/shard_map/all_to_all | solution.py:706
  11.6 5.5 %collective-permute-start.2 = (f32[8,512]{1,0:T(8,128)}, f32[8,512]{1,0:T(8,128)S(1)}, u32[]{:S(2)}, u32[]{:S(2)}) collective-permute-start(f32[8,512]{1,0:T(8,128)} %get-tuple-element.16), channel_id=1, source_target_pairs={{0,17}} | collective-permute-start | bytes 49160 | tf_op jit(solution)/shard_map/ppermute | solution.py:707
  17.1 0.0 copy-start
  17.1 1.3 %copy-done = bf16[1152,512]{1,0:T(8,128)(2,1)S(1)} copy-done((bf16[1152,512]{1,0:T(8,128)(2,1)S(1)}, bf16[1152,512]{1,0:T(8,128)(2,1)}, u32[]{:S(2)}) %copy-start) | copy-done | bytes 1179672
  18.3 1.1 %copy-done.2 = bf16[6,4,32,512]{3,2,1,0:T(8,128)(2,1)S(1)} copy-done((bf16[6,4,32,512]{3,2,1,0:T(8,128)(2,1)S(1)}, bf16[6,4,32,512]{3,2,1,0:T(8,128)(2,1)}, u32[]{:S(2)}) %copy-start.2) | copy-done | bytes 786456
  19.5 0.3 shard_map.123.own_part
  19.8 0.0 collective-permute-done.2.edge_at
  19.8 0.0 collective-permute-done.1.zero_at
  19.8 0.0 collective-permute-done.swapped.side
  19.8 0.3 shard_map.124
  20.1 0.7 %copy-done.3 = f32[6,32,512]{2,1,0:T(8,128)} copy-done((f32[6,32,512]{2,1,0:T(8,128)}, f32[6,32,512]{2,1,0:T(8,128)S(1)}, u32[]{:S(2)}) %copy-start.3) | copy-done | bytes 393240
  20.8 0.4 all-to-all-done
  21.2 1.0 %copy-done.4 = f32[6,32,512]{2,1,0:T(8,128)S(1)} copy-done((f32[6,32,512]{2,1,0:T(8,128)S(1)}, f32[6,32,512]{2,1,0:T(8,128)}, u32[]{:S(2)}) %copy-start.4) | copy-done | bytes 393240
  22.2 0.0 copy-start.8
  22.2 0.0 copy-start.9
  22.2 0.0 copy-start.10
  22.3 2.5 %shard_map.125 = f32[384,128]{1,0:T(8,128)} custom-call(f32[384,128]{1,0:T(8,128)S(1)} %bitcast.9, bf16[1152,512]{1,0:T(8,128)(2,1)S(1)} %copy-done.1, f32[6,32,512]{2,1,0:T(8,128)S(1)} %shard_map.123.own_part, f32[6,32,512]{2,1,0:T(8,128)S(1)} %copy-done.4, f32[6,64,512]{2,1,0:T(8,128)S(1)} %get-tuple-element.18.second), custom_call_target="tpu_custom_call" | custom-call | flops 536870912 | bytes 1048576 | tf_op jit(solution)/shard_map/pallas_call | solution.py:734
  24.8 5.2 %all-to-all-start.1 = ((f32[32,3,4,128]{3,2,1,0:T(4,128)}), f32[32,3,4,128]{3,2,1,0:T(4,128)S(1)}, u32[]{:S(2)}, u32[]{:S(2)}) async-start(f32[32,3,4,128]{3,2,1,0:T(4,128)} %bitcast.5), calls=%async_computation.1 | async-start | bytes 393216 | tf_op jit(solution)/shard_map/all_to_all | solution.py:742
  29.9 0.3 collective-permute-start.3
  30.2 0.0 copy-done.12
  30.2 0.7 %collective-permute-start.4 = (f32[96,128]{1,0:T(8,128)S(1)}, f32[96,128]{1,0:T(8,128)S(1)}, u32[]{:S(2)}, u32[]{:S(2)}) collective-permute-start(f32[96,128]{1,0:T(8,128)S(1)} %copy-done.12), channel_id=1, source_target_pairs={{2,4},{4,2},{6,8},{8,6},{10,12},{12,10},{14,16},{16,14},{18,20},{2... | collective-permute-start | bytes 147464 | tf_op jit(solution)/shard_map/ppermute | solution.py:712
  30.9 0.5 %collective-permute-done.3.near = f32[96,128]{1,0:T(8,128)S(1)} collective-permute-done((f32[96,128]{1,0:T(8,128)}, f32[96,128]{1,0:T(8,128)S(1)}, u32[]{:S(2)}, u32[]{:S(2)}) %collective-permute-start.3) | collective-permute-done | bytes 49184 | tf_op jit(solution)/shard_map/ppermute | solution.py:710
  31.4 0.0 collective-permute-done.4.next_
  31.4 0.0 copy-done.7
  31.5 0.0 copy-done.8
  31.5 0.0 copy-done.9
  31.5 0.7 %shard_map.126.base = f32[192,128]{1,0:T(8,128)S(1)} custom-call(f32[192,128]{1,0:T(8,128)S(1)} %copy-done.7, f32[192,640]{1,0:T(8,128)S(1)} %collective-permute-done.swapped.side, f32[96,128]{1,0:T(8,128)S(1)} %collective-permute-done.3.near, f32[96,128]{1,0:T(8,128)S(1)} %collective-permute-done.4.next_, s32[64,128]{1,0:T(8,128)S(1)} %bitcast.12, ...), custom_call_target="tpu_custom_call" | custom-call | flops 4194304 | bytes 524288 | tf_op jit(solution)/shard_map/pallas_call | solution.py:743
  32.2 7.4 %all-to-all-done.1 = f32[32,3,4,128]{3,2,1,0:T(4,128)S(1)} async-done(((f32[32,3,4,128]{3,2,1,0:T(4,128)}), f32[32,3,4,128]{3,2,1,0:T(4,128)S(1)}, u32[]{:S(2)}, u32[]{:S(2)}) %all-to-all-start.1) | async-done | bytes 196640 | tf_op jit(solution)/shard_map/all_to_all | solution.py:742
  39.6 1.5 %shard_map.127 = (f32[192,128]{1,0:T(8,128)}, f32[192,128]{1,0:T(8,128)}) custom-call(f32[384,128]{1,0:T(8,128)S(1)} %bitcast.10, bf16[384,384]{1,0:T(8,128)(2,1)S(1)} %copy-done.5, f32[192,128]{1,0:T(8,128)S(1)} %shard_map.126.base, f32[192,128]{1,0:T(8,128)S(1)} %copy-done.7, s32[64,128]{1,0:T(8,128)S(1)} %bitcast.13, f32[4]{0:T(128)S(1)} %copy-done.11), custom_call_target="tpu_custom_call" | custom-call | flops 268435456 | bytes 1048576 | tf_op jit(solution)/shard_map/pallas_call | solution.py:758
  (14 shorter events, 0.0 us)
Async XLA Ops:
  3.1 16.7 %collective-permute-start = (f32[192,640]{1,0:T(8,128)}, f32[192,640]{1,0:T(8,128)S(1)}, u32[]{:S(2)}, u32[]{:S(2)}) collective-permute-start(f32[192,640]{1,0:T(8,128)} %get-tuple-element.14), channel_id=1, source_target_pairs={{0,1},{1,0},{2,3},{3,2},{4,5},{5,4},{6,7},{7,6},{8,9},{9,8},{10,11... | collective-permute-start | bytes 1474568 | tf_op jit(solution)/shard_map/ppermute | solution.py:704
  6.1 13.7 %collective-permute-start.1 = (f32[192,512]{1,0:T(8,128)}, f32[192,512]{1,0:T(8,128)S(1)}, u32[]{:S(2)}, u32[]{:S(2)}) collective-permute-start(f32[192,512]{1,0:T(8,128)} %get-tuple-element.15), channel_id=1, source_target_pairs={{1,17}} | collective-permute-start | bytes 1179656 | tf_op jit(solution)/shard_map/ppermute | solution.py:708
  6.8 14.4 %all-to-all-start = ((f32[32,3,4,128]{3,2,1,0:T(4,128)}), f32[32,3,4,128]{3,2,1,0:T(4,128)S(1)}, u32[]{:S(2)}, u32[]{:S(2)}) async-start(f32[32,3,4,128]{3,2,1,0:T(4,128)} %bitcast.14), calls=%async_computation | async-start | bytes 393216 | tf_op jit(solution)/shard_map/all_to_all | solution.py:706
  11.6 8.2 %collective-permute-start.2 = (f32[8,512]{1,0:T(8,128)}, f32[8,512]{1,0:T(8,128)S(1)}, u32[]{:S(2)}, u32[]{:S(2)}) collective-permute-start(f32[8,512]{1,0:T(8,128)} %get-tuple-element.16), channel_id=1, source_target_pairs={{0,17}} | collective-permute-start | bytes 49160 | tf_op jit(solution)/shard_map/ppermute | solution.py:707
  17.1 1.3 %copy-start = (bf16[1152,512]{1,0:T(8,128)(2,1)S(1)}, bf16[1152,512]{1,0:T(8,128)(2,1)}, u32[]{:S(2)}) copy-start(bf16[1152,512]{1,0:T(8,128)(2,1)} %constant.8.clone.table) | copy-start | bytes 3538948
  18.3 1.1 %copy-start.2 = (bf16[6,4,32,512]{3,2,1,0:T(8,128)(2,1)S(1)}, bf16[6,4,32,512]{3,2,1,0:T(8,128)(2,1)}, u32[]{:S(2)}) copy-start(bf16[6,4,32,512]{3,2,1,0:T(8,128)(2,1)} %tensor.3) | copy-start | bytes 2359300
  19.5 1.7 %copy-start.1 = (bf16[1152,512]{1,0:T(8,128)(2,1)S(1)}, bf16[1152,512]{1,0:T(8,128)(2,1)}, u32[]{:S(2)}) copy-start(bf16[1152,512]{1,0:T(8,128)(2,1)} %constant.8.clone.table) | copy-start | bytes 3538948
  20.1 0.8 %copy-start.3 = (f32[6,32,512]{2,1,0:T(8,128)}, f32[6,32,512]{2,1,0:T(8,128)S(1)}, u32[]{:S(2)}) copy-start(f32[6,32,512]{2,1,0:T(8,128)S(1)} %get-tuple-element.17.far_part) | copy-start | bytes 1179652
  21.2 1.0 %copy-start.4 = (f32[6,32,512]{2,1,0:T(8,128)S(1)}, f32[6,32,512]{2,1,0:T(8,128)}, u32[]{:S(2)}) copy-start(f32[6,32,512]{2,1,0:T(8,128)} %copy-done.3) | copy-start | bytes 1179652
  22.2 8.0 %copy-start.12 = (f32[96,128]{1,0:T(8,128)S(1)}, f32[96,128]{1,0:T(8,128)}, u32[]{:S(2)}) copy-start(f32[96,128]{1,0:T(8,128)} %get-tuple-element.21) | copy-start | bytes 147460
  22.2 9.2 %copy-start.5 = (bf16[384,384]{1,0:T(8,128)(2,1)S(1)}, bf16[384,384]{1,0:T(8,128)(2,1)}, u32[]{:S(2)}) copy-start(bf16[384,384]{1,0:T(8,128)(2,1)} %constant.7.clone.table) | copy-start | bytes 884740
  22.2 9.2 %copy-start.6 = (s32[32,2,128]{2,1,0:T(2,128)S(1)}, s32[32,2,128]{2,1,0:T(2,128)}, u32[]{:S(2)}) copy-start(s32[32,2,128]{2,1,0:T(2,128)} %param.13) | copy-start | bytes 98308
  22.2 9.2 %copy-start.7 = (f32[192,128]{1,0:T(8,128)S(1)}, f32[192,128]{1,0:T(8,128)}, u32[]{:S(2)}) copy-start(f32[192,128]{1,0:T(8,128)} %get-tuple-element.19.turned) | copy-start | bytes 294916
  22.2 9.2 %copy-start.8 = (f32[4]{0:T(128)S(1)}, f32[4]{0:T(128)}, u32[]{:S(2)}) copy-start(f32[4]{0:T(128)} %saturation.1) | copy-start | bytes 52
  22.2 9.2 %copy-start.9 = (f32[4]{0:T(128)S(1)}, f32[4]{0:T(128)}, u32[]{:S(2)}) copy-start(f32[4]{0:T(128)} %anisotropy.1) | copy-start | bytes 52
  22.2 9.2 %copy-start.10 = (f32[3]{0:T(128)S(1)}, f32[3]{0:T(128)}, u32[]{:S(2)}) copy-start(f32[3]{0:T(128)} %applied.1) | copy-start | bytes 40
  24.8 14.8 %copy-start.11 = (f32[4]{0:T(128)S(1)}, f32[4]{0:T(128)}, u32[]{:S(2)}) copy-start(f32[4]{0:T(128)} %damping.1) | copy-start | bytes 52
  24.8 14.8 %all-to-all-start.1 = ((f32[32,3,4,128]{3,2,1,0:T(4,128)}), f32[32,3,4,128]{3,2,1,0:T(4,128)S(1)}, u32[]{:S(2)}, u32[]{:S(2)}) async-start(f32[32,3,4,128]{3,2,1,0:T(4,128)} %bitcast.5), calls=%async_computation.1 | async-start | bytes 393216 | tf_op jit(solution)/shard_map/all_to_all | solution.py:742
  29.9 1.5 %collective-permute-start.3 = (f32[96,128]{1,0:T(8,128)}, f32[96,128]{1,0:T(8,128)S(1)}, u32[]{:S(2)}, u32[]{:S(2)}) collective-permute-start(f32[96,128]{1,0:T(8,128)} %get-tuple-element.20), channel_id=1, source_target_pairs={{2,0},{0,2},{6,4},{4,6},{10,8},{8,10},{14,12},{12,14},{18,16},{16,... | collective-permute-start | bytes 147464 | tf_op jit(solution)/shard_map/ppermute | solution.py:710
  30.2 1.2 %collective-permute-start.4 = (f32[96,128]{1,0:T(8,128)S(1)}, f32[96,128]{1,0:T(8,128)S(1)}, u32[]{:S(2)}, u32[]{:S(2)}) collective-permute-start(f32[96,128]{1,0:T(8,128)S(1)} %copy-done.12), channel_id=1, source_target_pairs={{2,4},{4,2},{6,8},{8,6},{10,12},{12,10},{14,16},{16,14},{18,20},{2... | collective-permute-start | bytes 147464 | tf_op jit(solution)/shard_map/ppermute | solution.py:712

commit v2 on v1

--- a/solution.py
+++ b/solution.py
@@ -328,14 +328,13 @@
         cosine, sine = np.cos(angle), np.sin(angle)
         sine[:, 0] = 1.0 - 2.0 * (y % 2)
         ahead_y = np.concatenate([cosine, sine], 1)
-        back_y = np.ascontiguousarray(ahead_y.T)
         x = (np.arange(self.wide)[None] * self.width_x + np.arange(self.width_x)[:, None]).reshape(-1)
         kx = np.arange(self.length_x)
         angle = 2.0 * np.pi * ((kx[:, None] * x[None]) % self.length_x) / self.length_x
         cosine, sine = np.cos(angle), np.sin(angle)
         ahead_x = np.concatenate([cosine, sine], 0)
         back_x = np.block([[cosine.T, -sine.T], [sine.T, cosine.T]])
-        return ahead_y, back_y, ahead_x, back_x
+        return ahead_y, ahead_x, back_x
 
 
 def halves(value):
@@ -345,6 +344,10 @@
 
 def mul(left, right):
     return jnp.dot(left, right, preferred_element_type=jnp.float32)
+
+
+def mul_back(left, right):
+    return lax.dot_general(left, right, (((1,), (1,)), ((), ())), preferred_element_type=jnp.float32)
 
 
 def pick(material, entries, species):
@@ -363,22 +366,21 @@
 
 
 def first_kernel(plan, species, spin_at, region_at, material_at, saturation_at, table_at, tensor,
-                 out_at, near_at, next_at, swap_at, zero_at, edge_at, turned_at,
+                 out_at, near_at, next_at, swap_at, lower_at, upper_at, turned_at, side_at, mine_at,
                  spin, region, material, saturation, table, held, held0,
-                 out, near, next_, swap, zero, edge, turned, sems, done):
-    w, _, _, other = rows_of(plan)
+                 out, near, next_, swap, lower, upper, turned, side, mine, sems, done):
+    w, n, own, other = rows_of(plan)
     count = plan.rows_x
     moves = [
         pltpu.make_async_copy(source, target, sems.at[k])
         for k, (source, target) in enumerate((
             (saturation_at, saturation), (material_at, material), (region_at, region), (spin_at, spin),
-            (table_at, table), (tensor.at[:, other], held),
+            (table_at, table), (tensor.at[:, other], held), (tensor.at[:, own], mine),
         ))
     ]
     for move in moves:
         move.start()
-    fetch0 = pltpu.make_async_copy(tensor.at[:, 0], held0, sems.at[6])
-    send0 = pltpu.make_async_copy(zero, zero_at, sems.at[7])
+    fetch0 = pltpu.make_async_copy(tensor.at[:, 0], held0, sems.at[7])
 
     @pl.when(w == 0)
     def _():
@@ -400,7 +402,6 @@
     for c in range(3):
         direction = spin[c * cells : (c + 1) * cells, :] * magnet
         turned[c * cells : (c + 1) * cells, :] = direction
-        swap[c * cells : (c + 1) * cells, plan.length_y :] = direction
         a, b = halves(direction * sat)
         high.append(a)
         low.append(b)
@@ -411,6 +412,8 @@
         rows = slice(t * count, (t + 1) * count)
         swap[rows, : plan.length_y] = held[t].astype(jnp.float32)
     send(swap, swap_at)
+    moves[6].wait()
+    send(mine, mine_at)
     moves[4].wait()
     lines = out.shape[0]
     t_high, t_low = table[:lines, :], table[lines:, :]
@@ -422,19 +425,33 @@
     next_[...] = jnp.where(w % 2 == 0, down, up)
     send(near, near_at)
     send(next_, next_at)
+    column = lax.broadcasted_iota(jnp.int32, (8, plan.width_y), 1)
+    chosen = jnp.where(column == jnp.where(n == 0, plan.width_y - 1, 0), 1.0, 0.0).astype(jnp.bfloat16)
+    high = turned[...].astype(jnp.bfloat16)
+    rest = turned[...] - high.astype(jnp.float32)
+    middle, low = halves(rest)
+    side[...] = mul_back(chosen, high) + mul_back(chosen, middle) + mul_back(chosen, low)
+    send(side, side_at)
 
     @pl.when(w == 0)
     def _():
         fetch0.wait()
+        cut = SPLIT * count
+        lower[(6 - SPLIT) * count :, :] = jnp.zeros((8, plan.length_y), jnp.float32)
+        upper[cut:, :] = jnp.zeros((8, plan.length_y), jnp.float32)
         for t in range(6):
-            zero[t * count : (t + 1) * count, :] = held0[t].astype(jnp.float32)
-            edge[t : t + 1, :] = held0[t, 0:1, :].astype(jnp.float32)
-        edge[6:8, :] = jnp.zeros((2, plan.length_y), jnp.float32)
-        send0.start()
-        last = pltpu.make_async_copy(edge, edge_at, sems.at[8])
-        last.start()
-        last.wait()
-        send0.wait()
+            values, edge = held0[t].astype(jnp.float32), held0[t, 0:1, :].astype(jnp.float32)
+            if t < SPLIT:
+                upper[t * count : (t + 1) * count, :] = values
+                lower[(6 - SPLIT) * count + t : (6 - SPLIT) * count + t + 1, :] = edge
+            else:
+                lower[(t - SPLIT) * count : (t - SPLIT + 1) * count, :] = values
+                upper[cut + t : cut + t + 1, :] = edge
+        sends = [pltpu.make_async_copy(lower, lower_at, sems.at[8]), pltpu.make_async_copy(upper, upper_at, sems.at[9])]
+        for move in sends:
+            move.start()
+        for move in sends:
+            move.wait()
 
     for move in sent:
         move.wait()
@@ -445,58 +462,42 @@
     return jnp.where((sum_of == half) | (sum_of == 0), 1.0, 0.0).astype(jnp.bfloat16)
 
 
-def own_kernel(plan, tensor, table, full, held, sems):
-    _, _, own, _ = rows_of(plan)
-    fetch = pltpu.make_async_copy(tensor.at[:, own], held, sems.at[0])
-    fetch.start()
-    half = plan.cells_y
-    flip = flip_of(half)
-    fetch.wait()
+SPLIT = 3
+
+
+def unfold_zero(plan, lower, upper, second, flip):
+    half, count = plan.cells_y, plan.rows_x
+    cut = SPLIT * count
+    row = lax.broadcasted_iota(jnp.int32, (count, count), 0)
+    col = lax.broadcasted_iota(jnp.int32, (count, count), 1)
+    turn = jnp.where(row + col == count, 1.0, 0.0).astype(jnp.bfloat16)
+    first = lax.broadcasted_iota(jnp.int32, (count, half), 0) == 0
+    lane0 = lax.broadcasted_iota(jnp.int32, (count, half), 1) == 0
+    tail_lower, tail_upper = (6 - SPLIT) * count, cut
+    tail = jnp.concatenate([lower[tail_lower:, :], upper[tail_upper:, :]], 0)
+    tail_flip = mul(tail[:, half:].astype(jnp.bfloat16), flip)
     for t in range(6):
-        values = held[t]
-        full[t, :, :half] = values[:, :half].astype(jnp.float32)
-        full[t, :, half:] = mul(values[:, half:], flip)
-
-
-def far_kernel(plan, swapped, zero_at, edge_at, full, second, zero, edge, sems):
-    w, n, _, _ = rows_of(plan)
-    half, count = plan.cells_y, plan.rows_x
-    flip = flip_of(half)
-    for t in range(6):
-        rows = slice(t * count, (t + 1) * count)
-        full[t, :, :half] = swapped[rows, :half]
-        full[t, :, half:] = mul(swapped[rows, half : 2 * half].astype(jnp.bfloat16), flip)
-
-    @pl.when(jnp.logical_and(w == plan.wide // 2, n == 1))
-    def _():
-        moves = [pltpu.make_async_copy(zero_at, zero, sems.at[0]), pltpu.make_async_copy(edge_at, edge, sems.at[1])]
-        for move in moves:
-            move.start()
-        for move in moves:
-            move.wait()
-        row = lax.broadcasted_iota(jnp.int32, (count, count), 0)
-        col = lax.broadcasted_iota(jnp.int32, (count, count), 1)
-        turn = jnp.where(row + col == count, 1.0, 0.0).astype(jnp.bfloat16)
-        first = lax.broadcasted_iota(jnp.int32, (count, half), 0) == 0
-        lane0 = lax.broadcasted_iota(jnp.int32, (count, half), 1) == 0
-        edge_low = edge[:, :half]
-        edge_high = mul(edge[:, half:].astype(jnp.bfloat16), flip)
-        for t in range(6):
-            rows = slice(t * count, (t + 1) * count)
-            plus = zero[rows, :half]
-            minus = mul(zero[rows, half:].astype(jnp.bfloat16), flip)
-            second[t, :count, :half] = plus
-            second[t, :count, half:] = minus
-            swap_plus = mul(turn, jnp.where(lane0, plus, minus).astype(jnp.bfloat16))
-            swap_minus = mul(turn, jnp.where(lane0, minus, plus).astype(jnp.bfloat16))
-            second[t, count:, :half] = jnp.where(first, edge_low[t : t + 1, :], swap_plus)
-            second[t, count:, half:] = jnp.where(first, edge_high[t : t + 1, :], swap_minus)
+        here, at, edge = (upper, t, t) if t < SPLIT else (lower, t - SPLIT, 8 + t)
+        straight, mirrored = (slice(0, count), slice(count, 2 * count))[:: 1 if t < SPLIT else -1]
+        rows = slice(at * count, (at + 1) * count)
+        plus = here[rows, :half]
+        minus = mul(here[rows, half:].astype(jnp.bfloat16), flip)
+        second[t, straight, :half] = plus
+        second[t, straight, half:] = minus
+        swap_plus = mul(turn, jnp.where(lane0, plus, minus).astype(jnp.bfloat16))
+        swap_minus = mul(turn, jnp.where(lane0, minus, plus).astype(jnp.bfloat16))
+        second[t, mirrored, :half] = jnp.where(first, tail[edge : edge + 1, :half], swap_plus)
+        second[t, mirrored, half:] = jnp.where(first, tail_flip[edge : edge + 1, :], swap_minus)
 
 
 COUPLINGS = ((0, 3, 4), (3, 1, 5), (4, 5, 2))
 
 
-def plane_kernel(plan, got, table, own_part, far_part, second, out, mixed, packed):
+def ready_kernel(table, mine, token):
+    token[...] = table[:8, :128].astype(jnp.float32) + mine[0, :8, :128].astype(jnp.float32)
+
+
+def plane_kernel(plan, got, table, mine, swapped, lower, upper, token, out, mixed, packed, parts, second):
     w, n, _, _ = rows_of(plan)
     lanes, half, wide = plan.width_y, plan.cells_y, plan.wide
     cells_x, length_x = plan.cells_x, plan.length_x
@@ -512,11 +513,21 @@
     lines = jnp.concatenate(lines, 0)
     high, low = halves(lines)
     y_high, y_low = table[:half, :], table[half : 2 * half, :]
-    base = 4 * half
+    base = 2 * half
     x_ahead = table[base : base + 2 * length_x, : 3 * cells_x]
     xb_pair = table[base : base + per_c, half : half + 4 * length_x]
     xb_low = table[base + per_c : base + 2 * per_c, half : half + 2 * length_x]
     waves = mul(high, y_high) + (mul(low, y_high) + mul(high, y_low))
+    flip = flip_of(half)
+    count = plan.rows_x
+    turned_mine = mul(jnp.concatenate([mine[t, :, half:] for t in range(6)], 0), flip)
+    turned_far = mul(swapped[:, half : 2 * half].astype(jnp.bfloat16), flip)
+    for t in range(6):
+        rows = slice(t * count, (t + 1) * count)
+        parts[t, :count, :half] = mine[t, :, :half].astype(jnp.float32)
+        parts[t, :count, half:] = turned_mine[rows, :]
+        parts[t, count:, :half] = swapped[rows, :half]
+        parts[t, count:, half:] = turned_far[rows, :]
     for g in range(6):
         a, b = halves(waves[g * cells_x : (g + 1) * cells_x, :])
         mixed[g] = mul(x_ahead, jnp.concatenate([a, b, a], 0))
@@ -528,8 +539,6 @@
                 left = slice(lane, lane + 128)
                 right = slice(half + lane, half + lane + 128)
                 cr, sr = slice(row, row + step), slice(length_x + row, length_x + row + step)
-                part = own_part if row < plan.rows_x else far_part
-                at = slice(row % plan.rows_x, row % plan.rows_x + step)
                 fields = []
                 for g in range(6):
                     cp, sp = mixed[g, cr, left], mixed[g, sr, left]
@@ -552,7 +561,7 @@
                         real = imag = None
                         for j in range(3):
                             t = COUPLINGS[i][j]
-                            ka = part[t, at, lanes_at]
+                            ka = parts[t, cr, lanes_at]
                             if paired:
                                 kb = second[t, cr, lanes_at]
                                 a, b = fields[2 * j], fields[2 * j + 1]
@@ -578,17 +587,18 @@
                         packed[i, low_at : low_at + step, lanes_at] = b
 
     special = jnp.logical_and(w == plan.wide // 2, n == 1)
-    pl.when(special)(lambda: couple(True))
+
+    @pl.when(special)
+    def _():
+        unfold_zero(plan, lower, upper, second, flip)
+        couple(True)
+
     pl.when(jnp.logical_not(special))(lambda: couple(False))
     back = []
     for i in range(3):
         back.append(mul(xb_pair, packed[i]) + mul(xb_low, packed[i, : 2 * length_x, :]))
     high, low = halves(jnp.concatenate(back, 0))
-    result = None
-    for k in (slice(0, half), slice(half, 2 * half)):
-        yb_high, yb_low = table[2 * half : 3 * half, k], table[3 * half : 4 * half, k]
-        part = mul(high[:, k], yb_high) + (mul(low[:, k], yb_high) + mul(high[:, k], yb_low))
-        result = part if result is None else result + part
+    result = mul_back(high, y_high) + (mul_back(low, y_high) + mul_back(high, y_low))
     for c in range(3):
         for j in range(2 * plan.width_x):
             row = c * 2 * plan.width_x + j
@@ -598,7 +608,7 @@
 
 
 def local_kernel(plan, species, turned, side, near, next_, material, saturation, anisotropy,
-                 applied, table, out, woven):
+                 damping, applied, table, out, damp, woven):
     w, n = lax.axis_index("wide"), lax.axis_index("narrow")
     cells, layers = plan.layers * plan.width_x, plan.layers
     row = lax.broadcasted_iota(jnp.int32, (cells, plan.width_y), 0)
@@ -608,10 +618,14 @@
     ahead = jnp.where(n == 0, 1.0, 0.0)
     sat = pick(material[...], saturation, species)
     anis = pick(material[...], anisotropy, species)
+    damp[...] = pick(material[...], damping, species)
+    square = lax.broadcasted_iota(jnp.int32, (cells, cells), 0) == lax.broadcasted_iota(
+        jnp.int32, (cells, cells), 1)
     sums, present, own = [], jnp.zeros((cells, plan.width_y), jnp.float32), []
     for c in range(3):
         d = turned[c * cells : (c + 1) * cells, :]
-        s = side[c * cells : (c + 1) * cells, :]
+        line = jnp.broadcast_to(side[0:1, c * cells : (c + 1) * cells], (cells, cells))
+        s = jnp.sum(jnp.where(square, line, 0.0), axis=1, keepdims=True)
         a, b = near[c * layers : (c + 1) * layers, :], next_[c * layers : (c + 1) * layers, :]
         woven[pl.ds(0, layers, stride=2), :] = jnp.where(w % 2 == 0, b, a)
         woven[pl.ds(1, layers, stride=2), :] = jnp.where(w % 2 == 0, a, b)
@@ -637,12 +651,14 @@
         out[c * cells : (c + 1) * cells, :] = field
 
 
-def last_kernel(plan, species, got, table, base, turned, material, damping, rate, demag):
+def last_kernel(plan, got, table, base, turned, damping, rate_at, demag_at, rate, demag, sems):
     cells = plan.layers * plan.width_x
     t_high, t_low = table[: 3 * cells, :], table[3 * cells :, :]
     high, low = halves(got[...])
     demag[...] = mul(t_high, high) + (mul(t_low, high) + mul(t_high, low))
-    damp = pick(material[...], damping, species)
+    moves = [pltpu.make_async_copy(demag, demag_at, sems.at[3])]
+    moves[0].start()
+    damp = damping[...]
     d = [turned[c * cells : (c + 1) * cells, :] for c in range(3)]
     f = [demag[c * cells : (c + 1) * cells, :] + base[c * cells : (c + 1) * cells, :] for c in range(3)]
 
@@ -653,10 +669,15 @@
     again = turn(d, torque)
     scale = -1.0 / (1.0 + damp * damp)
     for c in range(3):
-        rate[c * cells : (c + 1) * cells, :] = (torque[c] + damp * again[c]) * scale
-
-
-LIMITS = (67043328, 24 << 20, 24 << 20, 16 << 20, 24 << 20)
+        rows = pl.ds(c * cells, cells)
+        rate[rows, :] = (torque[c] + damp * again[c]) * scale
+        moves.append(pltpu.make_async_copy(rate.at[rows], rate_at.at[rows], sems.at[c]))
+        moves[-1].start()
+    for move in moves:
+        move.wait()
+
+
+LIMITS = (67043328, 4 << 20, 12 << 20, 4 << 20, 8 << 20)
 VMEM = pl.BlockSpec(memory_space=pltpu.VMEM)
 SMEM = pl.BlockSpec(memory_space=pltpu.SMEM)
 HBM = pl.BlockSpec(memory_space=pltpu.HBM)
@@ -671,8 +692,8 @@
     spin2 = spin.reshape(3 * cells, lanes)
     region2, material2 = region.reshape(cells, lanes), material.reshape(cells, lanes)
     ahead_z, back_z = plan.thickness_tables()
-    ahead_y, back_y, ahead_x, back_x = plan.lateral_tables()
-    az, bz, ay, by = (split_table(t) for t in (ahead_z, back_z, ahead_y, back_y))
+    ahead_y, ahead_x, back_x = plan.lateral_tables()
+    az, bz, ay = (split_table(t) for t in (ahead_z, back_z, ahead_y))
     ax, bx = split_table(ahead_x), split_table(back_x)
     x_ahead = np.concatenate([ax[0], ax[0], ax[1]], 1)
     xb_pair = np.concatenate([bx[0], bx[0]], 1)
@@ -686,17 +707,19 @@
 
     rows6 = 6 * plan.rows_x
     table_in, table_out = jnp.asarray(np.concatenate(az, 0)), jnp.asarray(np.concatenate(bz, 0))
-    outs = ((count, lanes), (3 * plan.layers, lanes), (3 * plan.layers, lanes), (rows6, length_y + lanes),
-            (rows6, length_y), (8, length_y), (3 * cells, lanes))
-    out, near, next_, swap, zero, edge, turned = call(
+    outs = ((count, lanes), (3 * plan.layers, lanes), (3 * plan.layers, lanes), (rows6, length_y),
+            ((6 - SPLIT) * plan.rows_x + 8, length_y), (SPLIT * plan.rows_x + 8, length_y), (3 * cells, lanes),
+            (8, 3 * cells))
+    outs = tuple(shape(o, f32) for o in outs) + (shape((6, plan.rows_x, length_y), bf16),)
+    out, near, next_, swap, lower, upper, turned, side, mine = call(
         partial(first_kernel, plan, species),
-        tuple(shape(o, f32) for o in outs), [HBM] * 6, (HBM,) * len(outs),
+        outs, [HBM] * 6, (HBM,) * len(outs),
         [pltpu.VMEM((3 * cells, lanes), f32), pltpu.VMEM((cells, lanes), jnp.int32),
          pltpu.VMEM((cells, lanes), jnp.int32), pltpu.SMEM((species,), f32),
          pltpu.VMEM(table_in.shape, bf16),
          pltpu.VMEM((6, plan.rows_x, length_y), bf16), pltpu.VMEM((6, plan.rows_x, length_y), bf16)]
-        + [pltpu.VMEM(o, f32) for o in outs]
-        + [pltpu.SemaphoreType.DMA((9,)), pltpu.SemaphoreType.DMA((5,))],
+        + [pltpu.VMEM(o.shape, o.dtype) for o in outs]
+        + [pltpu.SemaphoreType.DMA((10,)), pltpu.SemaphoreType.DMA((7,))],
         1 << 28, LIMITS[0],
     )(spin2, region2, material2, saturation, table_in, demag_spectrum)
 
@@ -704,62 +727,44 @@
     swapped = lax.ppermute(swap, "narrow", [(0, 1), (1, 0)])
     blocks = (plan.devices, 3, 2 * plan.width_x, lanes)
     got = lax.all_to_all(out.reshape(blocks), both, 0, 0, tiled=True).reshape(count, lanes)
-    edge_a = lax.ppermute(edge, both, [(0, plan.special)])
-    zero_b = lax.ppermute(zero, both, [(1, plan.special)])
+    lower = lax.ppermute(lower, both, [(0, plan.special)])
+    upper = lax.ppermute(upper, both, [(1, plan.special)])
+    side = lax.ppermute(side, "narrow", [(0, 1), (1, 0)])
     pairs = [(i ^ 1, i) for i in range(plan.wide)]
     near = lax.ppermute(near, "wide", pairs)
     pairs = [(i, j) for i in range(1, plan.wide - 1, 2) for i, j in ((i, i + 1), (i + 1, i))]
     next_ = lax.ppermute(next_, "wide", pairs)
 
     half = plan.cells_y
-    folded = [np.concatenate([t[:half], t[half:]], 1) for t in by]
     small = np.zeros((2 * length_x, 2 * half), az[0].dtype)
     small[:, : 3 * plan.cells_x] = x_ahead
     small[: 2 * plan.cells_x, half : half + 4 * length_x] = xb_pair
     small[2 * plan.cells_x : 4 * plan.cells_x, half : half + 2 * length_x] = bx[1]
-    table = jnp.asarray(np.concatenate([ay[0], ay[1], *folded, small], 0))
-
-    own_part = call(
-        partial(own_kernel, plan), shape((6, plan.rows_x, length_y), f32), [HBM, VMEM], VMEM,
-        [pltpu.VMEM((6, plan.rows_x, length_y), bf16), pltpu.SemaphoreType.DMA((1,))], 1 << 26, LIMITS[1],
-    )(demag_spectrum, table)
-    far_part, second = call(
-        partial(far_kernel, plan),
-        (shape((6, plan.rows_x, length_y), f32), shape((6, length_x, length_y), f32)),
-        [VMEM, HBM, HBM], (VMEM, VMEM),
-        [pltpu.VMEM((rows6, length_y), f32), pltpu.VMEM((8, length_y), f32), pltpu.SemaphoreType.DMA((2,))],
-        1 << 26, LIMITS[1],
-    )(swapped, zero_b, edge_a)
-
+    table = jnp.asarray(np.concatenate([ay[0], ay[1], small], 0))
+
+    token = call(ready_kernel, shape((8, 128), f32), [VMEM, VMEM], VMEM, [], 1 << 20, LIMITS[1])(table, mine)
     sent = call(
         partial(plane_kernel, plan),
         shape((count, lanes), f32),
-        [VMEM] * 5, VMEM,
-        [pltpu.VMEM((6, 2 * length_x, length_y), f32), pltpu.VMEM((3, 4 * length_x, length_y), bf16)],
+        [VMEM] * 7, VMEM,
+        [pltpu.VMEM((6, 2 * length_x, length_y), f32), pltpu.VMEM((3, 4 * length_x, length_y), bf16),
+         pltpu.VMEM((6, length_x, length_y), f32), pltpu.VMEM((6, length_x, length_y), f32)],
         1 << 29, LIMITS[2],
-    )(got, table, own_part, far_part, second)
+    )(got, table, mine, swapped, lower, upper, token)
 
     back = lax.all_to_all(sent.reshape(blocks), both, 0, 0, tiled=True).reshape(count, lanes)
-    base = pl.pallas_call(
-        partial(local_kernel, plan, species),
-        grid=(1,),
-        out_shape=shape((3 * cells, lanes), f32),
-        in_specs=[pl.BlockSpec((3 * cells, lanes), lambda i: (0, 0)),
-                  pl.BlockSpec((3 * cells, lanes), lambda i: (0, length_y // lanes)),
-                  pl.BlockSpec((3 * plan.layers, lanes), lambda i: (0, 0)),
-                  pl.BlockSpec((3 * plan.layers, lanes), lambda i: (0, 0)),
-                  pl.BlockSpec((cells, lanes), lambda i: (0, 0)), SMEM, SMEM, SMEM, VMEM],
-        out_specs=pl.BlockSpec((3 * cells, lanes), lambda i: (0, 0)),
-        scratch_shapes=[pltpu.VMEM((cells, lanes), f32)],
-        compiler_params=pltpu.CompilerParams(vmem_limit_bytes=LIMITS[3]),
-        cost_estimate=pl.CostEstimate(flops=1 << 22, bytes_accessed=1 << 19, transcendentals=0),
-    )(turned, swapped, near, next_, material2, saturation, anisotropy, applied, table_out)
+    base, damp = call(
+        partial(local_kernel, plan, species), (shape((3 * cells, lanes), f32), shape((cells, lanes), f32)),
+        [VMEM] * 5 + [SMEM] * 4 + [VMEM], (VMEM, VMEM), [pltpu.VMEM((cells, lanes), f32)], 1 << 22, LIMITS[3],
+    )(turned, side, near, next_, material2, saturation, anisotropy, damping, applied, table_out)
 
     rate, demag = call(
-        partial(last_kernel, plan, species),
+        partial(last_kernel, plan),
         (shape((3 * cells, lanes), f32), shape((3 * cells, lanes), f32)),
-        [VMEM] * 5 + [SMEM], (VMEM, VMEM), [], 1 << 28, LIMITS[4],
-    )(back, table_out, base, turned, material2, damping)
+        [VMEM] * 5, (HBM, HBM),
+        [pltpu.VMEM((3 * cells, lanes), f32), pltpu.VMEM((3 * cells, lanes), f32), pltpu.SemaphoreType.DMA((4,))],
+        1 << 28, LIMITS[4],
+    )(back, table_out, base, turned, damp)
     return rate.reshape(spin.shape), demag.reshape(spin.shape)
 
 

time: 41.5 us -> 39.3 us (0.947)
  local copies, waits for them, and re-layouts: 4.18 us -> 1.14 us
  starting transfers between devices: 20.1 us -> 21.9 us
  Pallas kernels: 7.76 us -> 6.77 us
    ppermute x2 -> x3, waiting for transfers between devices: 0.01 us -> 3.89 us  [the longest x1 2.03 us: plane_shards(): side = lax.ppermute(side, 'narrow', [(0, 1), (1, 0)])]
    all_to_all x1, waiting for transfers between devices: 7.36 us -> 3.95 us  [plane_shards(): lax.all_to_all(sent.reshape(blocks), both, 0, 0, tiled=True)]
    unnamed x26, local copies, waits for them, and re-layouts: 4.18 us -> 1.14 us
    ppermute x2 -> x3, starting transfers between devices: 6.15 us -> 7.86 us  [the longest x1 5.49 us: plane_shards(): lower = lax.ppermute(lower, both, [(0, plan.special)])]
    pallas_call x6 -> x5, Pallas kernels: 7.76 us -> 6.77 us  [the longest x1 2.57 us: plane_shards(): call(partial(first_kernel, plan, species), outs, [HBM] * 6, (HBM,) * len(...]
    ppermute x1, waiting for transfers between devices: 0.53 us -> 0.01 us  [plane_shards(): near = lax.ppermute(near, 'wide', pairs)]
  transfers between devices with their start and end apart: 7 -> 8, of which waited for: 3 -> 4; matrix products, arithmetic and copies ran while one was open for 0% -> 0% of each run, Pallas kernels for 3% -> 2%
where the time goes in v2:
time: 39.3 us; the launch traced here: 39 us
  starting transfers between devices  21.9 us (56%)
  waiting for transfers between devices  8.33 us (21%)
  Pallas kernels  6.77 us (17%)
  local copies, waits for them, and re-layouts  1.14 us (3%)
  between operations  0.82 us (2%)
    ppermute x1, starting transfers between devices, plane_shards(): lower = lax.ppermute(lower, both, [(0, plan.special)])  5.49 us
    all_to_all x1, starting transfers between devices, plane_shards(): lax.all_to_all(sent.reshape(blocks), both, 0, 0, tiled=True)  5.29 us
    all_to_all x1, starting transfers between devices, plane_shards(): lax.all_to_all(out.reshape(blocks), both, 0, 0, tiled=True)  4.75 us
    all_to_all x1, waiting for transfers between devices, plane_shards(): lax.all_to_all(sent.reshape(blocks), both, 0, 0, tiled=True)  3.95 us
    ppermute x1, starting transfers between devices, plane_shards(): swapped = lax.ppermute(swap, 'narrow', [(0, 1), (1, 0)])  3.03 us
    pallas_call x1, Pallas kernels, plane_shards(): call(partial(first_kernel, plan, species), outs, [HBM] * 6, (HBM,) * len(...  2.57 us
    pallas_call x1, Pallas kernels, plane_shards(): call(partial(plane_kernel, plan), shape((count, lanes), f32), [VMEM] * 7,...  2.38 us
    ppermute x1, waiting for transfers between devices, plane_shards(): side = lax.ppermute(side, 'narrow', [(0, 1), (1, 0)])  2.03 us
  transfers between devices with their start and end apart: 8, of which 4 were waited for; matrix products, arithmetic and copies ran while one was open for 0% of the time, Pallas kernels for 2%

profile of v2, /device:TPU:0, one launch (start us, length us, event | category | flops | bytes accessed | tf_op | source)
XLA Modules:
  0.0 39.0 jit_solution(7677650618502538663)
XLA Ops:
  0.6 2.6 %shard_map.122 = (f32[384,128]{1,0:T(8,128)}, f32[96,128]{1,0:T(8,128)}, f32[96,128]{1,0:T(8,128)}, f32[192,512]{1,0:T(8,128)}, f32[104,512]{1,0:T(8,128)}, /*in...) custom-call(f32[192,128]{1,0:T(8,128)} %bitcast.14, s32[64,128]{1,0:T(8,128)} %bitcast.15, ...), custom_call_target="tpu_custom_call" | custom-call | flops 268435456 | bytes 1048576 | tf_op jit(solution)/shard_map/pallas_call | solution.py:714
  3.2 3.0 %collective-permute-start = (f32[192,512]{1,0:T(8,128)}, f32[192,512]{1,0:T(8,128)S(1)}, u32[]{:S(2)}, u32[]{:S(2)}) collective-permute-start(f32[192,512]{1,0:T(8,128)} %get-tuple-element.17), channel_id=1, source_target_pairs={{0,1},{1,0},{2,3},{3,2},{4,5},{5,4},{6,7},{7,6},{8,9},{9,8},{10,11... | collective-permute-start | bytes 1179656 | tf_op jit(solution)/shard_map/ppermute | solution.py:727
  6.2 4.8 %all-to-all-start = ((f32[32,3,4,128]{3,2,1,0:T(4,128)}), f32[32,3,4,128]{3,2,1,0:T(4,128)S(1)}, u32[]{:S(2)}, u32[]{:S(2)}) async-start(f32[32,3,4,128]{3,2,1,0:T(4,128)} %bitcast.13), calls=%async_computation | async-start | bytes 393216 | tf_op jit(solution)/shard_map/all_to_all | solution.py:729
  11.0 5.5 %collective-permute-start.1 = (f32[104,512]{1,0:T(8,128)}, f32[104,512]{1,0:T(8,128)S(1)}, u32[]{:S(2)}, u32[]{:S(2)}) collective-permute-start(f32[104,512]{1,0:T(8,128)} %get-tuple-element.18), channel_id=1, source_target_pairs={{0,17}} | collective-permute-start | bytes 638984 | tf_op jit(solution)/shard_map/ppermute | solution.py:730
  16.5 0.7 %collective-permute-start.2 = (f32[104,512]{1,0:T(8,128)}, f32[104,512]{1,0:T(8,128)S(1)}, u32[]{:S(2)}, u32[]{:S(2)}) collective-permute-start(f32[104,512]{1,0:T(8,128)} %get-tuple-element.19), channel_id=1, source_target_pairs={{1,17}} | collective-permute-start | bytes 638984 | tf_op jit(solution)/shard_map/ppermute | solution.py:731
  17.2 0.0 copy-start
  17.2 1.1 %copy-done = bf16[640,512]{1,0:T(8,128)(2,1)S(1)} copy-done((bf16[640,512]{1,0:T(8,128)(2,1)S(1)}, bf16[640,512]{1,0:T(8,128)(2,1)}, u32[]{:S(2)}) %copy-start) | copy-done | bytes 655384
  18.3 1.9 %collective-permute-done.1.lower = f32[104,512]{1,0:T(8,128)S(1)} collective-permute-done((f32[104,512]{1,0:T(8,128)}, f32[104,512]{1,0:T(8,128)S(1)}, u32[]{:S(2)}, u32[]{:S(2)}) %collective-permute-start.1) | collective-permute-done | bytes 213024 | tf_op jit(solution)/shard_map/ppermute | solution.py:730
  20.2 0.0 collective-permute-done.2.upper
  20.2 0.5 %all-to-all-done = f32[32,3,4,128]{3,2,1,0:T(4,128)S(1)} async-done(((f32[32,3,4,128]{3,2,1,0:T(4,128)}), f32[32,3,4,128]{3,2,1,0:T(4,128)S(1)}, u32[]{:S(2)}, u32[]{:S(2)}) %all-to-all-start) | async-done | bytes 196640 | tf_op jit(solution)/shard_map/all_to_all | solution.py:729
  20.6 0.0 collective-permute-done.swapped
  20.6 0.0 copy-done.1
  20.7 0.0 copy-start.5
  20.7 2.4 %shard_map.124 = f32[384,128]{1,0:T(8,128)} custom-call(f32[384,128]{1,0:T(8,128)S(1)} %bitcast.9, bf16[640,512]{1,0:T(8,128)(2,1)S(1)} %copy-done.1, bf16[6,32,512]{2,1,0:T(8,128)(2,1)S(1)} %copy-done.2, f32[192,512]{1,0:T(8,128)S(1)} %collective-permute-done.swapped, f32[104,512]{1,0:T(8,128)S(1)} %collective-permute-done.1.lower, ...), custom_call_target="tpu_custom_call" | custom-call | flops 536870912 | bytes 1048576 | tf_op jit(solution)/shard_map/pallas_call | solution.py:746
  23.1 5.3 %all-to-all-start.1 = ((f32[32,3,4,128]{3,2,1,0:T(4,128)}), f32[32,3,4,128]{3,2,1,0:T(4,128)S(1)}, u32[]{:S(2)}, u32[]{:S(2)}) async-start(f32[32,3,4,128]{3,2,1,0:T(4,128)} %bitcast.5), calls=%async_computation.1 | async-start | bytes 393216 | tf_op jit(solution)/shard_map/all_to_all | solution.py:755
  28.4 0.3 collective-permute-start.4
  28.7 0.7 %collective-permute-start.5 = (f32[96,128]{1,0:T(8,128)S(1)}, f32[96,128]{1,0:T(8,128)S(1)}, u32[]{:S(2)}, u32[]{:S(2)}) collective-permute-start(f32[96,128]{1,0:T(8,128)S(1)} %copy-done.10), channel_id=1, source_target_pairs={{2,4},{4,2},{6,8},{8,6},{10,12},{12,10},{14,16},{16,14},{18,20},{2... | collective-permute-start | bytes 147464 | tf_op jit(solution)/shard_map/ppermute | solution.py:736
  29.3 0.0 copy-start.9
  29.4 0.0 copy-start.6
  29.4 0.0 copy-start.7
  29.4 0.0 copy-start.8
  29.4 1.7 %collective-permute-start.3 = (f32[8,192]{1,0:T(8,128)S(1)}, f32[8,192]{1,0:T(8,128)S(1)}, u32[]{:S(2)}, u32[]{:S(2)}) collective-permute-start(f32[8,192]{1,0:T(8,128)S(1)} %copy-done.12), channel_id=1, source_target_pairs={{0,1},{1,0},{2,3},{3,2},{4,5},{5,4},{6,7},{7,6},{8,9},{9,8},{10,11... | collective-permute-start | bytes 18440 | tf_op jit(solution)/shard_map/ppermute | solution.py:732
  31.1 2.0 %collective-permute-done.3.side = f32[8,192]{1,0:T(8,128)S(1)} collective-permute-done((f32[8,192]{1,0:T(8,128)S(1)}, f32[8,192]{1,0:T(8,128)S(1)}, u32[]{:S(2)}, u32[]{:S(2)}) %collective-permute-start.3) | collective-permute-done | bytes 6176 | tf_op jit(solution)/shard_map/ppermute | solution.py:732
  33.1 0.0 collective-permute-done.4.near
  33.1 0.0 collective-permute-done.5.next_
  33.1 0.0 copy-done.3
  33.2 0.0 copy-done.4
  33.2 0.0 copy-done.9
  33.2 0.0 copy-done.6
  33.2 0.8 %shard_map.125 = (f32[192,128]{1,0:T(8,128)S(1)}, f32[64,128]{1,0:T(8,128)S(1)}) custom-call(f32[192,128]{1,0:T(8,128)S(1)} %copy-done.5, f32[8,192]{1,0:T(8,128)S(1)} %collective-permute-done.3.side, f32[96,128]{1,0:T(8,128)S(1)} %collective-permute-done.4.near, f32[96,128]{1,0:T(8,128)S(1)} %collective-permute-done.5.next_, s32[64,128]{1,0:T(8,128)S(1)} %bitcast.12, ...), custom_call_target="tpu_custom_call" | custom-call | flops 4194304 | bytes 1048576 | tf_op jit(solution)/shard_map/pallas_call | solution.py:756
  34.0 3.9 %all-to-all-done.1 = f32[32,3,4,128]{3,2,1,0:T(4,128)S(1)} async-done(((f32[32,3,4,128]{3,2,1,0:T(4,128)}), f32[32,3,4,128]{3,2,1,0:T(4,128)S(1)}, u32[]{:S(2)}, u32[]{:S(2)}) %all-to-all-start.1) | async-done | bytes 196640 | tf_op jit(solution)/shard_map/all_to_all | solution.py:755
  38.0 1.0 %shard_map.126 = (f32[192,128]{1,0:T(8,128)}, f32[192,128]{1,0:T(8,128)}) custom-call(f32[384,128]{1,0:T(8,128)S(1)} %bitcast.10, bf16[384,384]{1,0:T(8,128)(2,1)S(1)} %copy-done.3, f32[192,128]{1,0:T(8,128)S(1)} %get-tuple-element.24.base, f32[192,128]{1,0:T(8,128)S(1)} %copy-done.5, f32[64,128]{1,0:T(8,128)S(1)} %get-tuple-element.25.damping), custom_call_target="tpu_custom_call" | custom-call | flops 268435456 | bytes 1048576 | tf_op jit(solution)/shard_map/pallas_call | solution.py:761
  (15 shorter events, 0.0 us)
Async XLA Ops:
  3.2 17.4 %collective-permute-start = (f32[192,512]{1,0:T(8,128)}, f32[192,512]{1,0:T(8,128)S(1)}, u32[]{:S(2)}, u32[]{:S(2)}) collective-permute-start(f32[192,512]{1,0:T(8,128)} %get-tuple-element.17), channel_id=1, source_target_pairs={{0,1},{1,0},{2,3},{3,2},{4,5},{5,4},{6,7},{7,6},{8,9},{9,8},{10,11... | collective-permute-start | bytes 1179656 | tf_op jit(solution)/shard_map/ppermute | solution.py:727
  6.2 10.9 %copy-start.2 = (bf16[6,32,512]{2,1,0:T(8,128)(2,1)S(1)}, bf16[6,32,512]{2,1,0:T(8,128)(2,1)}, u32[]{:S(2)}) copy-start(bf16[6,32,512]{2,1,0:T(8,128)(2,1)} %get-tuple-element.16.mine) | copy-start | bytes 589828
  6.2 14.4 %all-to-all-start = ((f32[32,3,4,128]{3,2,1,0:T(4,128)}), f32[32,3,4,128]{3,2,1,0:T(4,128)S(1)}, u32[]{:S(2)}, u32[]{:S(2)}) async-start(f32[32,3,4,128]{3,2,1,0:T(4,128)} %bitcast.13), calls=%async_computation | async-start | bytes 393216 | tf_op jit(solution)/shard_map/all_to_all | solution.py:729
  11.0 9.1 %collective-permute-start.1 = (f32[104,512]{1,0:T(8,128)}, f32[104,512]{1,0:T(8,128)S(1)}, u32[]{:S(2)}, u32[]{:S(2)}) collective-permute-start(f32[104,512]{1,0:T(8,128)} %get-tuple-element.18), channel_id=1, source_target_pairs={{0,17}} | collective-permute-start | bytes 638984 | tf_op jit(solution)/shard_map/ppermute | solution.py:730
  16.5 3.7 %collective-permute-start.2 = (f32[104,512]{1,0:T(8,128)}, f32[104,512]{1,0:T(8,128)S(1)}, u32[]{:S(2)}, u32[]{:S(2)}) collective-permute-start(f32[104,512]{1,0:T(8,128)} %get-tuple-element.19), channel_id=1, source_target_pairs={{1,17}} | collective-permute-start | bytes 638984 | tf_op jit(solution)/shard_map/ppermute | solution.py:731
  17.2 1.1 %copy-start = (bf16[640,512]{1,0:T(8,128)(2,1)S(1)}, bf16[640,512]{1,0:T(8,128)(2,1)}, u32[]{:S(2)}) copy-start(bf16[640,512]{1,0:T(8,128)(2,1)} %constant.8.clone.table) | copy-start | bytes 1966084
  18.3 2.4 %copy-start.1 = (bf16[640,512]{1,0:T(8,128)(2,1)S(1)}, bf16[640,512]{1,0:T(8,128)(2,1)}, u32[]{:S(2)}) copy-start(bf16[640,512]{1,0:T(8,128)(2,1)} %constant.8.clone.table) | copy-start | bytes 1966084
  20.6 7.7 %copy-start.11 = (f32[96,128]{1,0:T(8,128)S(1)}, f32[96,128]{1,0:T(8,128)}, u32[]{:S(2)}) copy-start(f32[96,128]{1,0:T(8,128)} %get-tuple-element.22) | copy-start | bytes 147460
  20.7 12.5 %copy-start.5 = (f32[192,128]{1,0:T(8,128)S(1)}, f32[192,128]{1,0:T(8,128)}, u32[]{:S(2)}) copy-start(f32[192,128]{1,0:T(8,128)} %get-tuple-element.20.turned) | copy-start | bytes 294916
  23.0 10.1 %copy-start.3 = (bf16[384,384]{1,0:T(8,128)(2,1)S(1)}, bf16[384,384]{1,0:T(8,128)(2,1)}, u32[]{:S(2)}) copy-start(bf16[384,384]{1,0:T(8,128)(2,1)} %constant.7.clone.table) | copy-start | bytes 884740
  23.0 5.6 %copy-start.10 = (f32[96,128]{1,0:T(8,128)S(1)}, f32[96,128]{1,0:T(8,128)}, u32[]{:S(2)}) copy-start(f32[96,128]{1,0:T(8,128)} %get-tuple-element.23) | copy-start | bytes 147460
  23.0 6.3 %copy-start.12 = (f32[8,192]{1,0:T(8,128)S(1)}, f32[8,192]{1,0:T(8,128)}, u32[]{:S(2)}) copy-start(f32[8,192]{1,0:T(8,128)} %get-tuple-element.21) | copy-start | bytes 18436
  23.0 10.1 %copy-start.4 = (s32[32,2,128]{2,1,0:T(2,128)S(1)}, s32[32,2,128]{2,1,0:T(2,128)}, u32[]{:S(2)}) copy-start(s32[32,2,128]{2,1,0:T(2,128)} %param.13) | copy-start | bytes 98308
  23.1 14.9 %all-to-all-start.1 = ((f32[32,3,4,128]{3,2,1,0:T(4,128)}), f32[32,3,4,128]{3,2,1,0:T(4,128)S(1)}, u32[]{:S(2)}, u32[]{:S(2)}) async-start(f32[32,3,4,128]{3,2,1,0:T(4,128)} %bitcast.5), calls=%async_computation.1 | async-start | bytes 393216 | tf_op jit(solution)/shard_map/all_to_all | solution.py:755
  28.4 4.8 %collective-permute-start.4 = (f32[96,128]{1,0:T(8,128)S(1)}, f32[96,128]{1,0:T(8,128)S(1)}, u32[]{:S(2)}, u32[]{:S(2)}) collective-permute-start(f32[96,128]{1,0:T(8,128)S(1)} %copy-done.11), channel_id=1, source_target_pairs={{2,0},{0,2},{6,4},{4,6},{10,8},{8,10},{14,12},{12,14},{18,16},{16,... | collective-permute-start | bytes 147464 | tf_op jit(solution)/shard_map/ppermute | solution.py:734
  28.7 4.5 %collective-permute-start.5 = (f32[96,128]{1,0:T(8,128)S(1)}, f32[96,128]{1,0:T(8,128)S(1)}, u32[]{:S(2)}, u32[]{:S(2)}) collective-permute-start(f32[96,128]{1,0:T(8,128)S(1)} %copy-done.10), channel_id=1, source_target_pairs={{2,4},{4,2},{6,8},{8,6},{10,12},{12,10},{14,16},{16,14},{18,20},{2... | collective-permute-start | bytes 147464 | tf_op jit(solution)/shard_map/ppermute | solution.py:736
  29.3 3.8 %copy-start.9 = (f32[3]{0:T(128)S(1)}, f32[3]{0:T(128)}, u32[]{:S(2)}) copy-start(f32[3]{0:T(128)} %applied.1) | copy-start | bytes 40
  29.4 3.8 %copy-start.6 = (f32[4]{0:T(128)S(1)}, f32[4]{0:T(128)}, u32[]{:S(2)}) copy-start(f32[4]{0:T(128)} %saturation.1) | copy-start | bytes 52
  29.4 3.8 %copy-start.7 = (f32[4]{0:T(128)S(1)}, f32[4]{0:T(128)}, u32[]{:S(2)}) copy-start(f32[4]{0:T(128)} %anisotropy.1) | copy-start | bytes 52
  29.4 3.8 %copy-start.8 = (f32[4]{0:T(128)S(1)}, f32[4]{0:T(128)}, u32[]{:S(2)}) copy-start(f32[4]{0:T(128)} %damping.1) | copy-start | bytes 52
  29.4 3.7 %collective-permute-start.3 = (f32[8,192]{1,0:T(8,128)S(1)}, f32[8,192]{1,0:T(8,128)S(1)}, u32[]{:S(2)}, u32[]{:S(2)}) collective-permute-start(f32[8,192]{1,0:T(8,128)S(1)} %copy-done.12), channel_id=1, source_target_pairs={{0,1},{1,0},{2,3},{3,2},{4,5},{5,4},{6,7},{7,6},{8,9},{9,8},{10,11... | collective-permute-start | bytes 18440 | tf_op jit(solution)/shard_map/ppermute | solution.py:732

commit v3 on v2

--- a/solution.py
+++ b/solution.py
@@ -315,11 +315,11 @@
         x = np.arange(self.width_x)
         sign = 1.0 - 2.0 * ((n[:, None] * x[None]) % 2)
         unit_c, unit_x = np.eye(3), np.eye(self.width_x)
-        ahead = np.einsum("drz,dx,cb,xv->dcrxbzv", ahead, sign, unit_c, unit_x)
+        ahead = np.einsum("drz,dx,xv->rxdzv", ahead, sign, unit_x)
         back = np.einsum("drz,dx,cb,xv->bzvdcrx", back, sign, unit_c, unit_x)
         count = self.devices * 6 * self.width_x
         cells = 3 * self.layers * self.width_x
-        return ahead.reshape(count, cells), back.reshape(cells, count)
+        return ahead.reshape(count // 3, cells // 3), back.reshape(cells, count)
 
     def lateral_tables(self):
         half = self.cells_y
@@ -366,16 +366,16 @@
 
 
 def first_kernel(plan, species, spin_at, region_at, material_at, saturation_at, table_at, tensor,
-                 out_at, near_at, next_at, swap_at, lower_at, upper_at, turned_at, side_at, mine_at,
+                 out_at, near_at, next_at, swap_at, lower_at, upper_at, turned_at, side_at,
                  spin, region, material, saturation, table, held, held0,
-                 out, near, next_, swap, lower, upper, turned, side, mine, sems, done):
-    w, n, own, other = rows_of(plan)
+                 out, near, next_, swap, lower, upper, turned, side, sems, done):
+    w, n, _, other = rows_of(plan)
     count = plan.rows_x
     moves = [
         pltpu.make_async_copy(source, target, sems.at[k])
         for k, (source, target) in enumerate((
             (saturation_at, saturation), (material_at, material), (region_at, region), (spin_at, spin),
-            (table_at, table), (tensor.at[:, other], held), (tensor.at[:, own], mine),
+            (table_at, table), (tensor.at[:, other], held),
         ))
     ]
     for move in moves:
@@ -405,19 +405,20 @@
         a, b = halves(direction * sat)
         high.append(a)
         low.append(b)
-    high, low = jnp.concatenate(high, 0), jnp.concatenate(low, 0)
+    high, low = jnp.concatenate(high, 1), jnp.concatenate(low, 1)
     send(turned, turned_at)
     moves[5].wait()
     for t in range(6):
         rows = slice(t * count, (t + 1) * count)
         swap[rows, : plan.length_y] = held[t].astype(jnp.float32)
     send(swap, swap_at)
-    moves[6].wait()
-    send(mine, mine_at)
     moves[4].wait()
-    lines = out.shape[0]
-    t_high, t_low = table[:lines, :], table[lines:, :]
-    out[...] = mul(t_high, high) + (mul(t_low, high) + mul(t_high, low))
+    result = mul(table[...], jnp.concatenate([high, low, high], 0))
+    group, lanes = plan.devices, plan.width_y
+    for c in range(3):
+        for j in range(2 * plan.width_x):
+            out[pl.ds(c * 2 * plan.width_x + j, group, stride=6 * plan.width_x), :] = result[
+                j * group : (j + 1) * group, c * lanes : (c + 1) * lanes]
     send(out, out_at)
     layers3 = 3 * plan.layers
     up, down = turned[pl.ds(1, layers3, stride=2), :], turned[pl.ds(0, layers3, stride=2), :]
@@ -436,11 +437,15 @@
     @pl.when(w == 0)
     def _():
         fetch0.wait()
-        cut = SPLIT * count
+        cut, half = SPLIT * count, plan.cells_y
+        flip = flip_of(half)
+        minus = mul(jnp.concatenate([held0[t, :, half:] for t in range(6)], 0), flip)
         lower[(6 - SPLIT) * count :, :] = jnp.zeros((8, plan.length_y), jnp.float32)
         upper[cut:, :] = jnp.zeros((8, plan.length_y), jnp.float32)
         for t in range(6):
-            values, edge = held0[t].astype(jnp.float32), held0[t, 0:1, :].astype(jnp.float32)
+            plus = held0[t, :, :half].astype(jnp.float32)
+            values = jnp.concatenate([plus, minus[t * count : (t + 1) * count, :]], 1)
+            edge = values[0:1, :]
             if t < SPLIT:
                 upper[t * count : (t + 1) * count, :] = values
                 lower[(6 - SPLIT) * count + t : (6 - SPLIT) * count + t + 1, :] = edge
@@ -465,45 +470,44 @@
 SPLIT = 3
 
 
-def unfold_zero(plan, lower, upper, second, flip):
+def unfold_zero(plan, lower, upper, second):
     half, count = plan.cells_y, plan.rows_x
-    cut = SPLIT * count
     row = lax.broadcasted_iota(jnp.int32, (count, count), 0)
     col = lax.broadcasted_iota(jnp.int32, (count, count), 1)
     turn = jnp.where(row + col == count, 1.0, 0.0).astype(jnp.bfloat16)
-    first = lax.broadcasted_iota(jnp.int32, (count, half), 0) == 0
+    first = lax.broadcasted_iota(jnp.int32, (count, 2 * half), 0) == 0
     lane0 = lax.broadcasted_iota(jnp.int32, (count, half), 1) == 0
-    tail_lower, tail_upper = (6 - SPLIT) * count, cut
-    tail = jnp.concatenate([lower[tail_lower:, :], upper[tail_upper:, :]], 0)
-    tail_flip = mul(tail[:, half:].astype(jnp.bfloat16), flip)
     for t in range(6):
-        here, at, edge = (upper, t, t) if t < SPLIT else (lower, t - SPLIT, 8 + t)
+        here, at, there, edge = (
+            (upper, t, lower, (6 - SPLIT) * count + t) if t < SPLIT else (lower, t - SPLIT, upper, SPLIT * count + t)
+        )
         straight, mirrored = (slice(0, count), slice(count, 2 * count))[:: 1 if t < SPLIT else -1]
         rows = slice(at * count, (at + 1) * count)
-        plus = here[rows, :half]
-        minus = mul(here[rows, half:].astype(jnp.bfloat16), flip)
+        plus, minus = here[rows, :half], here[rows, half:]
         second[t, straight, :half] = plus
         second[t, straight, half:] = minus
-        swap_plus = mul(turn, jnp.where(lane0, plus, minus).astype(jnp.bfloat16))
-        swap_minus = mul(turn, jnp.where(lane0, minus, plus).astype(jnp.bfloat16))
-        second[t, mirrored, :half] = jnp.where(first, tail[edge : edge + 1, :half], swap_plus)
-        second[t, mirrored, half:] = jnp.where(first, tail_flip[edge : edge + 1, :], swap_minus)
+        crossed = jnp.concatenate([jnp.where(lane0, plus, minus), jnp.where(lane0, minus, plus)], 1)
+        crossed = mul(turn, crossed.astype(jnp.bfloat16))
+        second[t, mirrored, :] = jnp.where(first, there[edge : edge + 1, :], crossed)
 
 
 COUPLINGS = ((0, 3, 4), (3, 1, 5), (4, 5, 2))
 
 
-def ready_kernel(table, mine, token):
-    token[...] = table[:8, :128].astype(jnp.float32) + mine[0, :8, :128].astype(jnp.float32)
-
-
-def plane_kernel(plan, got, table, mine, swapped, lower, upper, token, out, mixed, packed, parts, second):
-    w, n, _, _ = rows_of(plan)
-    lanes, half, wide = plan.width_y, plan.cells_y, plan.wide
-    cells_x, length_x = plan.cells_x, plan.length_x
+def ready_kernel(plan, tensor, table_at, own_part, table):
+    _, _, own, _ = rows_of(plan)
+    half, count = plan.cells_y, plan.rows_x
+    table[...] = table_at[...]
+    turned = mul(jnp.concatenate([tensor[t, own, :, half:] for t in range(6)], 0), flip_of(half))
+    for t in range(6):
+        own_part[t, :, :half] = tensor[t, own, :, :half].astype(jnp.float32)
+        own_part[t, :, half:] = turned[t * count : (t + 1) * count, :]
+
+
+def ahead_kernel(plan, got, table, swapped, mixed, far_part):
+    half, wide = plan.cells_y, plan.wide
+    cells_x, length_x, narrow = plan.cells_x, plan.length_x, plan.narrow
     block = 6 * plan.width_x
-    per_c = 2 * cells_x
-    narrow = plan.narrow
     lines = []
     for c in range(3):
         for j in range(2 * plan.width_x):
@@ -513,24 +517,29 @@
     lines = jnp.concatenate(lines, 0)
     high, low = halves(lines)
     y_high, y_low = table[:half, :], table[half : 2 * half, :]
-    base = 2 * half
-    x_ahead = table[base : base + 2 * length_x, : 3 * cells_x]
-    xb_pair = table[base : base + per_c, half : half + 4 * length_x]
-    xb_low = table[base + per_c : base + 2 * per_c, half : half + 2 * length_x]
+    x_ahead = table[2 * half : 2 * half + 2 * length_x, : 3 * cells_x]
     waves = mul(high, y_high) + (mul(low, y_high) + mul(high, y_low))
     flip = flip_of(half)
     count = plan.rows_x
-    turned_mine = mul(jnp.concatenate([mine[t, :, half:] for t in range(6)], 0), flip)
     turned_far = mul(swapped[:, half : 2 * half].astype(jnp.bfloat16), flip)
     for t in range(6):
         rows = slice(t * count, (t + 1) * count)
-        parts[t, :count, :half] = mine[t, :, :half].astype(jnp.float32)
-        parts[t, :count, half:] = turned_mine[rows, :]
-        parts[t, count:, :half] = swapped[rows, :half]
-        parts[t, count:, half:] = turned_far[rows, :]
+        far_part[t, :, :half] = swapped[rows, :half]
+        far_part[t, :, half:] = turned_far[rows, :]
     for g in range(6):
         a, b = halves(waves[g * cells_x : (g + 1) * cells_x, :])
         mixed[g] = mul(x_ahead, jnp.concatenate([a, b, a], 0))
+
+
+def back_kernel(plan, mixed, own_part, far_part, table, lower, upper, out, packed, second):
+    w, n, _, _ = rows_of(plan)
+    lanes, half, wide = plan.width_y, plan.cells_y, plan.wide
+    length_x, narrow = plan.length_x, plan.narrow
+    block, per_c = 6 * plan.width_x, 2 * plan.cells_x
+    y_high, y_low = table[:half, :], table[half : 2 * half, :]
+    base = 2 * half
+    xb_pair = table[base : base + per_c, half : half + 4 * length_x]
+    xb_low = table[base + per_c : base + 2 * per_c, half : half + 2 * length_x]
     step = 16
 
     def couple(paired):
@@ -539,6 +548,8 @@
                 left = slice(lane, lane + 128)
                 right = slice(half + lane, half + lane + 128)
                 cr, sr = slice(row, row + step), slice(length_x + row, length_x + row + step)
+                part = own_part if row < plan.rows_x else far_part
+                at = slice(row % plan.rows_x, row % plan.rows_x + step)
                 fields = []
                 for g in range(6):
                     cp, sp = mixed[g, cr, left], mixed[g, sr, left]
@@ -561,7 +572,7 @@
                         real = imag = None
                         for j in range(3):
                             t = COUPLINGS[i][j]
-                            ka = parts[t, cr, lanes_at]
+                            ka = part[t, at, lanes_at]
                             if paired:
                                 kb = second[t, cr, lanes_at]
                                 a, b = fields[2 * j], fields[2 * j + 1]
@@ -590,7 +601,7 @@
 
     @pl.when(special)
     def _():
-        unfold_zero(plan, lower, upper, second, flip)
+        unfold_zero(plan, lower, upper, second)
         couple(True)
 
     pl.when(jnp.logical_not(special))(lambda: couple(False))
@@ -677,7 +688,7 @@
         move.wait()
 
 
-LIMITS = (67043328, 4 << 20, 12 << 20, 4 << 20, 8 << 20)
+LIMITS = (67043328, 8 << 20, 8 << 20, 4 << 20, 8 << 20)
 VMEM = pl.BlockSpec(memory_space=pltpu.VMEM)
 SMEM = pl.BlockSpec(memory_space=pltpu.SMEM)
 HBM = pl.BlockSpec(memory_space=pltpu.HBM)
@@ -706,12 +717,20 @@
         )
 
     rows6 = 6 * plan.rows_x
-    table_in, table_out = jnp.asarray(np.concatenate(az, 0)), jnp.asarray(np.concatenate(bz, 0))
+    table_in = jnp.asarray(np.concatenate([az[0], az[0], az[1]], 1))
+    table_out = jnp.asarray(np.concatenate(bz, 0))
     outs = ((count, lanes), (3 * plan.layers, lanes), (3 * plan.layers, lanes), (rows6, length_y),
             ((6 - SPLIT) * plan.rows_x + 8, length_y), (SPLIT * plan.rows_x + 8, length_y), (3 * cells, lanes),
             (8, 3 * cells))
-    outs = tuple(shape(o, f32) for o in outs) + (shape((6, plan.rows_x, length_y), bf16),)
-    out, near, next_, swap, lower, upper, turned, side, mine = call(
+    outs = tuple(shape(o, f32) for o in outs)
+    half = plan.cells_y
+    small = np.zeros((2 * length_x, 2 * half), ax[0].dtype)
+    small[:, : 3 * plan.cells_x] = x_ahead
+    small[: 2 * plan.cells_x, half : half + 4 * length_x] = xb_pair
+    small[2 * plan.cells_x : 4 * plan.cells_x, half : half + 2 * length_x] = bx[1]
+    table = jnp.asarray(np.concatenate([ay[0], ay[1], small], 0))
+
+    out, near, next_, swap, lower, upper, turned, side = call(
         partial(first_kernel, plan, species),
         outs, [HBM] * 6, (HBM,) * len(outs),
         [pltpu.VMEM((3 * cells, lanes), f32), pltpu.VMEM((cells, lanes), jnp.int32),
@@ -719,7 +738,7 @@
          pltpu.VMEM(table_in.shape, bf16),
          pltpu.VMEM((6, plan.rows_x, length_y), bf16), pltpu.VMEM((6, plan.rows_x, length_y), bf16)]
         + [pltpu.VMEM(o.shape, o.dtype) for o in outs]
-        + [pltpu.SemaphoreType.DMA((10,)), pltpu.SemaphoreType.DMA((7,))],
+        + [pltpu.SemaphoreType.DMA((10,)), pltpu.SemaphoreType.DMA((6,))],
         1 << 28, LIMITS[0],
     )(spin2, region2, material2, saturation, table_in, demag_spectrum)
 
@@ -735,22 +754,22 @@
     pairs = [(i, j) for i in range(1, plan.wide - 1, 2) for i, j in ((i, i + 1), (i + 1, i))]
     next_ = lax.ppermute(next_, "wide", pairs)
 
-    half = plan.cells_y
-    small = np.zeros((2 * length_x, 2 * half), az[0].dtype)
-    small[:, : 3 * plan.cells_x] = x_ahead
-    small[: 2 * plan.cells_x, half : half + 4 * length_x] = xb_pair
-    small[2 * plan.cells_x : 4 * plan.cells_x, half : half + 2 * length_x] = bx[1]
-    table = jnp.asarray(np.concatenate([ay[0], ay[1], small], 0))
-
-    token = call(ready_kernel, shape((8, 128), f32), [VMEM, VMEM], VMEM, [], 1 << 20, LIMITS[1])(table, mine)
+    half_shape = shape((6, plan.rows_x, length_y), f32)
+    own_part, table = call(
+        partial(ready_kernel, plan), (half_shape, shape(table.shape, bf16)), [VMEM] * 2, (VMEM, VMEM), [],
+        1 << 26, LIMITS[1],
+    )(demag_spectrum, table)
+    mixed, far_part = call(
+        partial(ahead_kernel, plan), (shape((6, 2 * length_x, length_y), f32), half_shape),
+        [VMEM] * 3, (VMEM, VMEM), [], 1 << 29, LIMITS[2],
+    )(got, table, swapped)
     sent = call(
-        partial(plane_kernel, plan),
+        partial(back_kernel, plan),
         shape((count, lanes), f32),
-        [VMEM] * 7, VMEM,
-        [pltpu.VMEM((6, 2 * length_x, length_y), f32), pltpu.VMEM((3, 4 * length_x, length_y), bf16),
-         pltpu.VMEM((6, length_x, length_y), f32), pltpu.VMEM((6, length_x, length_y), f32)],
+        [VMEM] * 6, VMEM,
+        [pltpu.VMEM((3, 4 * length_x, length_y), bf16), pltpu.VMEM((6, length_x, length_y), f32)],
         1 << 29, LIMITS[2],
-    )(got, table, mine, swapped, lower, upper, token)
+    )(mixed, own_part, far_part, table, lower, upper)
 
     back = lax.all_to_all(sent.reshape(blocks), both, 0, 0, tiled=True).reshape(count, lanes)
     base, damp = call(

time: 39.3 us -> 37.9 us (0.964)
  starting transfers between devices: 21.9 us -> 20.4 us
  waiting for transfers between devices: 8.33 us -> 7.06 us
  local copies, waits for them, and re-layouts: 1.14 us -> 2.27 us
    ppermute x1, waiting for transfers between devices: 1.86 us -> 0.01 us  [plane_shards(): lower = lax.ppermute(lower, both, [(0, plan.special)])]
    all_to_all x1, starting transfers between devices: 5.29 us -> 3.94 us  [plane_shards(): lax.all_to_all(sent.reshape(blocks), both, 0, 0, tiled=True)]
    unnamed x26 -> x24, local copies, waits for them, and re-layouts: 1.14 us -> 2.27 us
    all_to_all x1, waiting for transfers between devices: 0.48 us -> 1.02 us  [plane_shards(): lax.all_to_all(out.reshape(blocks), both, 0, 0, tiled=True)]
    pallas_call x2 -> x3, Pallas kernels: 2.38 us -> 2.66 us  [the longest x1 1.78 us: plane_shards(): call(partial(back_kernel, plan), shape((count, lanes), f32), [VMEM] * 6,...]
  transfers between devices with their start and end apart: 8 -> 8, of which waited for: 4 -> 3; matrix products, arithmetic and copies ran while one was open for 0% -> 0% of each run, Pallas kernels for 2% -> 5%
where the time goes in v3:
time: 37.9 us; the launch traced here: 37.5 us
  starting transfers between devices  20.4 us (54%)
  waiting for transfers between devices  7.06 us (19%)
  Pallas kernels  6.89 us (18%)
  local copies, waits for them, and re-layouts  2.27 us (6%)
  between operations  0.87 us (2%)
    ppermute x1, starting transfers between devices, plane_shards(): lower = lax.ppermute(lower, both, [(0, plan.special)])  5.49 us
    all_to_all x1, starting transfers between devices, plane_shards(): lax.all_to_all(out.reshape(blocks), both, 0, 0, tiled=True)  4.63 us
    all_to_all x1, waiting for transfers between devices, plane_shards(): lax.all_to_all(sent.reshape(blocks), both, 0, 0, tiled=True)  3.99 us
    all_to_all x1, starting transfers between devices, plane_shards(): lax.all_to_all(sent.reshape(blocks), both, 0, 0, tiled=True)  3.94 us
    ppermute x1, starting transfers between devices, plane_shards(): swapped = lax.ppermute(swap, 'narrow', [(0, 1), (1, 0)])  3.03 us
    pallas_call x1, Pallas kernels, plane_shards(): call(partial(first_kernel, plan, species), outs, [HBM] * 6, (HBM,) * len(...  2.42 us
    unnamed x24, local copies, waits for them, and re-layouts  2.27 us
    ppermute x1, waiting for transfers between devices, plane_shards(): side = lax.ppermute(side, 'narrow', [(0, 1), (1, 0)])  2.03 us
  transfers between devices with their start and end apart: 8, of which 3 were waited for; matrix products, arithmetic and copies ran while one was open for 0% of the time, Pallas kernels for 5%

profile of v3, /device:TPU:0, one launch (start us, length us, event | category | flops | bytes accessed | tf_op | source)
XLA Modules:
  0.0 37.5 jit_solution(3565508947875447502)
XLA Ops:
  0.6 2.4 %shard_map.122 = (f32[384,128]{1,0:T(8,128)}, f32[96,128]{1,0:T(8,128)}, f32[96,128]{1,0:T(8,128)}, f32[192,512]{1,0:T(8,128)}, f32[104,512]{1,0:T(8,128)}, /*in...) custom-call(f32[192,128]{1,0:T(8,128)} %bitcast.14, s32[64,128]{1,0:T(8,128)} %bitcast.15, ...), custom_call_target="tpu_custom_call" | custom-call | flops 268435456 | bytes 1048576 | tf_op jit(solution)/shard_map/pallas_call | solution.py:733
  3.1 3.0 %collective-permute-start = (f32[192,512]{1,0:T(8,128)}, f32[192,512]{1,0:T(8,128)S(1)}, u32[]{:S(2)}, u32[]{:S(2)}) collective-permute-start(f32[192,512]{1,0:T(8,128)} %get-tuple-element.20), channel_id=1, source_target_pairs={{0,1},{1,0},{2,3},{3,2},{4,5},{5,4},{6,7},{7,6},{8,9},{9,8},{10,11... | collective-permute-start | bytes 1179656 | tf_op jit(solution)/shard_map/ppermute | solution.py:746
  6.1 4.6 %all-to-all-start = ((f32[32,3,4,128]{3,2,1,0:T(4,128)}), f32[32,3,4,128]{3,2,1,0:T(4,128)S(1)}, u32[]{:S(2)}, u32[]{:S(2)}) async-start(f32[32,3,4,128]{3,2,1,0:T(4,128)} %bitcast.13), calls=%async_computation | async-start | bytes 393216 | tf_op jit(solution)/shard_map/all_to_all | solution.py:748
  10.7 5.5 %collective-permute-start.1 = (f32[104,512]{1,0:T(8,128)}, f32[104,512]{1,0:T(8,128)S(1)}, u32[]{:S(2)}, u32[]{:S(2)}) collective-permute-start(f32[104,512]{1,0:T(8,128)} %get-tuple-element.24), channel_id=1, source_target_pairs={{0,17}} | collective-permute-start | bytes 638984 | tf_op jit(solution)/shard_map/ppermute | solution.py:749
  16.2 0.7 %collective-permute-start.2 = (f32[104,512]{1,0:T(8,128)}, f32[104,512]{1,0:T(8,128)S(1)}, u32[]{:S(2)}, u32[]{:S(2)}) collective-permute-start(f32[104,512]{1,0:T(8,128)} %get-tuple-element.25), channel_id=1, source_target_pairs={{1,17}} | collective-permute-start | bytes 638984 | tf_op jit(solution)/shard_map/ppermute | solution.py:750
  16.9 0.0 copy-start
  16.9 1.1 %copy-done = bf16[6,4,32,512]{3,2,1,0:T(8,128)(2,1)S(1)} copy-done((bf16[6,4,32,512]{3,2,1,0:T(8,128)(2,1)S(1)}, bf16[6,4,32,512]{3,2,1,0:T(8,128)(2,1)}, u32[]{:S(2)}) %copy-start) | copy-done | bytes 786456
  18.0 1.1 %copy-done.1 = bf16[640,512]{1,0:T(8,128)(2,1)S(1)} copy-done((bf16[640,512]{1,0:T(8,128)(2,1)S(1)}, bf16[640,512]{1,0:T(8,128)(2,1)}, u32[]{:S(2)}) %copy-start.1) | copy-done | bytes 655384
  19.1 0.2 shard_map.123
  19.3 1.0 %all-to-all-done = f32[32,3,4,128]{3,2,1,0:T(4,128)S(1)} async-done(((f32[32,3,4,128]{3,2,1,0:T(4,128)}), f32[32,3,4,128]{3,2,1,0:T(4,128)S(1)}, u32[]{:S(2)}, u32[]{:S(2)}) %all-to-all-start) | async-done | bytes 196640 | tf_op jit(solution)/shard_map/all_to_all | solution.py:748
  20.4 0.0 collective-permute-done.swapped
  20.4 0.7 %shard_map.124 = (f32[6,128,512]{2,1,0:T(8,128)S(1)}, f32[6,32,512]{2,1,0:T(8,128)S(1)}) custom-call(f32[384,128]{1,0:T(8,128)S(1)} %bitcast.10, bf16[640,512]{1,0:T(8,128)(2,1)S(1)} %get-tuple-element.19.table, f32[192,512]{1,0:T(8,128)S(1)} %collective-permute-done.swapped), custom_call_target="tpu_custom_call" | custom-call | flops 536870912 | bytes 1048576 | tf_op jit(solution)/shard_map/pallas_call | solution.py:762
  21.0 0.0 collective-permute-done.2.upper
  21.1 0.0 copy-start.10
  21.1 0.0 copy-start.2
  21.1 0.0 copy-start.3
  21.1 0.0 copy-start.4
  21.1 0.0 copy-start.5
  21.1 0.0 copy-start.6
  21.1 0.0 copy-start.7
  21.2 0.0 copy-start.8
  21.2 1.8 %shard_map.125 = f32[384,128]{1,0:T(8,128)} custom-call(f32[6,128,512]{2,1,0:T(8,128)S(1)} %get-tuple-element.21.mixed, f32[6,32,512]{2,1,0:T(8,128)S(1)} %get-tuple-element.22.own_part, f32[6,32,512]{2,1,0:T(8,128)S(1)} %get-tuple-element.23.far_part, bf16[640,512]{1,0:T(8,128)(2,1)S(1)} %get-tuple-element.19.table, ...), custom_call_target="tpu_custom_call" | custom-call | flops 536870912 | bytes 1048576 | tf_op jit(solution)/shard_map/pallas_call | solution.py:766
  22.9 3.9 %all-to-all-start.1 = ((f32[32,3,4,128]{3,2,1,0:T(4,128)}), f32[32,3,4,128]{3,2,1,0:T(4,128)S(1)}, u32[]{:S(2)}, u32[]{:S(2)}) async-start(f32[32,3,4,128]{3,2,1,0:T(4,128)} %bitcast.5), calls=%async_computation.1 | async-start | bytes 393216 | tf_op jit(solution)/shard_map/all_to_all | solution.py:774
  26.9 0.3 collective-permute-start.4
  27.2 0.7 %collective-permute-start.5 = (f32[96,128]{1,0:T(8,128)S(1)}, f32[96,128]{1,0:T(8,128)S(1)}, u32[]{:S(2)}, u32[]{:S(2)}) collective-permute-start(f32[96,128]{1,0:T(8,128)S(1)} %copy-done.9), channel_id=1, source_target_pairs={{2,4},{4,2},{6,8},{8,6},{10,12},{12,10},{14,16},{16,14},{18,20},{2... | collective-permute-start | bytes 147464 | tf_op jit(solution)/shard_map/ppermute | solution.py:755
  27.9 1.7 %collective-permute-start.3 = (f32[8,192]{1,0:T(8,128)S(1)}, f32[8,192]{1,0:T(8,128)S(1)}, u32[]{:S(2)}, u32[]{:S(2)}) collective-permute-start(f32[8,192]{1,0:T(8,128)S(1)} %copy-done.11), channel_id=1, source_target_pairs={{0,1},{1,0},{2,3},{3,2},{4,5},{5,4},{6,7},{7,6},{8,9},{9,8},{10,11... | collective-permute-start | bytes 18440 | tf_op jit(solution)/shard_map/ppermute | solution.py:751
  29.6 2.0 %collective-permute-done.3.side = f32[8,192]{1,0:T(8,128)S(1)} collective-permute-done((f32[8,192]{1,0:T(8,128)S(1)}, f32[8,192]{1,0:T(8,128)S(1)}, u32[]{:S(2)}, u32[]{:S(2)}) %collective-permute-start.3) | collective-permute-done | bytes 6176 | tf_op jit(solution)/shard_map/ppermute | solution.py:751
  31.6 0.0 collective-permute-done.4.near
  31.6 0.0 collective-permute-done.5.next_
  31.7 0.8 %shard_map.126 = (f32[192,128]{1,0:T(8,128)S(1)}, f32[64,128]{1,0:T(8,128)S(1)}) custom-call(f32[192,128]{1,0:T(8,128)S(1)} %copy-done.4, f32[8,192]{1,0:T(8,128)S(1)} %collective-permute-done.3.side, f32[96,128]{1,0:T(8,128)S(1)} %collective-permute-done.4.near, f32[96,128]{1,0:T(8,128)S(1)} %collective-permute-done.5.next_, s32[64,128]{1,0:T(8,128)S(1)} %bitcast.12, ...), custom_call_target="tpu_custom_call" | custom-call | flops 4194304 | bytes 1048576 | tf_op jit(solution)/shard_map/pallas_call | solution.py:775
  32.5 4.0 %all-to-all-done.1 = f32[32,3,4,128]{3,2,1,0:T(4,128)S(1)} async-done(((f32[32,3,4,128]{3,2,1,0:T(4,128)}), f32[32,3,4,128]{3,2,1,0:T(4,128)S(1)}, u32[]{:S(2)}, u32[]{:S(2)}) %all-to-all-start.1) | async-done | bytes 196640 | tf_op jit(solution)/shard_map/all_to_all | solution.py:774
  36.5 1.0 %shard_map.127 = (f32[192,128]{1,0:T(8,128)}, f32[192,128]{1,0:T(8,128)}) custom-call(f32[384,128]{1,0:T(8,128)S(1)} %bitcast.9, bf16[384,384]{1,0:T(8,128)(2,1)S(1)} %copy-done.2, f32[192,128]{1,0:T(8,128)S(1)} %get-tuple-element.30.base, f32[192,128]{1,0:T(8,128)S(1)} %copy-done.4, f32[64,128]{1,0:T(8,128)S(1)} %get-tuple-element.31.damping), custom_call_target="tpu_custom_call" | custom-call | flops 268435456 | bytes 1048576 | tf_op jit(solution)/shard_map/pallas_call | solution.py:780
  (14 shorter events, 0.0 us)
Async XLA Ops:
  3.1 17.3 %collective-permute-start = (f32[192,512]{1,0:T(8,128)}, f32[192,512]{1,0:T(8,128)S(1)}, u32[]{:S(2)}, u32[]{:S(2)}) collective-permute-start(f32[192,512]{1,0:T(8,128)} %get-tuple-element.20), channel_id=1, source_target_pairs={{0,1},{1,0},{2,3},{3,2},{4,5},{5,4},{6,7},{7,6},{8,9},{9,8},{10,11... | collective-permute-start | bytes 1179656 | tf_op jit(solution)/shard_map/ppermute | solution.py:746
  6.1 14.3 %all-to-all-start = ((f32[32,3,4,128]{3,2,1,0:T(4,128)}), f32[32,3,4,128]{3,2,1,0:T(4,128)S(1)}, u32[]{:S(2)}, u32[]{:S(2)}) async-start(f32[32,3,4,128]{3,2,1,0:T(4,128)} %bitcast.13), calls=%async_computation | async-start | bytes 393216 | tf_op jit(solution)/shard_map/all_to_all | solution.py:748
  10.7 10.3 %collective-permute-start.1 = (f32[104,512]{1,0:T(8,128)}, f32[104,512]{1,0:T(8,128)S(1)}, u32[]{:S(2)}, u32[]{:S(2)}) collective-permute-start(f32[104,512]{1,0:T(8,128)} %get-tuple-element.24), channel_id=1, source_target_pairs={{0,17}} | collective-permute-start | bytes 638984 | tf_op jit(solution)/shard_map/ppermute | solution.py:749
  16.2 4.8 %collective-permute-start.2 = (f32[104,512]{1,0:T(8,128)}, f32[104,512]{1,0:T(8,128)S(1)}, u32[]{:S(2)}, u32[]{:S(2)}) collective-permute-start(f32[104,512]{1,0:T(8,128)} %get-tuple-element.25), channel_id=1, source_target_pairs={{1,17}} | collective-permute-start | bytes 638984 | tf_op jit(solution)/shard_map/ppermute | solution.py:750
  16.9 1.1 %copy-start = (bf16[6,4,32,512]{3,2,1,0:T(8,128)(2,1)S(1)}, bf16[6,4,32,512]{3,2,1,0:T(8,128)(2,1)}, u32[]{:S(2)}) copy-start(bf16[6,4,32,512]{3,2,1,0:T(8,128)(2,1)} %tensor.3) | copy-start | bytes 2359300
  18.0 1.1 %copy-start.1 = (bf16[640,512]{1,0:T(8,128)(2,1)S(1)}, bf16[640,512]{1,0:T(8,128)(2,1)}, u32[]{:S(2)}) copy-start(bf16[640,512]{1,0:T(8,128)(2,1)} %constant.8.clone.table_at) | copy-start | bytes 1966084
  21.1 5.8 %copy-start.10 = (f32[96,128]{1,0:T(8,128)S(1)}, f32[96,128]{1,0:T(8,128)}, u32[]{:S(2)}) copy-start(f32[96,128]{1,0:T(8,128)} %get-tuple-element.28) | copy-start | bytes 147460
  21.1 6.2 %copy-start.9 = (f32[96,128]{1,0:T(8,128)S(1)}, f32[96,128]{1,0:T(8,128)}, u32[]{:S(2)}) copy-start(f32[96,128]{1,0:T(8,128)} %get-tuple-element.29) | copy-start | bytes 147460
  21.1 6.8 %copy-start.11 = (f32[8,192]{1,0:T(8,128)S(1)}, f32[8,192]{1,0:T(8,128)}, u32[]{:S(2)}) copy-start(f32[8,192]{1,0:T(8,128)} %get-tuple-element.27) | copy-start | bytes 18436
  21.1 10.6 %copy-start.2 = (bf16[384,384]{1,0:T(8,128)(2,1)S(1)}, bf16[384,384]{1,0:T(8,128)(2,1)}, u32[]{:S(2)}) copy-start(bf16[384,384]{1,0:T(8,128)(2,1)} %constant.7.clone.table) | copy-start | bytes 884740
  21.1 10.5 %copy-start.3 = (s32[32,2,128]{2,1,0:T(2,128)S(1)}, s32[32,2,128]{2,1,0:T(2,128)}, u32[]{:S(2)}) copy-start(s32[32,2,128]{2,1,0:T(2,128)} %param.13) | copy-start | bytes 98308
  21.1 10.5 %copy-start.4 = (f32[192,128]{1,0:T(8,128)S(1)}, f32[192,128]{1,0:T(8,128)}, u32[]{:S(2)}) copy-start(f32[192,128]{1,0:T(8,128)} %get-tuple-element.26.turned) | copy-start | bytes 294916
  21.1 10.5 %copy-start.5 = (f32[4]{0:T(128)S(1)}, f32[4]{0:T(128)}, u32[]{:S(2)}) copy-start(f32[4]{0:T(128)} %saturation.1) | copy-start | bytes 52
  21.1 10.5 %copy-start.6 = (f32[4]{0:T(128)S(1)}, f32[4]{0:T(128)}, u32[]{:S(2)}) copy-start(f32[4]{0:T(128)} %anisotropy.1) | copy-start | bytes 52
  21.1 10.5 %copy-start.7 = (f32[4]{0:T(128)S(1)}, f32[4]{0:T(128)}, u32[]{:S(2)}) copy-start(f32[4]{0:T(128)} %damping.1) | copy-start | bytes 52
  21.2 10.5 %copy-start.8 = (f32[3]{0:T(128)S(1)}, f32[3]{0:T(128)}, u32[]{:S(2)}) copy-start(f32[3]{0:T(128)} %applied.1) | copy-start | bytes 40
  22.9 13.6 %all-to-all-start.1 = ((f32[32,3,4,128]{3,2,1,0:T(4,128)}), f32[32,3,4,128]{3,2,1,0:T(4,128)S(1)}, u32[]{:S(2)}, u32[]{:S(2)}) async-start(f32[32,3,4,128]{3,2,1,0:T(4,128)} %bitcast.5), calls=%async_computation.1 | async-start | bytes 393216 | tf_op jit(solution)/shard_map/all_to_all | solution.py:774
  26.9 4.7 %collective-permute-start.4 = (f32[96,128]{1,0:T(8,128)S(1)}, f32[96,128]{1,0:T(8,128)S(1)}, u32[]{:S(2)}, u32[]{:S(2)}) collective-permute-start(f32[96,128]{1,0:T(8,128)S(1)} %copy-done.10), channel_id=1, source_target_pairs={{2,0},{0,2},{6,4},{4,6},{10,8},{8,10},{14,12},{12,14},{18,16},{16,... | collective-permute-start | bytes 147464 | tf_op jit(solution)/shard_map/ppermute | solution.py:753
  27.2 4.4 %collective-permute-start.5 = (f32[96,128]{1,0:T(8,128)S(1)}, f32[96,128]{1,0:T(8,128)S(1)}, u32[]{:S(2)}, u32[]{:S(2)}) collective-permute-start(f32[96,128]{1,0:T(8,128)S(1)} %copy-done.9), channel_id=1, source_target_pairs={{2,4},{4,2},{6,8},{8,6},{10,12},{12,10},{14,16},{16,14},{18,20},{2... | collective-permute-start | bytes 147464 | tf_op jit(solution)/shard_map/ppermute | solution.py:755
  27.9 3.7 %collective-permute-start.3 = (f32[8,192]{1,0:T(8,128)S(1)}, f32[8,192]{1,0:T(8,128)S(1)}, u32[]{:S(2)}, u32[]{:S(2)}) collective-permute-start(f32[8,192]{1,0:T(8,128)S(1)} %copy-done.11), channel_id=1, source_target_pairs={{0,1},{1,0},{2,3},{3,2},{4,5},{5,4},{6,7},{7,6},{8,9},{9,8},{10,11... | collective-permute-start | bytes 18440 | tf_op jit(solution)/shard_map/ppermute | solution.py:751

commit v4 on v3

--- a/solution.py
+++ b/solution.py
@@ -279,7 +279,7 @@
         self.length_z, self.length_x, self.length_y = planes * wide, rows_x * narrow, length_y
         self.cells_x, self.cells_y = width_x * wide, width_y * narrow
         self.devices = wide * narrow
-        self.special = self.narrow * (wide // 2) + 1
+        self.special, self.holder = 1, self.narrow * (wide // 2)
 
     def fits(self):
         return (
@@ -299,7 +299,7 @@
 
     def wave(self):
         w, n = np.divmod(np.arange(self.devices), self.narrow)
-        return self.planes * w + np.where(w < self.wide // 2, 1 + n, 1 - n)
+        return self.planes * w + np.where(w < self.wide // 2, 1 - n, 1 + n)
 
     def thickness_tables(self):
         wave = self.wave()
@@ -307,9 +307,10 @@
         angle = 2.0 * np.pi * ((wave[:, None] * z[None]) % self.length_z) / self.length_z
         ahead = np.stack([np.cos(angle), -np.sin(angle)], 1)
         back = np.stack([2.0 * np.cos(angle), -2.0 * np.sin(angle)], 1)
-        ahead[self.special, 1] = 1.0
-        back[self.special, 0] = np.cos(angle[self.special])
-        back[self.special, 1] = 1.0
+        middle = 1.0 - 2.0 * (z % 2)
+        ahead[self.special, 1] = middle
+        back[self.special, 0] = 1.0
+        back[self.special, 1] = middle
         back *= -1.0 / (self.length_z * self.length_x * self.length_y)
         n = np.arange(self.devices) % self.narrow
         x = np.arange(self.width_x)
@@ -359,7 +360,7 @@
 
 def rows_of(plan):
     w, n = lax.axis_index("wide"), lax.axis_index("narrow")
-    low = w < plan.wide // 2
+    low = w >= plan.wide // 2
     own = jnp.where(low, 1 + n, 1 - n)
     other = jnp.where(low, 2 - n, n)
     return w, n, own, other
@@ -382,7 +383,7 @@
         move.start()
     fetch0 = pltpu.make_async_copy(tensor.at[:, 0], held0, sems.at[7])
 
-    @pl.when(w == 0)
+    @pl.when(w == plan.wide // 2)
     def _():
         fetch0.start()
 
@@ -434,7 +435,7 @@
     side[...] = mul_back(chosen, high) + mul_back(chosen, middle) + mul_back(chosen, low)
     send(side, side_at)
 
-    @pl.when(w == 0)
+    @pl.when(w == plan.wide // 2)
     def _():
         fetch0.wait()
         cut, half = SPLIT * count, plan.cells_y
@@ -597,7 +598,7 @@
                         packed[i, high_at : high_at + step, lanes_at] = a
                         packed[i, low_at : low_at + step, lanes_at] = b
 
-    special = jnp.logical_and(w == plan.wide // 2, n == 1)
+    special = jnp.logical_and(w == 0, n == 1)
 
     @pl.when(special)
     def _():
@@ -746,8 +747,8 @@
     swapped = lax.ppermute(swap, "narrow", [(0, 1), (1, 0)])
     blocks = (plan.devices, 3, 2 * plan.width_x, lanes)
     got = lax.all_to_all(out.reshape(blocks), both, 0, 0, tiled=True).reshape(count, lanes)
-    lower = lax.ppermute(lower, both, [(0, plan.special)])
-    upper = lax.ppermute(upper, both, [(1, plan.special)])
+    lower = lax.ppermute(lower, both, [(plan.holder, plan.special)])
+    upper = lax.ppermute(upper, both, [(plan.holder + 1, plan.special)])
     side = lax.ppermute(side, "narrow", [(0, 1), (1, 0)])
     pairs = [(i ^ 1, i) for i in range(plan.wide)]
     near = lax.ppermute(near, "wide", pairs)

time: 37.9 us -> 36.8 us (0.971)
  starting transfers between devices: 20.4 us -> 14.8 us
  waiting for transfers between devices: 7.06 us -> 11.9 us
    ppermute x2, starting transfers between devices: 6.16 us -> 1.35 us  [the longest x1 0.67 us: plane_shards(): lower = lax.ppermute(lower, both, [(plan.holder, plan.special)])]
    all_to_all x1, waiting for transfers between devices: 1.02 us -> 5.83 us  [plane_shards(): lax.all_to_all(out.reshape(blocks), both, 0, 0, tiled=True)]
    all_to_all x1, starting transfers between devices: 3.94 us -> 2.84 us  [plane_shards(): lax.all_to_all(sent.reshape(blocks), both, 0, 0, tiled=True)]
where the time goes in v4:
time: 36.8 us; the launch traced here: 36.4 us
  starting transfers between devices  14.8 us (40%)
  waiting for transfers between devices  11.9 us (32%)
  Pallas kernels  6.6 us (18%)
  local copies, waits for them, and re-layouts  2.27 us (6%)
  between operations  0.86 us (2%)
    all_to_all x1, waiting for transfers between devices, plane_shards(): lax.all_to_all(out.reshape(blocks), both, 0, 0, tiled=True)  5.83 us
    all_to_all x1, starting transfers between devices, plane_shards(): lax.all_to_all(out.reshape(blocks), both, 0, 0, tiled=True)  4.92 us
    all_to_all x1, waiting for transfers between devices, plane_shards(): lax.all_to_all(sent.reshape(blocks), both, 0, 0, tiled=True)  3.99 us
    ppermute x1, starting transfers between devices, plane_shards(): swapped = lax.ppermute(swap, 'narrow', [(0, 1), (1, 0)])  3.03 us
    all_to_all x1, starting transfers between devices, plane_shards(): lax.all_to_all(sent.reshape(blocks), both, 0, 0, tiled=True)  2.84 us
    unnamed x24, local copies, waits for them, and re-layouts  2.27 us
    pallas_call x1, Pallas kernels, plane_shards(): call(partial(first_kernel, plan, species), outs, [HBM] * 6, (HBM,) * len(...  2.12 us
    ppermute x1, waiting for transfers between devices, plane_shards(): side = lax.ppermute(side, 'narrow', [(0, 1), (1, 0)])  2.03 us
  transfers between devices with their start and end apart: 8, of which 3 were waited for; matrix products, arithmetic and copies ran while one was open for 0% of the time, Pallas kernels for 5%

profile of v4, /device:TPU:0, one launch (start us, length us, event | category | flops | bytes accessed | tf_op | source)
XLA Modules:
  0.0 36.4 jit_solution(10932843728177368549)
XLA Ops:
  0.6 2.1 %shard_map.122 = (f32[384,128]{1,0:T(8,128)}, f32[96,128]{1,0:T(8,128)}, f32[96,128]{1,0:T(8,128)}, f32[192,512]{1,0:T(8,128)}, f32[104,512]{1,0:T(8,128)}, /*in...) custom-call(f32[192,128]{1,0:T(8,128)} %bitcast.14, s32[64,128]{1,0:T(8,128)} %bitcast.15, ...), custom_call_target="tpu_custom_call" | custom-call | flops 268435456 | bytes 1048576 | tf_op jit(solution)/shard_map/pallas_call | solution.py:734
  2.8 3.0 %collective-permute-start = (f32[192,512]{1,0:T(8,128)}, f32[192,512]{1,0:T(8,128)S(1)}, u32[]{:S(2)}, u32[]{:S(2)}) collective-permute-start(f32[192,512]{1,0:T(8,128)} %get-tuple-element.20), channel_id=1, source_target_pairs={{0,1},{1,0},{2,3},{3,2},{4,5},{5,4},{6,7},{7,6},{8,9},{9,8},{10,11... | collective-permute-start | bytes 1179656 | tf_op jit(solution)/shard_map/ppermute | solution.py:747
  5.8 4.9 %all-to-all-start = ((f32[32,3,4,128]{3,2,1,0:T(4,128)}), f32[32,3,4,128]{3,2,1,0:T(4,128)S(1)}, u32[]{:S(2)}, u32[]{:S(2)}) async-start(f32[32,3,4,128]{3,2,1,0:T(4,128)} %bitcast.13), calls=%async_computation | async-start | bytes 393216 | tf_op jit(solution)/shard_map/all_to_all | solution.py:749
  10.7 0.7 %collective-permute-start.1 = (f32[104,512]{1,0:T(8,128)}, f32[104,512]{1,0:T(8,128)S(1)}, u32[]{:S(2)}, u32[]{:S(2)}) collective-permute-start(f32[104,512]{1,0:T(8,128)} %get-tuple-element.24), channel_id=1, source_target_pairs={{16,1}} | collective-permute-start | bytes 638984 | tf_op jit(solution)/shard_map/ppermute | solution.py:750
  11.4 0.7 %collective-permute-start.2 = (f32[104,512]{1,0:T(8,128)}, f32[104,512]{1,0:T(8,128)S(1)}, u32[]{:S(2)}, u32[]{:S(2)}) collective-permute-start(f32[104,512]{1,0:T(8,128)} %get-tuple-element.25), channel_id=1, source_target_pairs={{17,1}} | collective-permute-start | bytes 638984 | tf_op jit(solution)/shard_map/ppermute | solution.py:751
  12.1 0.0 copy-start
  12.1 1.1 %copy-done = bf16[6,4,32,512]{3,2,1,0:T(8,128)(2,1)S(1)} copy-done((bf16[6,4,32,512]{3,2,1,0:T(8,128)(2,1)S(1)}, bf16[6,4,32,512]{3,2,1,0:T(8,128)(2,1)}, u32[]{:S(2)}) %copy-start) | copy-done | bytes 786456
  13.2 1.1 %copy-done.1 = bf16[640,512]{1,0:T(8,128)(2,1)S(1)} copy-done((bf16[640,512]{1,0:T(8,128)(2,1)S(1)}, bf16[640,512]{1,0:T(8,128)(2,1)}, u32[]{:S(2)}) %copy-start.1) | copy-done | bytes 655384
  14.3 0.2 shard_map.123
  14.5 5.8 %all-to-all-done = f32[32,3,4,128]{3,2,1,0:T(4,128)S(1)} async-done(((f32[32,3,4,128]{3,2,1,0:T(4,128)}), f32[32,3,4,128]{3,2,1,0:T(4,128)S(1)}, u32[]{:S(2)}, u32[]{:S(2)}) %all-to-all-start) | async-done | bytes 196640 | tf_op jit(solution)/shard_map/all_to_all | solution.py:749
  20.4 0.0 collective-permute-done.swapped
  20.4 0.7 %shard_map.124 = (f32[6,128,512]{2,1,0:T(8,128)S(1)}, f32[6,32,512]{2,1,0:T(8,128)S(1)}) custom-call(f32[384,128]{1,0:T(8,128)S(1)} %bitcast.10, bf16[640,512]{1,0:T(8,128)(2,1)S(1)} %get-tuple-element.19.table, f32[192,512]{1,0:T(8,128)S(1)} %collective-permute-done.swapped), custom_call_target="tpu_custom_call" | custom-call | flops 536870912 | bytes 1048576 | tf_op jit(solution)/shard_map/pallas_call | solution.py:763
  21.0 0.0 collective-permute-done.1.lower
  21.0 0.0 collective-permute-done.2.upper
  21.1 0.0 copy-start.10
  21.1 0.0 copy-start.2
  21.1 0.0 copy-start.3
  21.1 0.0 copy-start.4
  21.1 0.0 copy-start.5
  21.1 0.0 copy-start.6
  21.1 0.0 copy-start.7
  21.2 0.0 copy-start.8
  21.2 1.8 %shard_map.125 = f32[384,128]{1,0:T(8,128)} custom-call(f32[6,128,512]{2,1,0:T(8,128)S(1)} %get-tuple-element.21.mixed, f32[6,32,512]{2,1,0:T(8,128)S(1)} %get-tuple-element.22.own_part, f32[6,32,512]{2,1,0:T(8,128)S(1)} %get-tuple-element.23.far_part, bf16[640,512]{1,0:T(8,128)(2,1)S(1)} %get-tuple-element.19.table, ...), custom_call_target="tpu_custom_call" | custom-call | flops 536870912 | bytes 1048576 | tf_op jit(solution)/shard_map/pallas_call | solution.py:767
  22.9 2.8 %all-to-all-start.1 = ((f32[32,3,4,128]{3,2,1,0:T(4,128)}), f32[32,3,4,128]{3,2,1,0:T(4,128)S(1)}, u32[]{:S(2)}, u32[]{:S(2)}) async-start(f32[32,3,4,128]{3,2,1,0:T(4,128)} %bitcast.5), calls=%async_computation.1 | async-start | bytes 393216 | tf_op jit(solution)/shard_map/all_to_all | solution.py:775
  25.8 0.3 collective-permute-start.4
  26.1 0.7 %collective-permute-start.5 = (f32[96,128]{1,0:T(8,128)S(1)}, f32[96,128]{1,0:T(8,128)S(1)}, u32[]{:S(2)}, u32[]{:S(2)}) collective-permute-start(f32[96,128]{1,0:T(8,128)S(1)} %copy-done.9), channel_id=1, source_target_pairs={{2,4},{4,2},{6,8},{8,6},{10,12},{12,10},{14,16},{16,14},{18,20},{2... | collective-permute-start | bytes 147464 | tf_op jit(solution)/shard_map/ppermute | solution.py:756
  26.8 1.7 %collective-permute-start.3 = (f32[8,192]{1,0:T(8,128)S(1)}, f32[8,192]{1,0:T(8,128)S(1)}, u32[]{:S(2)}, u32[]{:S(2)}) collective-permute-start(f32[8,192]{1,0:T(8,128)S(1)} %copy-done.11), channel_id=1, source_target_pairs={{0,1},{1,0},{2,3},{3,2},{4,5},{5,4},{6,7},{7,6},{8,9},{9,8},{10,11... | collective-permute-start | bytes 18440 | tf_op jit(solution)/shard_map/ppermute | solution.py:752
  28.5 2.0 %collective-permute-done.3.side = f32[8,192]{1,0:T(8,128)S(1)} collective-permute-done((f32[8,192]{1,0:T(8,128)S(1)}, f32[8,192]{1,0:T(8,128)S(1)}, u32[]{:S(2)}, u32[]{:S(2)}) %collective-permute-start.3) | collective-permute-done | bytes 6176 | tf_op jit(solution)/shard_map/ppermute | solution.py:752
  30.5 0.0 collective-permute-done.4.near
  30.6 0.8 %shard_map.126 = (f32[192,128]{1,0:T(8,128)S(1)}, f32[64,128]{1,0:T(8,128)S(1)}) custom-call(f32[192,128]{1,0:T(8,128)S(1)} %copy-done.4, f32[8,192]{1,0:T(8,128)S(1)} %collective-permute-done.3.side, f32[96,128]{1,0:T(8,128)S(1)} %collective-permute-done.4.near, f32[96,128]{1,0:T(8,128)S(1)} %collective-permute-done.5.next_, s32[64,128]{1,0:T(8,128)S(1)} %bitcast.12, ...), custom_call_target="tpu_custom_call" | custom-call | flops 4194304 | bytes 1048576 | tf_op jit(solution)/shard_map/pallas_call | solution.py:776
  31.4 4.0 %all-to-all-done.1 = f32[32,3,4,128]{3,2,1,0:T(4,128)S(1)} async-done(((f32[32,3,4,128]{3,2,1,0:T(4,128)}), f32[32,3,4,128]{3,2,1,0:T(4,128)S(1)}, u32[]{:S(2)}, u32[]{:S(2)}) %all-to-all-start.1) | async-done | bytes 196640 | tf_op jit(solution)/shard_map/all_to_all | solution.py:775
  35.4 1.0 %shard_map.127 = (f32[192,128]{1,0:T(8,128)}, f32[192,128]{1,0:T(8,128)}) custom-call(f32[384,128]{1,0:T(8,128)S(1)} %bitcast.9, bf16[384,384]{1,0:T(8,128)(2,1)S(1)} %copy-done.2, f32[192,128]{1,0:T(8,128)S(1)} %get-tuple-element.30.base, f32[192,128]{1,0:T(8,128)S(1)} %copy-done.4, f32[64,128]{1,0:T(8,128)S(1)} %get-tuple-element.31.damping), custom_call_target="tpu_custom_call" | custom-call | flops 268435456 | bytes 1048576 | tf_op jit(solution)/shard_map/pallas_call | solution.py:781
  (14 shorter events, 0.0 us)
Async XLA Ops:
  2.8 17.6 %collective-permute-start = (f32[192,512]{1,0:T(8,128)}, f32[192,512]{1,0:T(8,128)S(1)}, u32[]{:S(2)}, u32[]{:S(2)}) collective-permute-start(f32[192,512]{1,0:T(8,128)} %get-tuple-element.20), channel_id=1, source_target_pairs={{0,1},{1,0},{2,3},{3,2},{4,5},{5,4},{6,7},{7,6},{8,9},{9,8},{10,11... | collective-permute-start | bytes 1179656 | tf_op jit(solution)/shard_map/ppermute | solution.py:747
  5.8 14.6 %all-to-all-start = ((f32[32,3,4,128]{3,2,1,0:T(4,128)}), f32[32,3,4,128]{3,2,1,0:T(4,128)S(1)}, u32[]{:S(2)}, u32[]{:S(2)}) async-start(f32[32,3,4,128]{3,2,1,0:T(4,128)} %bitcast.13), calls=%async_computation | async-start | bytes 393216 | tf_op jit(solution)/shard_map/all_to_all | solution.py:749
  10.7 10.3 %collective-permute-start.1 = (f32[104,512]{1,0:T(8,128)}, f32[104,512]{1,0:T(8,128)S(1)}, u32[]{:S(2)}, u32[]{:S(2)}) collective-permute-start(f32[104,512]{1,0:T(8,128)} %get-tuple-element.24), channel_id=1, source_target_pairs={{16,1}} | collective-permute-start | bytes 638984 | tf_op jit(solution)/shard_map/ppermute | solution.py:750
  11.4 9.6 %collective-permute-start.2 = (f32[104,512]{1,0:T(8,128)}, f32[104,512]{1,0:T(8,128)S(1)}, u32[]{:S(2)}, u32[]{:S(2)}) collective-permute-start(f32[104,512]{1,0:T(8,128)} %get-tuple-element.25), channel_id=1, source_target_pairs={{17,1}} | collective-permute-start | bytes 638984 | tf_op jit(solution)/shard_map/ppermute | solution.py:751
  12.1 1.1 %copy-start = (bf16[6,4,32,512]{3,2,1,0:T(8,128)(2,1)S(1)}, bf16[6,4,32,512]{3,2,1,0:T(8,128)(2,1)}, u32[]{:S(2)}) copy-start(bf16[6,4,32,512]{3,2,1,0:T(8,128)(2,1)} %tensor.3) | copy-start | bytes 2359300
  13.2 1.1 %copy-start.1 = (bf16[640,512]{1,0:T(8,128)(2,1)S(1)}, bf16[640,512]{1,0:T(8,128)(2,1)}, u32[]{:S(2)}) copy-start(bf16[640,512]{1,0:T(8,128)(2,1)} %constant.8.clone.table_at) | copy-start | bytes 1966084
  21.1 4.7 %copy-start.10 = (f32[96,128]{1,0:T(8,128)S(1)}, f32[96,128]{1,0:T(8,128)}, u32[]{:S(2)}) copy-start(f32[96,128]{1,0:T(8,128)} %get-tuple-element.28) | copy-start | bytes 147460
  21.1 5.1 %copy-start.9 = (f32[96,128]{1,0:T(8,128)S(1)}, f32[96,128]{1,0:T(8,128)}, u32[]{:S(2)}) copy-start(f32[96,128]{1,0:T(8,128)} %get-tuple-element.29) | copy-start | bytes 147460
  21.1 5.7 %copy-start.11 = (f32[8,192]{1,0:T(8,128)S(1)}, f32[8,192]{1,0:T(8,128)}, u32[]{:S(2)}) copy-start(f32[8,192]{1,0:T(8,128)} %get-tuple-element.27) | copy-start | bytes 18436
  21.1 9.5 %copy-start.2 = (bf16[384,384]{1,0:T(8,128)(2,1)S(1)}, bf16[384,384]{1,0:T(8,128)(2,1)}, u32[]{:S(2)}) copy-start(bf16[384,384]{1,0:T(8,128)(2,1)} %constant.7.clone.table) | copy-start | bytes 884740
  21.1 9.4 %copy-start.3 = (s32[32,2,128]{2,1,0:T(2,128)S(1)}, s32[32,2,128]{2,1,0:T(2,128)}, u32[]{:S(2)}) copy-start(s32[32,2,128]{2,1,0:T(2,128)} %param.13) | copy-start | bytes 98308
  21.1 9.4 %copy-start.4 = (f32[192,128]{1,0:T(8,128)S(1)}, f32[192,128]{1,0:T(8,128)}, u32[]{:S(2)}) copy-start(f32[192,128]{1,0:T(8,128)} %get-tuple-element.26.turned) | copy-start | bytes 294916
  21.1 9.4 %copy-start.5 = (f32[4]{0:T(128)S(1)}, f32[4]{0:T(128)}, u32[]{:S(2)}) copy-start(f32[4]{0:T(128)} %saturation.1) | copy-start | bytes 52
  21.1 9.4 %copy-start.6 = (f32[4]{0:T(128)S(1)}, f32[4]{0:T(128)}, u32[]{:S(2)}) copy-start(f32[4]{0:T(128)} %anisotropy.1) | copy-start | bytes 52
  21.1 9.4 %copy-start.7 = (f32[4]{0:T(128)S(1)}, f32[4]{0:T(128)}, u32[]{:S(2)}) copy-start(f32[4]{0:T(128)} %damping.1) | copy-start | bytes 52
  21.2 9.4 %copy-start.8 = (f32[3]{0:T(128)S(1)}, f32[3]{0:T(128)}, u32[]{:S(2)}) copy-start(f32[3]{0:T(128)} %applied.1) | copy-start | bytes 40
  22.9 12.5 %all-to-all-start.1 = ((f32[32,3,4,128]{3,2,1,0:T(4,128)}), f32[32,3,4,128]{3,2,1,0:T(4,128)S(1)}, u32[]{:S(2)}, u32[]{:S(2)}) async-start(f32[32,3,4,128]{3,2,1,0:T(4,128)} %bitcast.5), calls=%async_computation.1 | async-start | bytes 393216 | tf_op jit(solution)/shard_map/all_to_all | solution.py:775
  25.8 4.7 %collective-permute-start.4 = (f32[96,128]{1,0:T(8,128)S(1)}, f32[96,128]{1,0:T(8,128)S(1)}, u32[]{:S(2)}, u32[]{:S(2)}) collective-permute-start(f32[96,128]{1,0:T(8,128)S(1)} %copy-done.10), channel_id=1, source_target_pairs={{2,0},{0,2},{6,4},{4,6},{10,8},{8,10},{14,12},{12,14},{18,16},{16,... | collective-permute-start | bytes 147464 | tf_op jit(solution)/shard_map/ppermute | solution.py:754
  26.1 4.4 %collective-permute-start.5 = (f32[96,128]{1,0:T(8,128)S(1)}, f32[96,128]{1,0:T(8,128)S(1)}, u32[]{:S(2)}, u32[]{:S(2)}) collective-permute-start(f32[96,128]{1,0:T(8,128)S(1)} %copy-done.9), channel_id=1, source_target_pairs={{2,4},{4,2},{6,8},{8,6},{10,12},{12,10},{14,16},{16,14},{18,20},{2... | collective-permute-start | bytes 147464 | tf_op jit(solution)/shard_map/ppermute | solution.py:756
  26.8 3.7 %collective-permute-start.3 = (f32[8,192]{1,0:T(8,128)S(1)}, f32[8,192]{1,0:T(8,128)S(1)}, u32[]{:S(2)}, u32[]{:S(2)}) collective-permute-start(f32[8,192]{1,0:T(8,128)S(1)} %copy-done.11), channel_id=1, source_target_pairs={{0,1},{1,0},{2,3},{3,2},{4,5},{5,4},{6,7},{7,6},{8,9},{9,8},{10,11... | collective-permute-start | bytes 18440 | tf_op jit(solution)/shard_map/ppermute | solution.py:752

commit v5 on v4

--- a/solution.py
+++ b/solution.py
@@ -293,6 +293,7 @@
             and self.width_x == 2
             and self.width_y % 128 == 0
             and self.rows_x % 16 == 0
+            and 6 * self.cells_x <= self.cells_y
             and (self.layers * self.width_x) % 8 == 0
             and 6 * self.rows_x == 3 * self.layers * self.width_x
         )
@@ -333,7 +334,7 @@
         kx = np.arange(self.length_x)
         angle = 2.0 * np.pi * ((kx[:, None] * x[None]) % self.length_x) / self.length_x
         cosine, sine = np.cos(angle), np.sin(angle)
-        ahead_x = np.concatenate([cosine, sine], 0)
+        ahead_x = np.block([[cosine, sine], [-sine, cosine]])
         back_x = np.block([[cosine.T, -sine.T], [sine.T, cosine.T]])
         return ahead_y, ahead_x, back_x
 
@@ -506,6 +507,7 @@
 
 
 def ahead_kernel(plan, got, table, swapped, mixed, far_part):
+    w, n, _, _ = rows_of(plan)
     half, wide = plan.cells_y, plan.wide
     cells_x, length_x, narrow = plan.cells_x, plan.length_x, plan.narrow
     block = 6 * plan.width_x
@@ -518,7 +520,7 @@
     lines = jnp.concatenate(lines, 0)
     high, low = halves(lines)
     y_high, y_low = table[:half, :], table[half : 2 * half, :]
-    x_ahead = table[2 * half : 2 * half + 2 * length_x, : 3 * cells_x]
+    x_ahead = table[2 * half : 2 * half + 2 * length_x, : 6 * cells_x]
     waves = mul(high, y_high) + (mul(low, y_high) + mul(high, y_low))
     flip = flip_of(half)
     count = plan.rows_x
@@ -527,9 +529,30 @@
         rows = slice(t * count, (t + 1) * count)
         far_part[t, :, :half] = swapped[rows, :half]
         far_part[t, :, half:] = turned_far[rows, :]
-    for g in range(6):
-        a, b = halves(waves[g * cells_x : (g + 1) * cells_x, :])
+    edge = lax.broadcasted_iota(jnp.int32, (cells_x, half), 1) == 0
+    parts = [(waves[g * cells_x : (g + 1) * cells_x, :half], waves[g * cells_x : (g + 1) * cells_x, half:])
+             for g in range(6)]
+
+    def stage(g, real, imag):
+        (pr, qr), (pi, qi) = real, imag
+        plus = jnp.where(edge, pr, pr + qi), jnp.where(edge, pi, pi - qr)
+        minus = jnp.where(edge, qr, pr - qi), jnp.where(edge, qi, pi + qr)
+        stack = jnp.concatenate([jnp.concatenate([p, m], 1) for p, m in zip(plus, minus)], 0)
+        a, b = halves(stack)
         mixed[g] = mul(x_ahead, jnp.concatenate([a, b, a], 0))
+
+    special = jnp.logical_and(w == 0, n == 1)
+
+    @pl.when(special)
+    def _():
+        none = jnp.zeros((cells_x, half), jnp.float32)
+        for g in range(6):
+            stage(g, parts[g], (none, none))
+
+    @pl.when(jnp.logical_not(special))
+    def _():
+        for c in range(3):
+            stage(c, parts[2 * c], parts[2 * c + 1])
 
 
 def back_kernel(plan, mixed, own_part, far_part, table, lower, upper, out, packed, second):
@@ -551,22 +574,12 @@
                 cr, sr = slice(row, row + step), slice(length_x + row, length_x + row + step)
                 part = own_part if row < plan.rows_x else far_part
                 at = slice(row % plan.rows_x, row % plan.rows_x + step)
-                fields = []
-                for g in range(6):
-                    cp, sp = mixed[g, cr, left], mixed[g, sr, left]
-                    cq, sq = mixed[g, cr, right], mixed[g, sr, right]
-                    if lane == 0:
-                        edge = lax.broadcasted_iota(jnp.int32, cp.shape, 1) == 0
-                        cq0, sq0 = jnp.where(edge, 0.0, cq), jnp.where(edge, 0.0, sq)
-                        fields.append((cp - sq0, -(sp + cq0),
-                                       jnp.where(edge, cq, cp + sq), jnp.where(edge, -sq, cq - sp)))
-                    else:
-                        fields.append((cp - sq, -(sp + cq), cp + sq, cq - sp))
-                if not paired:
-                    fields = [
-                        (a[0] - b[1], a[1] + b[0], a[2] - b[3], a[3] + b[2])
-                        for a, b in zip(fields[0::2], fields[1::2])
-                    ]
+                if lane == 0:
+                    edge = lax.broadcasted_iota(jnp.int32, (step, 128), 1) == 0
+                fields = [
+                    (mixed[g, cr, left], mixed[g, sr, left], mixed[g, cr, right], mixed[g, sr, right])
+                    for g in range(6 if paired else 3)
+                ]
                 for i in range(3):
                     sums = []
                     for s, lanes_at in ((0, left), (2, right)):
@@ -726,7 +739,7 @@
     outs = tuple(shape(o, f32) for o in outs)
     half = plan.cells_y
     small = np.zeros((2 * length_x, 2 * half), ax[0].dtype)
-    small[:, : 3 * plan.cells_x] = x_ahead
+    small[:, : 6 * plan.cells_x] = x_ahead
     small[: 2 * plan.cells_x, half : half + 4 * length_x] = xb_pair
     small[2 * plan.cells_x : 4 * plan.cells_x, half : half + 2 * length_x] = bx[1]
     table = jnp.asarray(np.concatenate([ay[0], ay[1], small], 0))

time: 36.8 us -> 36.6 us (level)
  no operation moved by 1% of the time
where the time goes in v5:
time: 36.6 us; the launch traced here: 36.3 us
  starting transfers between devices  14.8 us (40%)
  waiting for transfers between devices  11.9 us (33%)
  Pallas kernels  6.44 us (18%)
  local copies, waits for them, and re-layouts  2.27 us (6%)
  between operations  0.87 us (2%)
    all_to_all x1, waiting for transfers between devices, plane_shards(): lax.all_to_all(out.reshape(blocks), both, 0, 0, tiled=True)  5.83 us
    all_to_all x1, starting transfers between devices, plane_shards(): lax.all_to_all(out.reshape(blocks), both, 0, 0, tiled=True)  4.92 us
    all_to_all x1, waiting for transfers between devices, plane_shards(): lax.all_to_all(sent.reshape(blocks), both, 0, 0, tiled=True)  3.99 us
    ppermute x1, starting transfers between devices, plane_shards(): swapped = lax.ppermute(swap, 'narrow', [(0, 1), (1, 0)])  3.03 us
    all_to_all x1, starting transfers between devices, plane_shards(): lax.all_to_all(sent.reshape(blocks), both, 0, 0, tiled=True)  2.84 us
    unnamed x24, local copies, waits for them, and re-layouts  2.27 us
    pallas_call x1, Pallas kernels, plane_shards(): call(partial(first_kernel, plan, species), outs, [HBM] * 6, (HBM,) * len(...  2.12 us
    ppermute x1, waiting for transfers between devices, plane_shards(): side = lax.ppermute(side, 'narrow', [(0, 1), (1, 0)])  2.03 us
  transfers between devices with their start and end apart: 8, of which 3 were waited for; matrix products, arithmetic and copies ran while one was open for 0% of the time, Pallas kernels for 5%

profile of v5, /device:TPU:0, one launch (start us, length us, event | category | flops | bytes accessed | tf_op | source)
XLA Modules:
  0.0 36.3 jit_solution(8935524804425065311)
XLA Ops:
  0.6 2.1 %shard_map.122 = (f32[384,128]{1,0:T(8,128)}, f32[96,128]{1,0:T(8,128)}, f32[96,128]{1,0:T(8,128)}, f32[192,512]{1,0:T(8,128)}, f32[104,512]{1,0:T(8,128)}, /*in...) custom-call(f32[192,128]{1,0:T(8,128)} %bitcast.14, s32[64,128]{1,0:T(8,128)} %bitcast.15, ...), custom_call_target="tpu_custom_call" | custom-call | flops 268435456 | bytes 1048576 | tf_op jit(solution)/shard_map/pallas_call | solution.py:747
  2.8 3.0 %collective-permute-start = (f32[192,512]{1,0:T(8,128)}, f32[192,512]{1,0:T(8,128)S(1)}, u32[]{:S(2)}, u32[]{:S(2)}) collective-permute-start(f32[192,512]{1,0:T(8,128)} %get-tuple-element.20), channel_id=1, source_target_pairs={{0,1},{1,0},{2,3},{3,2},{4,5},{5,4},{6,7},{7,6},{8,9},{9,8},{10,11... | collective-permute-start | bytes 1179656 | tf_op jit(solution)/shard_map/ppermute | solution.py:760
  5.8 4.9 %all-to-all-start = ((f32[32,3,4,128]{3,2,1,0:T(4,128)}), f32[32,3,4,128]{3,2,1,0:T(4,128)S(1)}, u32[]{:S(2)}, u32[]{:S(2)}) async-start(f32[32,3,4,128]{3,2,1,0:T(4,128)} %bitcast.13), calls=%async_computation | async-start | bytes 393216 | tf_op jit(solution)/shard_map/all_to_all | solution.py:762
  10.7 0.7 %collective-permute-start.1 = (f32[104,512]{1,0:T(8,128)}, f32[104,512]{1,0:T(8,128)S(1)}, u32[]{:S(2)}, u32[]{:S(2)}) collective-permute-start(f32[104,512]{1,0:T(8,128)} %get-tuple-element.24), channel_id=1, source_target_pairs={{16,1}} | collective-permute-start | bytes 638984 | tf_op jit(solution)/shard_map/ppermute | solution.py:763
  11.4 0.7 %collective-permute-start.2 = (f32[104,512]{1,0:T(8,128)}, f32[104,512]{1,0:T(8,128)S(1)}, u32[]{:S(2)}, u32[]{:S(2)}) collective-permute-start(f32[104,512]{1,0:T(8,128)} %get-tuple-element.25), channel_id=1, source_target_pairs={{17,1}} | collective-permute-start | bytes 638984 | tf_op jit(solution)/shard_map/ppermute | solution.py:764
  12.1 0.0 copy-start
  12.1 1.1 %copy-done = bf16[6,4,32,512]{3,2,1,0:T(8,128)(2,1)S(1)} copy-done((bf16[6,4,32,512]{3,2,1,0:T(8,128)(2,1)S(1)}, bf16[6,4,32,512]{3,2,1,0:T(8,128)(2,1)}, u32[]{:S(2)}) %copy-start) | copy-done | bytes 786456
  13.2 1.1 %copy-done.1 = bf16[640,512]{1,0:T(8,128)(2,1)S(1)} copy-done((bf16[640,512]{1,0:T(8,128)(2,1)S(1)}, bf16[640,512]{1,0:T(8,128)(2,1)}, u32[]{:S(2)}) %copy-start.1) | copy-done | bytes 655384
  14.3 0.2 shard_map.123
  14.5 5.8 %all-to-all-done = f32[32,3,4,128]{3,2,1,0:T(4,128)S(1)} async-done(((f32[32,3,4,128]{3,2,1,0:T(4,128)}), f32[32,3,4,128]{3,2,1,0:T(4,128)S(1)}, u32[]{:S(2)}, u32[]{:S(2)}) %all-to-all-start) | async-done | bytes 196640 | tf_op jit(solution)/shard_map/all_to_all | solution.py:762
  20.4 0.0 collective-permute-done.swapped
  20.4 0.6 %shard_map.124 = (f32[6,128,512]{2,1,0:T(8,128)S(1)}, f32[6,32,512]{2,1,0:T(8,128)S(1)}) custom-call(f32[384,128]{1,0:T(8,128)S(1)} %bitcast.10, bf16[640,512]{1,0:T(8,128)(2,1)S(1)} %get-tuple-element.19.table, f32[192,512]{1,0:T(8,128)S(1)} %collective-permute-done.swapped), custom_call_target="tpu_custom_call" | custom-call | flops 536870912 | bytes 1048576 | tf_op jit(solution)/shard_map/pallas_call | solution.py:776
  21.0 0.0 collective-permute-done.1.lower
  21.0 0.0 collective-permute-done.2.upper
  21.0 0.0 copy-start.10
  21.0 0.0 copy-start.2
  21.1 0.0 copy-start.3
  21.1 0.0 copy-start.4
  21.1 0.0 copy-start.5
  21.1 0.0 copy-start.6
  21.1 0.0 copy-start.7
  21.1 0.0 copy-start.8
  21.1 1.7 %shard_map.125 = f32[384,128]{1,0:T(8,128)} custom-call(f32[6,128,512]{2,1,0:T(8,128)S(1)} %get-tuple-element.21.mixed, f32[6,32,512]{2,1,0:T(8,128)S(1)} %get-tuple-element.22.own_part, f32[6,32,512]{2,1,0:T(8,128)S(1)} %get-tuple-element.23.far_part, bf16[640,512]{1,0:T(8,128)(2,1)S(1)} %get-tuple-element.19.table, ...), custom_call_target="tpu_custom_call" | custom-call | flops 536870912 | bytes 1048576 | tf_op jit(solution)/shard_map/pallas_call | solution.py:780
  22.8 2.8 %all-to-all-start.1 = ((f32[32,3,4,128]{3,2,1,0:T(4,128)}), f32[32,3,4,128]{3,2,1,0:T(4,128)S(1)}, u32[]{:S(2)}, u32[]{:S(2)}) async-start(f32[32,3,4,128]{3,2,1,0:T(4,128)} %bitcast.5), calls=%async_computation.1 | async-start | bytes 393216 | tf_op jit(solution)/shard_map/all_to_all | solution.py:788
  25.6 0.3 collective-permute-start.4
  26.0 0.7 %collective-permute-start.5 = (f32[96,128]{1,0:T(8,128)S(1)}, f32[96,128]{1,0:T(8,128)S(1)}, u32[]{:S(2)}, u32[]{:S(2)}) collective-permute-start(f32[96,128]{1,0:T(8,128)S(1)} %copy-done.9), channel_id=1, source_target_pairs={{2,4},{4,2},{6,8},{8,6},{10,12},{12,10},{14,16},{16,14},{18,20},{2... | collective-permute-start | bytes 147464 | tf_op jit(solution)/shard_map/ppermute | solution.py:769
  26.6 1.7 %collective-permute-start.3 = (f32[8,192]{1,0:T(8,128)S(1)}, f32[8,192]{1,0:T(8,128)S(1)}, u32[]{:S(2)}, u32[]{:S(2)}) collective-permute-start(f32[8,192]{1,0:T(8,128)S(1)} %copy-done.11), channel_id=1, source_target_pairs={{0,1},{1,0},{2,3},{3,2},{4,5},{5,4},{6,7},{7,6},{8,9},{9,8},{10,11... | collective-permute-start | bytes 18440 | tf_op jit(solution)/shard_map/ppermute | solution.py:765
  28.3 2.0 %collective-permute-done.3.side = f32[8,192]{1,0:T(8,128)S(1)} collective-permute-done((f32[8,192]{1,0:T(8,128)S(1)}, f32[8,192]{1,0:T(8,128)S(1)}, u32[]{:S(2)}, u32[]{:S(2)}) %collective-permute-start.3) | collective-permute-done | bytes 6176 | tf_op jit(solution)/shard_map/ppermute | solution.py:765
  30.4 0.0 collective-permute-done.4.near
  30.4 0.8 %shard_map.126 = (f32[192,128]{1,0:T(8,128)S(1)}, f32[64,128]{1,0:T(8,128)S(1)}) custom-call(f32[192,128]{1,0:T(8,128)S(1)} %copy-done.4, f32[8,192]{1,0:T(8,128)S(1)} %collective-permute-done.3.side, f32[96,128]{1,0:T(8,128)S(1)} %collective-permute-done.4.near, f32[96,128]{1,0:T(8,128)S(1)} %collective-permute-done.5.next_, s32[64,128]{1,0:T(8,128)S(1)} %bitcast.12, ...), custom_call_target="tpu_custom_call" | custom-call | flops 4194304 | bytes 1048576 | tf_op jit(solution)/shard_map/pallas_call | solution.py:789
  31.3 4.0 %all-to-all-done.1 = f32[32,3,4,128]{3,2,1,0:T(4,128)S(1)} async-done(((f32[32,3,4,128]{3,2,1,0:T(4,128)}), f32[32,3,4,128]{3,2,1,0:T(4,128)S(1)}, u32[]{:S(2)}, u32[]{:S(2)}) %all-to-all-start.1) | async-done | bytes 196640 | tf_op jit(solution)/shard_map/all_to_all | solution.py:788
  35.3 1.0 %shard_map.127 = (f32[192,128]{1,0:T(8,128)}, f32[192,128]{1,0:T(8,128)}) custom-call(f32[384,128]{1,0:T(8,128)S(1)} %bitcast.9, bf16[384,384]{1,0:T(8,128)(2,1)S(1)} %copy-done.2, f32[192,128]{1,0:T(8,128)S(1)} %get-tuple-element.30.base, f32[192,128]{1,0:T(8,128)S(1)} %copy-done.4, f32[64,128]{1,0:T(8,128)S(1)} %get-tuple-element.31.damping), custom_call_target="tpu_custom_call" | custom-call | flops 268435456 | bytes 1048576 | tf_op jit(solution)/shard_map/pallas_call | solution.py:794
  (14 shorter events, 0.0 us)
Async XLA Ops:
  2.8 17.6 %collective-permute-start = (f32[192,512]{1,0:T(8,128)}, f32[192,512]{1,0:T(8,128)S(1)}, u32[]{:S(2)}, u32[]{:S(2)}) collective-permute-start(f32[192,512]{1,0:T(8,128)} %get-tuple-element.20), channel_id=1, source_target_pairs={{0,1},{1,0},{2,3},{3,2},{4,5},{5,4},{6,7},{7,6},{8,9},{9,8},{10,11... | collective-permute-start | bytes 1179656 | tf_op jit(solution)/shard_map/ppermute | solution.py:760
  5.8 14.6 %all-to-all-start = ((f32[32,3,4,128]{3,2,1,0:T(4,128)}), f32[32,3,4,128]{3,2,1,0:T(4,128)S(1)}, u32[]{:S(2)}, u32[]{:S(2)}) async-start(f32[32,3,4,128]{3,2,1,0:T(4,128)} %bitcast.13), calls=%async_computation | async-start | bytes 393216 | tf_op jit(solution)/shard_map/all_to_all | solution.py:762
  10.7 10.3 %collective-permute-start.1 = (f32[104,512]{1,0:T(8,128)}, f32[104,512]{1,0:T(8,128)S(1)}, u32[]{:S(2)}, u32[]{:S(2)}) collective-permute-start(f32[104,512]{1,0:T(8,128)} %get-tuple-element.24), channel_id=1, source_target_pairs={{16,1}} | collective-permute-start | bytes 638984 | tf_op jit(solution)/shard_map/ppermute | solution.py:763
  11.4 9.6 %collective-permute-start.2 = (f32[104,512]{1,0:T(8,128)}, f32[104,512]{1,0:T(8,128)S(1)}, u32[]{:S(2)}, u32[]{:S(2)}) collective-permute-start(f32[104,512]{1,0:T(8,128)} %get-tuple-element.25), channel_id=1, source_target_pairs={{17,1}} | collective-permute-start | bytes 638984 | tf_op jit(solution)/shard_map/ppermute | solution.py:764
  12.1 1.1 %copy-start = (bf16[6,4,32,512]{3,2,1,0:T(8,128)(2,1)S(1)}, bf16[6,4,32,512]{3,2,1,0:T(8,128)(2,1)}, u32[]{:S(2)}) copy-start(bf16[6,4,32,512]{3,2,1,0:T(8,128)(2,1)} %tensor.3) | copy-start | bytes 2359300
  13.2 1.1 %copy-start.1 = (bf16[640,512]{1,0:T(8,128)(2,1)S(1)}, bf16[640,512]{1,0:T(8,128)(2,1)}, u32[]{:S(2)}) copy-start(bf16[640,512]{1,0:T(8,128)(2,1)} %constant.8.clone.table_at) | copy-start | bytes 1966084
  21.0 4.6 %copy-start.10 = (f32[96,128]{1,0:T(8,128)S(1)}, f32[96,128]{1,0:T(8,128)}, u32[]{:S(2)}) copy-start(f32[96,128]{1,0:T(8,128)} %get-tuple-element.28) | copy-start | bytes 147460
  21.0 4.9 %copy-start.9 = (f32[96,128]{1,0:T(8,128)S(1)}, f32[96,128]{1,0:T(8,128)}, u32[]{:S(2)}) copy-start(f32[96,128]{1,0:T(8,128)} %get-tuple-element.29) | copy-start | bytes 147460
  21.0 5.6 %copy-start.11 = (f32[8,192]{1,0:T(8,128)S(1)}, f32[8,192]{1,0:T(8,128)}, u32[]{:S(2)}) copy-start(f32[8,192]{1,0:T(8,128)} %get-tuple-element.27) | copy-start | bytes 18436
  21.0 9.3 %copy-start.2 = (bf16[384,384]{1,0:T(8,128)(2,1)S(1)}, bf16[384,384]{1,0:T(8,128)(2,1)}, u32[]{:S(2)}) copy-start(bf16[384,384]{1,0:T(8,128)(2,1)} %constant.7.clone.table) | copy-start | bytes 884740
  21.1 9.3 %copy-start.3 = (s32[32,2,128]{2,1,0:T(2,128)S(1)}, s32[32,2,128]{2,1,0:T(2,128)}, u32[]{:S(2)}) copy-start(s32[32,2,128]{2,1,0:T(2,128)} %param.13) | copy-start | bytes 98308
  21.1 9.3 %copy-start.4 = (f32[192,128]{1,0:T(8,128)S(1)}, f32[192,128]{1,0:T(8,128)}, u32[]{:S(2)}) copy-start(f32[192,128]{1,0:T(8,128)} %get-tuple-element.26.turned) | copy-start | bytes 294916
  21.1 9.3 %copy-start.5 = (f32[4]{0:T(128)S(1)}, f32[4]{0:T(128)}, u32[]{:S(2)}) copy-start(f32[4]{0:T(128)} %saturation.1) | copy-start | bytes 52
  21.1 9.3 %copy-start.6 = (f32[4]{0:T(128)S(1)}, f32[4]{0:T(128)}, u32[]{:S(2)}) copy-start(f32[4]{0:T(128)} %anisotropy.1) | copy-start | bytes 52
  21.1 9.3 %copy-start.7 = (f32[4]{0:T(128)S(1)}, f32[4]{0:T(128)}, u32[]{:S(2)}) copy-start(f32[4]{0:T(128)} %damping.1) | copy-start | bytes 52
  21.1 9.3 %copy-start.8 = (f32[3]{0:T(128)S(1)}, f32[3]{0:T(128)}, u32[]{:S(2)}) copy-start(f32[3]{0:T(128)} %applied.1) | copy-start | bytes 40
  22.8 12.5 %all-to-all-start.1 = ((f32[32,3,4,128]{3,2,1,0:T(4,128)}), f32[32,3,4,128]{3,2,1,0:T(4,128)S(1)}, u32[]{:S(2)}, u32[]{:S(2)}) async-start(f32[32,3,4,128]{3,2,1,0:T(4,128)} %bitcast.5), calls=%async_computation.1 | async-start | bytes 393216 | tf_op jit(solution)/shard_map/all_to_all | solution.py:788
  25.6 4.7 %collective-permute-start.4 = (f32[96,128]{1,0:T(8,128)S(1)}, f32[96,128]{1,0:T(8,128)S(1)}, u32[]{:S(2)}, u32[]{:S(2)}) collective-permute-start(f32[96,128]{1,0:T(8,128)S(1)} %copy-done.10), channel_id=1, source_target_pairs={{2,0},{0,2},{6,4},{4,6},{10,8},{8,10},{14,12},{12,14},{18,16},{16,... | collective-permute-start | bytes 147464 | tf_op jit(solution)/shard_map/ppermute | solution.py:767
  26.0 4.4 %collective-permute-start.5 = (f32[96,128]{1,0:T(8,128)S(1)}, f32[96,128]{1,0:T(8,128)S(1)}, u32[]{:S(2)}, u32[]{:S(2)}) collective-permute-start(f32[96,128]{1,0:T(8,128)S(1)} %copy-done.9), channel_id=1, source_target_pairs={{2,4},{4,2},{6,8},{8,6},{10,12},{12,10},{14,16},{16,14},{18,20},{2... | collective-permute-start | bytes 147464 | tf_op jit(solution)/shard_map/ppermute | solution.py:769
  26.6 3.7 %collective-permute-start.3 = (f32[8,192]{1,0:T(8,128)S(1)}, f32[8,192]{1,0:T(8,128)S(1)}, u32[]{:S(2)}, u32[]{:S(2)}) collective-permute-start(f32[8,192]{1,0:T(8,128)S(1)} %copy-done.11), channel_id=1, source_target_pairs={{0,1},{1,0},{2,3},{3,2},{4,5},{5,4},{6,7},{7,6},{8,9},{9,8},{10,11... | collective-permute-start | bytes 18440 | tf_op jit(solution)/shard_map/ppermute | solution.py:765

commit v6 on v5

--- a/solution.py
+++ b/solution.py
@@ -316,12 +316,12 @@
         n = np.arange(self.devices) % self.narrow
         x = np.arange(self.width_x)
         sign = 1.0 - 2.0 * ((n[:, None] * x[None]) % 2)
-        unit_c, unit_x = np.eye(3), np.eye(self.width_x)
+        unit_x = np.eye(self.width_x)
         ahead = np.einsum("drz,dx,xv->rxdzv", ahead, sign, unit_x)
-        back = np.einsum("drz,dx,cb,xv->bzvdcrx", back, sign, unit_c, unit_x)
+        back = np.einsum("drz,dx,xv->zvrxd", back, sign, unit_x)
         count = self.devices * 6 * self.width_x
         cells = 3 * self.layers * self.width_x
-        return ahead.reshape(count // 3, cells // 3), back.reshape(cells, count)
+        return ahead.reshape(count // 3, cells // 3), back.reshape(cells // 3, count // 3)
 
     def lateral_tables(self):
         half = self.cells_y
@@ -445,15 +445,15 @@
         lower[(6 - SPLIT) * count :, :] = jnp.zeros((8, plan.length_y), jnp.float32)
         upper[cut:, :] = jnp.zeros((8, plan.length_y), jnp.float32)
         for t in range(6):
-            plus = held0[t, :, :half].astype(jnp.float32)
-            values = jnp.concatenate([plus, minus[t * count : (t + 1) * count, :]], 1)
-            edge = values[0:1, :]
+            plus, rest = held0[t, :, :half].astype(jnp.float32), minus[t * count : (t + 1) * count, :]
             if t < SPLIT:
-                upper[t * count : (t + 1) * count, :] = values
-                lower[(6 - SPLIT) * count + t : (6 - SPLIT) * count + t + 1, :] = edge
+                here, there, at, edge = upper, lower, t * count, (6 - SPLIT) * count + t
             else:
-                lower[(t - SPLIT) * count : (t - SPLIT + 1) * count, :] = values
-                upper[cut + t : cut + t + 1, :] = edge
+                here, there, at, edge = lower, upper, (t - SPLIT) * count, cut + t
+            here[at : at + count, :half] = plus
+            here[at : at + count, half:] = rest
+            there[edge : edge + 1, :half] = plus[0:1, :]
+            there[edge : edge + 1, half:] = rest[0:1, :]
         sends = [pltpu.make_async_copy(lower, lower_at, sems.at[8]), pltpu.make_async_copy(upper, upper_at, sems.at[9])]
         for move in sends:
             move.start()
@@ -469,7 +469,7 @@
     return jnp.where((sum_of == half) | (sum_of == 0), 1.0, 0.0).astype(jnp.bfloat16)
 
 
-SPLIT = 3
+SPLIT = 4
 
 
 def unfold_zero(plan, lower, upper, second):
@@ -483,14 +483,11 @@
         here, at, there, edge = (
             (upper, t, lower, (6 - SPLIT) * count + t) if t < SPLIT else (lower, t - SPLIT, upper, SPLIT * count + t)
         )
-        straight, mirrored = (slice(0, count), slice(count, 2 * count))[:: 1 if t < SPLIT else -1]
         rows = slice(at * count, (at + 1) * count)
         plus, minus = here[rows, :half], here[rows, half:]
-        second[t, straight, :half] = plus
-        second[t, straight, half:] = minus
         crossed = jnp.concatenate([jnp.where(lane0, plus, minus), jnp.where(lane0, minus, plus)], 1)
         crossed = mul(turn, crossed.astype(jnp.bfloat16))
-        second[t, mirrored, :] = jnp.where(first, there[edge : edge + 1, :], crossed)
+        second[t] = jnp.where(first, there[edge : edge + 1, :], crossed)
 
 
 COUPLINGS = ((0, 3, 4), (3, 1, 5), (4, 5, 2))
@@ -588,7 +585,10 @@
                             t = COUPLINGS[i][j]
                             ka = part[t, at, lanes_at]
                             if paired:
-                                kb = second[t, cr, lanes_at]
+                                straight = (row < plan.rows_x) == (t < SPLIT)
+                                base_at = (t if t < SPLIT else t - SPLIT) * plan.rows_x + row % plan.rows_x
+                                source = upper if t < SPLIT else lower
+                                kb = source[base_at : base_at + step, lanes_at] if straight else second[t, at, lanes_at]
                                 a, b = fields[2 * j], fields[2 * j + 1]
                                 re = ka * a[s] - kb * b[s + 1]
                                 im = ka * a[s + 1] + kb * b[s]
@@ -678,9 +678,15 @@
 
 def last_kernel(plan, got, table, base, turned, damping, rate_at, demag_at, rate, demag, sems):
     cells = plan.layers * plan.width_x
-    t_high, t_low = table[: 3 * cells, :], table[3 * cells :, :]
-    high, low = halves(got[...])
-    demag[...] = mul(t_high, high) + (mul(t_low, high) + mul(t_high, low))
+    group, lanes, block = plan.devices, plan.width_y, 2 * plan.width_x
+    lines = jnp.concatenate([
+        jnp.concatenate([got[pl.ds(c * block + j, group, stride=3 * block), :] for c in range(3)], 1)
+        for j in range(block)
+    ], 0)
+    high, low = halves(lines)
+    result = mul(table[...], jnp.concatenate([high, low, high], 0))
+    for c in range(3):
+        demag[c * cells : (c + 1) * cells, :] = result[:, c * lanes : (c + 1) * lanes]
     moves = [pltpu.make_async_copy(demag, demag_at, sems.at[3])]
     moves[0].start()
     damp = damping[...]
@@ -732,7 +738,7 @@
 
     rows6 = 6 * plan.rows_x
     table_in = jnp.asarray(np.concatenate([az[0], az[0], az[1]], 1))
-    table_out = jnp.asarray(np.concatenate(bz, 0))
+    table_out = jnp.asarray(np.concatenate([bz[0], bz[0], bz[1]], 1))
     outs = ((count, lanes), (3 * plan.layers, lanes), (3 * plan.layers, lanes), (rows6, length_y),
             ((6 - SPLIT) * plan.rows_x + 8, length_y), (SPLIT * plan.rows_x + 8, length_y), (3 * cells, lanes),
             (8, 3 * cells))
@@ -781,7 +787,7 @@
         partial(back_kernel, plan),
         shape((count, lanes), f32),
         [VMEM] * 6, VMEM,
-        [pltpu.VMEM((3, 4 * length_x, length_y), bf16), pltpu.VMEM((6, length_x, length_y), f32)],
+        [pltpu.VMEM((3, 4 * length_x, length_y), bf16), pltpu.VMEM((6, plan.rows_x, length_y), f32)],
         1 << 29, LIMITS[2],
     )(mixed, own_part, far_part, table, lower, upper)
 

time: 36.6 us -> 36.5 us (level)
  no operation moved by 1% of the time
where the time goes in v6:
time: 36.5 us; the launch traced here: 36.2 us
  starting transfers between devices  14.8 us (41%)
  waiting for transfers between devices  11.9 us (33%)
  Pallas kernels  6.33 us (17%)
  local copies, waits for them, and re-layouts  2.27 us (6%)
  between operations  0.87 us (2%)
    all_to_all x1, waiting for transfers between devices, plane_shards(): lax.all_to_all(out.reshape(blocks), both, 0, 0, tiled=True)  5.83 us
    all_to_all x1, starting transfers between devices, plane_shards(): lax.all_to_all(out.reshape(blocks), both, 0, 0, tiled=True)  4.92 us
    all_to_all x1, waiting for transfers between devices, plane_shards(): lax.all_to_all(sent.reshape(blocks), both, 0, 0, tiled=True)  3.99 us
    ppermute x1, starting transfers between devices, plane_shards(): swapped = lax.ppermute(swap, 'narrow', [(0, 1), (1, 0)])  3.03 us
    all_to_all x1, starting transfers between devices, plane_shards(): lax.all_to_all(sent.reshape(blocks), both, 0, 0, tiled=True)  2.84 us
    unnamed x24, local copies, waits for them, and re-layouts  2.27 us
    pallas_call x1, Pallas kernels, plane_shards(): call(partial(first_kernel, plan, species), outs, [HBM] * 6, (HBM,) * len(...  2.12 us
    ppermute x1, waiting for transfers between devices, plane_shards(): side = lax.ppermute(side, 'narrow', [(0, 1), (1, 0)])  2.03 us
  transfers between devices with their start and end apart: 8, of which 3 were waited for; matrix products, arithmetic and copies ran while one was open for 0% of the time, Pallas kernels for 5%

profile of v6, /device:TPU:0, one launch (start us, length us, event | category | flops | bytes accessed | tf_op | source)
XLA Modules:
  0.0 36.2 jit_solution(7206792018430725329)
XLA Ops:
  0.6 2.1 %shard_map.122 = (f32[384,128]{1,0:T(8,128)}, f32[96,128]{1,0:T(8,128)}, f32[96,128]{1,0:T(8,128)}, f32[192,512]{1,0:T(8,128)}, f32[72,512]{1,0:T(8,128)}, /*ind...) custom-call(f32[192,128]{1,0:T(8,128)} %bitcast.14, s32[64,128]{1,0:T(8,128)} %bitcast.15, ...), custom_call_target="tpu_custom_call" | custom-call | flops 268435456 | bytes 1048576 | tf_op jit(solution)/shard_map/pallas_call | solution.py:753
  2.8 3.0 %collective-permute-start = (f32[192,512]{1,0:T(8,128)}, f32[192,512]{1,0:T(8,128)S(1)}, u32[]{:S(2)}, u32[]{:S(2)}) collective-permute-start(f32[192,512]{1,0:T(8,128)} %get-tuple-element.20), channel_id=1, source_target_pairs={{0,1},{1,0},{2,3},{3,2},{4,5},{5,4},{6,7},{7,6},{8,9},{9,8},{10,11... | collective-permute-start | bytes 1179656 | tf_op jit(solution)/shard_map/ppermute | solution.py:766
  5.8 4.9 %all-to-all-start = ((f32[32,3,4,128]{3,2,1,0:T(4,128)}), f32[32,3,4,128]{3,2,1,0:T(4,128)S(1)}, u32[]{:S(2)}, u32[]{:S(2)}) async-start(f32[32,3,4,128]{3,2,1,0:T(4,128)} %bitcast.13), calls=%async_computation | async-start | bytes 393216 | tf_op jit(solution)/shard_map/all_to_all | solution.py:768
  10.7 0.7 %collective-permute-start.2 = (f32[136,512]{1,0:T(8,128)}, f32[136,512]{1,0:T(8,128)S(1)}, u32[]{:S(2)}, u32[]{:S(2)}) collective-permute-start(f32[136,512]{1,0:T(8,128)} %get-tuple-element.25), channel_id=1, source_target_pairs={{17,1}} | collective-permute-start | bytes 835592 | tf_op jit(solution)/shard_map/ppermute | solution.py:770
  11.4 0.7 %collective-permute-start.1 = (f32[72,512]{1,0:T(8,128)}, f32[72,512]{1,0:T(8,128)S(1)}, u32[]{:S(2)}, u32[]{:S(2)}) collective-permute-start(f32[72,512]{1,0:T(8,128)} %get-tuple-element.24), channel_id=1, source_target_pairs={{16,1}} | collective-permute-start | bytes 442376 | tf_op jit(solution)/shard_map/ppermute | solution.py:769
  12.1 0.0 copy-start
  12.1 1.1 %copy-done = bf16[6,4,32,512]{3,2,1,0:T(8,128)(2,1)S(1)} copy-done((bf16[6,4,32,512]{3,2,1,0:T(8,128)(2,1)S(1)}, bf16[6,4,32,512]{3,2,1,0:T(8,128)(2,1)}, u32[]{:S(2)}) %copy-start) | copy-done | bytes 786456
  13.2 1.1 %copy-done.1 = bf16[640,512]{1,0:T(8,128)(2,1)S(1)} copy-done((bf16[640,512]{1,0:T(8,128)(2,1)S(1)}, bf16[640,512]{1,0:T(8,128)(2,1)}, u32[]{:S(2)}) %copy-start.1) | copy-done | bytes 655384
  14.3 0.2 shard_map.123
  14.5 5.8 %all-to-all-done = f32[32,3,4,128]{3,2,1,0:T(4,128)S(1)} async-done(((f32[32,3,4,128]{3,2,1,0:T(4,128)}), f32[32,3,4,128]{3,2,1,0:T(4,128)S(1)}, u32[]{:S(2)}, u32[]{:S(2)}) %all-to-all-start) | async-done | bytes 196640 | tf_op jit(solution)/shard_map/all_to_all | solution.py:768
  20.4 0.0 collective-permute-done.swapped
  20.4 0.6 %shard_map.124 = (f32[6,128,512]{2,1,0:T(8,128)S(1)}, f32[6,32,512]{2,1,0:T(8,128)S(1)}) custom-call(f32[384,128]{1,0:T(8,128)S(1)} %bitcast.10, bf16[640,512]{1,0:T(8,128)(2,1)S(1)} %get-tuple-element.19.table, f32[192,512]{1,0:T(8,128)S(1)} %collective-permute-done.swapped), custom_call_target="tpu_custom_call" | custom-call | flops 536870912 | bytes 1048576 | tf_op jit(solution)/shard_map/pallas_call | solution.py:782
  21.0 0.0 collective-permute-done.1.lower
  21.0 0.0 collective-permute-done.2.upper
  21.0 0.0 copy-start.10
  21.0 0.0 copy-start.2
  21.1 0.0 copy-start.3
  21.1 0.0 copy-start.4
  21.1 0.0 copy-start.5
  21.1 0.0 copy-start.6
  21.1 0.0 copy-start.7
  21.1 0.0 copy-start.8
  21.1 1.7 %shard_map.125 = f32[384,128]{1,0:T(8,128)} custom-call(f32[6,128,512]{2,1,0:T(8,128)S(1)} %get-tuple-element.21.mixed, f32[6,32,512]{2,1,0:T(8,128)S(1)} %get-tuple-element.22.own_part, f32[6,32,512]{2,1,0:T(8,128)S(1)} %get-tuple-element.23.far_part, bf16[640,512]{1,0:T(8,128)(2,1)S(1)} %get-tuple-element.19.table, ...), custom_call_target="tpu_custom_call" | custom-call | flops 536870912 | bytes 1048576 | tf_op jit(solution)/shard_map/pallas_call | solution.py:786
  22.8 2.8 %all-to-all-start.1 = ((f32[32,3,4,128]{3,2,1,0:T(4,128)}), f32[32,3,4,128]{3,2,1,0:T(4,128)S(1)}, u32[]{:S(2)}, u32[]{:S(2)}) async-start(f32[32,3,4,128]{3,2,1,0:T(4,128)} %bitcast.5), calls=%async_computation.1 | async-start | bytes 393216 | tf_op jit(solution)/shard_map/all_to_all | solution.py:794
  25.6 0.3 collective-permute-start.4
  26.0 0.7 %collective-permute-start.5 = (f32[96,128]{1,0:T(8,128)S(1)}, f32[96,128]{1,0:T(8,128)S(1)}, u32[]{:S(2)}, u32[]{:S(2)}) collective-permute-start(f32[96,128]{1,0:T(8,128)S(1)} %copy-done.9), channel_id=1, source_target_pairs={{2,4},{4,2},{6,8},{8,6},{10,12},{12,10},{14,16},{16,14},{18,20},{2... | collective-permute-start | bytes 147464 | tf_op jit(solution)/shard_map/ppermute | solution.py:775
  26.6 1.7 %collective-permute-start.3 = (f32[8,192]{1,0:T(8,128)S(1)}, f32[8,192]{1,0:T(8,128)S(1)}, u32[]{:S(2)}, u32[]{:S(2)}) collective-permute-start(f32[8,192]{1,0:T(8,128)S(1)} %copy-done.11), channel_id=1, source_target_pairs={{0,1},{1,0},{2,3},{3,2},{4,5},{5,4},{6,7},{7,6},{8,9},{9,8},{10,11... | collective-permute-start | bytes 18440 | tf_op jit(solution)/shard_map/ppermute | solution.py:771
  28.3 2.0 %collective-permute-done.3.side = f32[8,192]{1,0:T(8,128)S(1)} collective-permute-done((f32[8,192]{1,0:T(8,128)S(1)}, f32[8,192]{1,0:T(8,128)S(1)}, u32[]{:S(2)}, u32[]{:S(2)}) %collective-permute-start.3) | collective-permute-done | bytes 6176 | tf_op jit(solution)/shard_map/ppermute | solution.py:771
  30.4 0.0 collective-permute-done.4.near
  30.4 0.8 %shard_map.126 = (f32[192,128]{1,0:T(8,128)S(1)}, f32[64,128]{1,0:T(8,128)S(1)}) custom-call(f32[192,128]{1,0:T(8,128)S(1)} %copy-done.3, f32[8,192]{1,0:T(8,128)S(1)} %collective-permute-done.3.side, f32[96,128]{1,0:T(8,128)S(1)} %collective-permute-done.4.near, f32[96,128]{1,0:T(8,128)S(1)} %collective-permute-done.5.next_, s32[64,128]{1,0:T(8,128)S(1)} %bitcast.12, ...), custom_call_target="tpu_custom_call" | custom-call | flops 4194304 | bytes 1048576 | tf_op jit(solution)/shard_map/pallas_call | solution.py:795
  31.3 4.0 %all-to-all-done.1 = f32[32,3,4,128]{3,2,1,0:T(4,128)S(1)} async-done(((f32[32,3,4,128]{3,2,1,0:T(4,128)}), f32[32,3,4,128]{3,2,1,0:T(4,128)S(1)}, u32[]{:S(2)}, u32[]{:S(2)}) %all-to-all-start.1) | async-done | bytes 196640 | tf_op jit(solution)/shard_map/all_to_all | solution.py:794
  35.3 0.9 %shard_map.127 = (f32[192,128]{1,0:T(8,128)}, f32[192,128]{1,0:T(8,128)}) custom-call(f32[384,128]{1,0:T(8,128)S(1)} %bitcast.9, bf16[64,384]{1,0:T(8,128)(2,1)S(1)} %copy-done.4, f32[192,128]{1,0:T(8,128)S(1)} %get-tuple-element.30.base, f32[192,128]{1,0:T(8,128)S(1)} %copy-done.3, f32[64,128]{1,0:T(8,128)S(1)} %get-tuple-element.31.damping), custom_call_target="tpu_custom_call" | custom-call | flops 268435456 | bytes 1048576 | tf_op jit(solution)/shard_map/pallas_call | solution.py:800
  (14 shorter events, 0.0 us)
Async XLA Ops:
  2.8 17.6 %collective-permute-start = (f32[192,512]{1,0:T(8,128)}, f32[192,512]{1,0:T(8,128)S(1)}, u32[]{:S(2)}, u32[]{:S(2)}) collective-permute-start(f32[192,512]{1,0:T(8,128)} %get-tuple-element.20), channel_id=1, source_target_pairs={{0,1},{1,0},{2,3},{3,2},{4,5},{5,4},{6,7},{7,6},{8,9},{9,8},{10,11... | collective-permute-start | bytes 1179656 | tf_op jit(solution)/shard_map/ppermute | solution.py:766
  5.8 14.6 %all-to-all-start = ((f32[32,3,4,128]{3,2,1,0:T(4,128)}), f32[32,3,4,128]{3,2,1,0:T(4,128)S(1)}, u32[]{:S(2)}, u32[]{:S(2)}) async-start(f32[32,3,4,128]{3,2,1,0:T(4,128)} %bitcast.13), calls=%async_computation | async-start | bytes 393216 | tf_op jit(solution)/shard_map/all_to_all | solution.py:768
  10.7 10.3 %collective-permute-start.2 = (f32[136,512]{1,0:T(8,128)}, f32[136,512]{1,0:T(8,128)S(1)}, u32[]{:S(2)}, u32[]{:S(2)}) collective-permute-start(f32[136,512]{1,0:T(8,128)} %get-tuple-element.25), channel_id=1, source_target_pairs={{17,1}} | collective-permute-start | bytes 835592 | tf_op jit(solution)/shard_map/ppermute | solution.py:770
  11.4 9.6 %collective-permute-start.1 = (f32[72,512]{1,0:T(8,128)}, f32[72,512]{1,0:T(8,128)S(1)}, u32[]{:S(2)}, u32[]{:S(2)}) collective-permute-start(f32[72,512]{1,0:T(8,128)} %get-tuple-element.24), channel_id=1, source_target_pairs={{16,1}} | collective-permute-start | bytes 442376 | tf_op jit(solution)/shard_map/ppermute | solution.py:769
  12.1 1.1 %copy-start = (bf16[6,4,32,512]{3,2,1,0:T(8,128)(2,1)S(1)}, bf16[6,4,32,512]{3,2,1,0:T(8,128)(2,1)}, u32[]{:S(2)}) copy-start(bf16[6,4,32,512]{3,2,1,0:T(8,128)(2,1)} %tensor.3) | copy-start | bytes 2359300
  13.2 1.1 %copy-start.1 = (bf16[640,512]{1,0:T(8,128)(2,1)S(1)}, bf16[640,512]{1,0:T(8,128)(2,1)}, u32[]{:S(2)}) copy-start(bf16[640,512]{1,0:T(8,128)(2,1)} %constant.8.clone.table_at) | copy-start | bytes 1966084
  21.0 4.6 %copy-start.10 = (f32[96,128]{1,0:T(8,128)S(1)}, f32[96,128]{1,0:T(8,128)}, u32[]{:S(2)}) copy-start(f32[96,128]{1,0:T(8,128)} %get-tuple-element.28) | copy-start | bytes 147460
  21.0 4.9 %copy-start.9 = (f32[96,128]{1,0:T(8,128)S(1)}, f32[96,128]{1,0:T(8,128)}, u32[]{:S(2)}) copy-start(f32[96,128]{1,0:T(8,128)} %get-tuple-element.29) | copy-start | bytes 147460
  21.0 5.6 %copy-start.11 = (f32[8,192]{1,0:T(8,128)S(1)}, f32[8,192]{1,0:T(8,128)}, u32[]{:S(2)}) copy-start(f32[8,192]{1,0:T(8,128)} %get-tuple-element.27) | copy-start | bytes 18436
  21.0 9.3 %copy-start.2 = (s32[32,2,128]{2,1,0:T(2,128)S(1)}, s32[32,2,128]{2,1,0:T(2,128)}, u32[]{:S(2)}) copy-start(s32[32,2,128]{2,1,0:T(2,128)} %param.13) | copy-start | bytes 98308
  21.1 9.3 %copy-start.3 = (f32[192,128]{1,0:T(8,128)S(1)}, f32[192,128]{1,0:T(8,128)}, u32[]{:S(2)}) copy-start(f32[192,128]{1,0:T(8,128)} %get-tuple-element.26.turned) | copy-start | bytes 294916
  21.1 9.3 %copy-start.4 = (bf16[64,384]{1,0:T(8,128)(2,1)S(1)}, bf16[64,384]{1,0:T(8,128)(2,1)}, u32[]{:S(2)}) copy-start(bf16[64,384]{1,0:T(8,128)(2,1)} %constant.7.clone.table) | copy-start | bytes 147460
  21.1 9.3 %copy-start.5 = (f32[4]{0:T(128)S(1)}, f32[4]{0:T(128)}, u32[]{:S(2)}) copy-start(f32[4]{0:T(128)} %saturation.1) | copy-start | bytes 52
  21.1 9.3 %copy-start.6 = (f32[4]{0:T(128)S(1)}, f32[4]{0:T(128)}, u32[]{:S(2)}) copy-start(f32[4]{0:T(128)} %anisotropy.1) | copy-start | bytes 52
  21.1 9.3 %copy-start.7 = (f32[4]{0:T(128)S(1)}, f32[4]{0:T(128)}, u32[]{:S(2)}) copy-start(f32[4]{0:T(128)} %damping.1) | copy-start | bytes 52
  21.1 9.3 %copy-start.8 = (f32[3]{0:T(128)S(1)}, f32[3]{0:T(128)}, u32[]{:S(2)}) copy-start(f32[3]{0:T(128)} %applied.1) | copy-start | bytes 40
  22.8 12.5 %all-to-all-start.1 = ((f32[32,3,4,128]{3,2,1,0:T(4,128)}), f32[32,3,4,128]{3,2,1,0:T(4,128)S(1)}, u32[]{:S(2)}, u32[]{:S(2)}) async-start(f32[32,3,4,128]{3,2,1,0:T(4,128)} %bitcast.5), calls=%async_computation.1 | async-start | bytes 393216 | tf_op jit(solution)/shard_map/all_to_all | solution.py:794
  25.6 4.7 %collective-permute-start.4 = (f32[96,128]{1,0:T(8,128)S(1)}, f32[96,128]{1,0:T(8,128)S(1)}, u32[]{:S(2)}, u32[]{:S(2)}) collective-permute-start(f32[96,128]{1,0:T(8,128)S(1)} %copy-done.10), channel_id=1, source_target_pairs={{2,0},{0,2},{6,4},{4,6},{10,8},{8,10},{14,12},{12,14},{18,16},{16,... | collective-permute-start | bytes 147464 | tf_op jit(solution)/shard_map/ppermute | solution.py:773
  26.0 4.4 %collective-permute-start.5 = (f32[96,128]{1,0:T(8,128)S(1)}, f32[96,128]{1,0:T(8,128)S(1)}, u32[]{:S(2)}, u32[]{:S(2)}) collective-permute-start(f32[96,128]{1,0:T(8,128)S(1)} %copy-done.9), channel_id=1, source_target_pairs={{2,4},{4,2},{6,8},{8,6},{10,12},{12,10},{14,16},{16,14},{18,20},{2... | collective-permute-start | bytes 147464 | tf_op jit(solution)/shard_map/ppermute | solution.py:775
  26.6 3.7 %collective-permute-start.3 = (f32[8,192]{1,0:T(8,128)S(1)}, f32[8,192]{1,0:T(8,128)S(1)}, u32[]{:S(2)}, u32[]{:S(2)}) collective-permute-start(f32[8,192]{1,0:T(8,128)S(1)} %copy-done.11), channel_id=1, source_target_pairs={{0,1},{1,0},{2,3},{3,2},{4,5},{5,4},{6,7},{7,6},{8,9},{9,8},{10,11... | collective-permute-start | bytes 18440 | tf_op jit(solution)/shard_map/ppermute | solution.py:771

commit v7 on v6

--- a/solution.py
+++ b/solution.py
@@ -368,10 +368,10 @@
 
 
 def first_kernel(plan, species, spin_at, region_at, material_at, saturation_at, table_at, tensor,
-                 out_at, near_at, next_at, swap_at, lower_at, upper_at, turned_at, side_at,
+                 out_at, swap_at, lower_at, upper_at,
                  spin, region, material, saturation, table, held, held0,
-                 out, near, next_, swap, lower, upper, turned, side, sems, done):
-    w, n, _, other = rows_of(plan)
+                 out, swap, lower, upper, sems, done):
+    w, _, _, other = rows_of(plan)
     count = plan.rows_x
     moves = [
         pltpu.make_async_copy(source, target, sems.at[k])
@@ -403,12 +403,10 @@
     high, low = [], []
     for c in range(3):
         direction = spin[c * cells : (c + 1) * cells, :] * magnet
-        turned[c * cells : (c + 1) * cells, :] = direction
         a, b = halves(direction * sat)
         high.append(a)
         low.append(b)
     high, low = jnp.concatenate(high, 1), jnp.concatenate(low, 1)
-    send(turned, turned_at)
     moves[5].wait()
     for t in range(6):
         rows = slice(t * count, (t + 1) * count)
@@ -422,19 +420,6 @@
             out[pl.ds(c * 2 * plan.width_x + j, group, stride=6 * plan.width_x), :] = result[
                 j * group : (j + 1) * group, c * lanes : (c + 1) * lanes]
     send(out, out_at)
-    layers3 = 3 * plan.layers
-    up, down = turned[pl.ds(1, layers3, stride=2), :], turned[pl.ds(0, layers3, stride=2), :]
-    near[...] = jnp.where(w % 2 == 0, up, down)
-    next_[...] = jnp.where(w % 2 == 0, down, up)
-    send(near, near_at)
-    send(next_, next_at)
-    column = lax.broadcasted_iota(jnp.int32, (8, plan.width_y), 1)
-    chosen = jnp.where(column == jnp.where(n == 0, plan.width_y - 1, 0), 1.0, 0.0).astype(jnp.bfloat16)
-    high = turned[...].astype(jnp.bfloat16)
-    rest = turned[...] - high.astype(jnp.float32)
-    middle, low = halves(rest)
-    side[...] = mul_back(chosen, high) + mul_back(chosen, middle) + mul_back(chosen, low)
-    send(side, side_at)
 
     @pl.when(w == plan.wide // 2)
     def _():
@@ -462,6 +447,24 @@
 
     for move in sent:
         move.wait()
+
+
+def halo_kernel(plan, spin, region, turned, near, next_, side):
+    w, n = lax.axis_index("wide"), lax.axis_index("narrow")
+    cells = plan.layers * plan.width_x
+    magnet = region[...].astype(jnp.float32)
+    for c in range(3):
+        turned[c * cells : (c + 1) * cells, :] = spin[c * cells : (c + 1) * cells, :] * magnet
+    layers3 = 3 * plan.layers
+    up, down = turned[pl.ds(1, layers3, stride=2), :], turned[pl.ds(0, layers3, stride=2), :]
+    near[...] = jnp.where(w % 2 == 0, up, down)
+    next_[...] = jnp.where(w % 2 == 0, down, up)
+    column = lax.broadcasted_iota(jnp.int32, (8, plan.width_y), 1)
+    chosen = jnp.where(column == jnp.where(n == 0, plan.width_y - 1, 0), 1.0, 0.0).astype(jnp.bfloat16)
+    high = turned[...].astype(jnp.bfloat16)
+    rest = turned[...] - high.astype(jnp.float32)
+    middle, low = halves(rest)
+    side[...] = mul_back(chosen, high) + mul_back(chosen, middle) + mul_back(chosen, low)
 
 
 def flip_of(half):
@@ -739,9 +742,8 @@
     rows6 = 6 * plan.rows_x
     table_in = jnp.asarray(np.concatenate([az[0], az[0], az[1]], 1))
     table_out = jnp.asarray(np.concatenate([bz[0], bz[0], bz[1]], 1))
-    outs = ((count, lanes), (3 * plan.layers, lanes), (3 * plan.layers, lanes), (rows6, length_y),
-            ((6 - SPLIT) * plan.rows_x + 8, length_y), (SPLIT * plan.rows_x + 8, length_y), (3 * cells, lanes),
-            (8, 3 * cells))
+    outs = ((count, lanes), (rows6, length_y), ((6 - SPLIT) * plan.rows_x + 8, length_y),
+            (SPLIT * plan.rows_x + 8, length_y))
     outs = tuple(shape(o, f32) for o in outs)
     half = plan.cells_y
     small = np.zeros((2 * length_x, 2 * half), ax[0].dtype)
@@ -750,7 +752,7 @@
     small[2 * plan.cells_x : 4 * plan.cells_x, half : half + 2 * length_x] = bx[1]
     table = jnp.asarray(np.concatenate([ay[0], ay[1], small], 0))
 
-    out, near, next_, swap, lower, upper, turned, side = call(
+    out, swap, lower, upper = call(
         partial(first_kernel, plan, species),
         outs, [HBM] * 6, (HBM,) * len(outs),
         [pltpu.VMEM((3 * cells, lanes), f32), pltpu.VMEM((cells, lanes), jnp.int32),
@@ -758,7 +760,7 @@
          pltpu.VMEM(table_in.shape, bf16),
          pltpu.VMEM((6, plan.rows_x, length_y), bf16), pltpu.VMEM((6, plan.rows_x, length_y), bf16)]
         + [pltpu.VMEM(o.shape, o.dtype) for o in outs]
-        + [pltpu.SemaphoreType.DMA((10,)), pltpu.SemaphoreType.DMA((6,))],
+        + [pltpu.SemaphoreType.DMA((10,)), pltpu.SemaphoreType.DMA((2,))],
         1 << 28, LIMITS[0],
     )(spin2, region2, material2, saturation, table_in, demag_spectrum)
 
@@ -768,6 +770,12 @@
     got = lax.all_to_all(out.reshape(blocks), both, 0, 0, tiled=True).reshape(count, lanes)
     lower = lax.ppermute(lower, both, [(plan.holder, plan.special)])
     upper = lax.ppermute(upper, both, [(plan.holder + 1, plan.special)])
+    edge_shape = shape((3 * plan.layers, lanes), f32)
+    turned, near, next_, side = call(
+        partial(halo_kernel, plan),
+        (shape((3 * cells, lanes), f32), edge_shape, edge_shape, shape((8, 3 * cells), f32)),
+        [VMEM] * 2, (VMEM,) * 4, [], 1 << 22, LIMITS[1],
+    )(spin2, region2)
     side = lax.ppermute(side, "narrow", [(0, 1), (1, 0)])
     pairs = [(i ^ 1, i) for i in range(plan.wide)]
     near = lax.ppermute(near, "wide", pairs)

time: 36.5 us -> 36.4 us (level)
    unnamed x24 -> x20, local copies, waits for them, and re-layouts: 2.27 us -> 2.27 us
where the time goes in v7:
time: 36.4 us; the launch traced here: 36.1 us
  starting transfers between devices  14.8 us (41%)
  waiting for transfers between devices  11.7 us (32%)
  Pallas kernels  6.4 us (18%)
  local copies, waits for them, and re-layouts  2.27 us (6%)
  between operations  0.84 us (2%)
    all_to_all x1, waiting for transfers between devices, plane_shards(): lax.all_to_all(out.reshape(blocks), both, 0, 0, tiled=True)  5.83 us
    all_to_all x1, starting transfers between devices, plane_shards(): lax.all_to_all(out.reshape(blocks), both, 0, 0, tiled=True)  4.92 us
    all_to_all x1, waiting for transfers between devices, plane_shards(): lax.all_to_all(sent.reshape(blocks), both, 0, 0, tiled=True)  3.85 us
    ppermute x1, starting transfers between devices, plane_shards(): swapped = lax.ppermute(swap, 'narrow', [(0, 1), (1, 0)])  3.03 us
    all_to_all x1, starting transfers between devices, plane_shards(): lax.all_to_all(sent.reshape(blocks), both, 0, 0, tiled=True)  2.83 us
    unnamed x20, local copies, waits for them, and re-layouts  2.27 us
    pallas_call x1, Pallas kernels, plane_shards(): call(partial(first_kernel, plan, species), outs, [HBM] * 6, (HBM,) * len(...  2.05 us
    ppermute x1, waiting for transfers between devices, plane_shards(): side = lax.ppermute(side, 'narrow', [(0, 1), (1, 0)])  2.03 us
  transfers between devices with their start and end apart: 8, of which 3 were waited for; matrix products, arithmetic and copies ran while one was open for 0% of the time, Pallas kernels for 5%

profile of v7, /device:TPU:0, one launch (start us, length us, event | category | flops | bytes accessed | tf_op | source)
XLA Modules:
  0.0 36.1 jit_solution(4936595905621024670)
XLA Ops:
  0.6 2.0 %shard_map.122 = (f32[384,128]{1,0:T(8,128)}, f32[192,512]{1,0:T(8,128)}, f32[72,512]{1,0:T(8,128)}, f32[136,512]{1,0:T(8,128)}) custom-call(f32[192,128]{1,0:T(8,128)} %bitcast.9, s32[64,128]{1,0:T(8,128)} %bitcast.15, s32[64,128]{1,0:T(8,128)} %bitcast.13, f32[4]{0:T(128)} %saturation.1, bf16[128,192]{1,0:T(8,128)(2,1)} %constant.6.clone.table_at, ...), custom_call_target="tpu_custom_call" | custom-call | flops 268435456 | bytes 1048576 | tf_op jit(solution)/shard_map/pallas_call | solution.py:755
  2.7 3.0 %collective-permute-start = (f32[192,512]{1,0:T(8,128)}, f32[192,512]{1,0:T(8,128)S(1)}, u32[]{:S(2)}, u32[]{:S(2)}) collective-permute-start(f32[192,512]{1,0:T(8,128)} %get-tuple-element.20), channel_id=1, source_target_pairs={{0,1},{1,0},{2,3},{3,2},{4,5},{5,4},{6,7},{7,6},{8,9},{9,8},{10,11... | collective-permute-start | bytes 1179656 | tf_op jit(solution)/shard_map/ppermute | solution.py:768
  5.7 4.9 %all-to-all-start = ((f32[32,3,4,128]{3,2,1,0:T(4,128)}), f32[32,3,4,128]{3,2,1,0:T(4,128)S(1)}, u32[]{:S(2)}, u32[]{:S(2)}) async-start(f32[32,3,4,128]{3,2,1,0:T(4,128)} %bitcast.17), calls=%async_computation | async-start | bytes 393216 | tf_op jit(solution)/shard_map/all_to_all | solution.py:770
  10.6 0.7 %collective-permute-start.2 = (f32[136,512]{1,0:T(8,128)}, f32[136,512]{1,0:T(8,128)S(1)}, u32[]{:S(2)}, u32[]{:S(2)}) collective-permute-start(f32[136,512]{1,0:T(8,128)} %get-tuple-element.25), channel_id=1, source_target_pairs={{17,1}} | collective-permute-start | bytes 835592 | tf_op jit(solution)/shard_map/ppermute | solution.py:772
  11.3 0.7 %collective-permute-start.1 = (f32[72,512]{1,0:T(8,128)}, f32[72,512]{1,0:T(8,128)S(1)}, u32[]{:S(2)}, u32[]{:S(2)}) collective-permute-start(f32[72,512]{1,0:T(8,128)} %get-tuple-element.24), channel_id=1, source_target_pairs={{16,1}} | collective-permute-start | bytes 442376 | tf_op jit(solution)/shard_map/ppermute | solution.py:771
  12.0 0.0 copy-start
  12.0 1.1 %copy-done = bf16[6,4,32,512]{3,2,1,0:T(8,128)(2,1)S(1)} copy-done((bf16[6,4,32,512]{3,2,1,0:T(8,128)(2,1)S(1)}, bf16[6,4,32,512]{3,2,1,0:T(8,128)(2,1)}, u32[]{:S(2)}) %copy-start) | copy-done | bytes 786456
  13.1 1.1 %copy-done.1 = bf16[640,512]{1,0:T(8,128)(2,1)S(1)} copy-done((bf16[640,512]{1,0:T(8,128)(2,1)S(1)}, bf16[640,512]{1,0:T(8,128)(2,1)}, u32[]{:S(2)}) %copy-start.1) | copy-done | bytes 655384
  14.2 0.2 shard_map.123
  14.4 5.8 %all-to-all-done = f32[32,3,4,128]{3,2,1,0:T(4,128)S(1)} async-done(((f32[32,3,4,128]{3,2,1,0:T(4,128)}), f32[32,3,4,128]{3,2,1,0:T(4,128)S(1)}, u32[]{:S(2)}, u32[]{:S(2)}) %all-to-all-start) | async-done | bytes 196640 | tf_op jit(solution)/shard_map/all_to_all | solution.py:770
  20.3 0.0 collective-permute-done.swapped
  20.3 0.6 %shard_map.124 = (f32[6,128,512]{2,1,0:T(8,128)S(1)}, f32[6,32,512]{2,1,0:T(8,128)S(1)}) custom-call(f32[384,128]{1,0:T(8,128)S(1)} %bitcast.12, bf16[640,512]{1,0:T(8,128)(2,1)S(1)} %get-tuple-element.19.table, f32[192,512]{1,0:T(8,128)S(1)} %collective-permute-done.swapped), custom_call_target="tpu_custom_call" | custom-call | flops 536870912 | bytes 1048576 | tf_op jit(solution)/shard_map/pallas_call | solution.py:790
  20.9 0.0 collective-permute-done.1.lower
  20.9 0.0 collective-permute-done.2.upper
  20.9 0.0 copy-start.2
  21.0 0.0 copy-start.4
  21.0 0.0 copy-start.3
  21.0 0.0 copy-start.5
  21.0 0.0 copy-start.6
  21.0 0.0 copy-start.7
  21.0 0.0 copy-start.8
  21.0 0.0 copy-start.9
  21.0 1.7 %shard_map.125 = f32[384,128]{1,0:T(8,128)} custom-call(f32[6,128,512]{2,1,0:T(8,128)S(1)} %get-tuple-element.21.mixed, f32[6,32,512]{2,1,0:T(8,128)S(1)} %get-tuple-element.22.own_part, f32[6,32,512]{2,1,0:T(8,128)S(1)} %get-tuple-element.23.far_part, bf16[640,512]{1,0:T(8,128)(2,1)S(1)} %get-tuple-element.19.table, ...), custom_call_target="tpu_custom_call" | custom-call | flops 536870912 | bytes 1048576 | tf_op jit(solution)/shard_map/pallas_call | solution.py:794
  22.7 2.8 %all-to-all-start.1 = ((f32[32,3,4,128]{3,2,1,0:T(4,128)}), f32[32,3,4,128]{3,2,1,0:T(4,128)S(1)}, u32[]{:S(2)}, u32[]{:S(2)}) async-start(f32[32,3,4,128]{3,2,1,0:T(4,128)} %bitcast.5), calls=%async_computation.1 | async-start | bytes 393216 | tf_op jit(solution)/shard_map/all_to_all | solution.py:802
  25.6 0.1 shard_map.126
  25.7 0.3 collective-permute-start.4
  26.0 0.7 %collective-permute-start.5 = (f32[96,128]{1,0:T(8,128)S(1)}, f32[96,128]{1,0:T(8,128)S(1)}, u32[]{:S(2)}, u32[]{:S(2)}) collective-permute-start(f32[96,128]{1,0:T(8,128)S(1)} %get-tuple-element.29), channel_id=1, source_target_pairs={{2,4},{4,2},{6,8},{8,6},{10,12},{12,10},{14,16},{16,14},{18,20},{2... | collective-permute-start | bytes 147464 | tf_op jit(solution)/shard_map/ppermute | solution.py:783
  26.7 1.7 %collective-permute-start.3 = (f32[8,192]{1,0:T(8,128)S(1)}, f32[8,192]{1,0:T(8,128)S(1)}, u32[]{:S(2)}, u32[]{:S(2)}) collective-permute-start(f32[8,192]{1,0:T(8,128)S(1)} %get-tuple-element.27), channel_id=1, source_target_pairs={{0,1},{1,0},{2,3},{3,2},{4,5},{5,4},{6,7},{7,6},{8,9},{9,8},{10,11... | collective-permute-start | bytes 18440 | tf_op jit(solution)/shard_map/ppermute | solution.py:779
  28.4 2.0 %collective-permute-done.3.side = f32[8,192]{1,0:T(8,128)S(1)} collective-permute-done((f32[8,192]{1,0:T(8,128)S(1)}, f32[8,192]{1,0:T(8,128)S(1)}, u32[]{:S(2)}, u32[]{:S(2)}) %collective-permute-start.3) | collective-permute-done | bytes 6176 | tf_op jit(solution)/shard_map/ppermute | solution.py:779
  30.5 0.8 %shard_map.127 = (f32[192,128]{1,0:T(8,128)S(1)}, f32[64,128]{1,0:T(8,128)S(1)}) custom-call(f32[192,128]{1,0:T(8,128)S(1)} %get-tuple-element.26.turned, f32[8,192]{1,0:T(8,128)S(1)} %collective-permute-done.3.side, f32[96,128]{1,0:T(8,128)S(1)} %collective-permute-done.4.near, f32[96,128]{1,0:T(8,128)S(1)} %collective-permute-done.5.next_, ...), custom_call_target="tpu_custom_call" | custom-call | flops 4194304 | bytes 1048576 | tf_op jit(solution)/shard_map/pallas_call | solution.py:803
  31.3 3.9 %all-to-all-done.1 = f32[32,3,4,128]{3,2,1,0:T(4,128)S(1)} async-done(((f32[32,3,4,128]{3,2,1,0:T(4,128)}), f32[32,3,4,128]{3,2,1,0:T(4,128)S(1)}, u32[]{:S(2)}, u32[]{:S(2)}) %all-to-all-start.1) | async-done | bytes 196640 | tf_op jit(solution)/shard_map/all_to_all | solution.py:802
  35.2 0.9 %shard_map.128 = (f32[192,128]{1,0:T(8,128)}, f32[192,128]{1,0:T(8,128)}) custom-call(f32[384,128]{1,0:T(8,128)S(1)} %bitcast.11, bf16[64,384]{1,0:T(8,128)(2,1)S(1)} %copy-done.5, f32[192,128]{1,0:T(8,128)S(1)} %get-tuple-element.30.base, f32[192,128]{1,0:T(8,128)S(1)} %get-tuple-element.26.turned, f32[64,128]{1,0:T(8,128)S(1)} %get-tuple-element.31.damping), custom_call_target="tpu_custom_call" | custom-call | flops 268435456 | bytes 1048576 | tf_op jit(solution)/shard_map/pallas_call | solution.py:808
  (11 shorter events, 0.0 us)
Async XLA Ops:
  2.7 17.6 %collective-permute-start = (f32[192,512]{1,0:T(8,128)}, f32[192,512]{1,0:T(8,128)S(1)}, u32[]{:S(2)}, u32[]{:S(2)}) collective-permute-start(f32[192,512]{1,0:T(8,128)} %get-tuple-element.20), channel_id=1, source_target_pairs={{0,1},{1,0},{2,3},{3,2},{4,5},{5,4},{6,7},{7,6},{8,9},{9,8},{10,11... | collective-permute-start | bytes 1179656 | tf_op jit(solution)/shard_map/ppermute | solution.py:768
  5.7 14.6 %all-to-all-start = ((f32[32,3,4,128]{3,2,1,0:T(4,128)}), f32[32,3,4,128]{3,2,1,0:T(4,128)S(1)}, u32[]{:S(2)}, u32[]{:S(2)}) async-start(f32[32,3,4,128]{3,2,1,0:T(4,128)} %bitcast.17), calls=%async_computation | async-start | bytes 393216 | tf_op jit(solution)/shard_map/all_to_all | solution.py:770
  10.6 10.3 %collective-permute-start.2 = (f32[136,512]{1,0:T(8,128)}, f32[136,512]{1,0:T(8,128)S(1)}, u32[]{:S(2)}, u32[]{:S(2)}) collective-permute-start(f32[136,512]{1,0:T(8,128)} %get-tuple-element.25), channel_id=1, source_target_pairs={{17,1}} | collective-permute-start | bytes 835592 | tf_op jit(solution)/shard_map/ppermute | solution.py:772
  11.3 9.6 %collective-permute-start.1 = (f32[72,512]{1,0:T(8,128)}, f32[72,512]{1,0:T(8,128)S(1)}, u32[]{:S(2)}, u32[]{:S(2)}) collective-permute-start(f32[72,512]{1,0:T(8,128)} %get-tuple-element.24), channel_id=1, source_target_pairs={{16,1}} | collective-permute-start | bytes 442376 | tf_op jit(solution)/shard_map/ppermute | solution.py:771
  12.0 1.1 %copy-start = (bf16[6,4,32,512]{3,2,1,0:T(8,128)(2,1)S(1)}, bf16[6,4,32,512]{3,2,1,0:T(8,128)(2,1)}, u32[]{:S(2)}) copy-start(bf16[6,4,32,512]{3,2,1,0:T(8,128)(2,1)} %tensor.3) | copy-start | bytes 2359300
  13.1 1.1 %copy-start.1 = (bf16[640,512]{1,0:T(8,128)(2,1)S(1)}, bf16[640,512]{1,0:T(8,128)(2,1)}, u32[]{:S(2)}) copy-start(bf16[640,512]{1,0:T(8,128)(2,1)} %constant.8.clone.table_at) | copy-start | bytes 1966084
  20.9 4.6 %copy-start.2 = (f32[3,32,2,128]{3,2,1,0:T(2,128)S(1)}, f32[3,32,2,128]{3,2,1,0:T(2,128)}, u32[]{:S(2)}) copy-start(f32[3,32,2,128]{3,2,1,0:T(2,128)} %param.11) | copy-start | bytes 294916
  21.0 4.6 %copy-start.4 = (s32[32,2,128]{2,1,0:T(2,128)S(1)}, s32[32,2,128]{2,1,0:T(2,128)}, u32[]{:S(2)}) copy-start(s32[32,2,128]{2,1,0:T(2,128)} %param.12) | copy-start | bytes 98308
  21.0 9.5 %copy-start.3 = (s32[32,2,128]{2,1,0:T(2,128)S(1)}, s32[32,2,128]{2,1,0:T(2,128)}, u32[]{:S(2)}) copy-start(s32[32,2,128]{2,1,0:T(2,128)} %param.13) | copy-start | bytes 98308
  21.0 9.5 %copy-start.5 = (bf16[64,384]{1,0:T(8,128)(2,1)S(1)}, bf16[64,384]{1,0:T(8,128)(2,1)}, u32[]{:S(2)}) copy-start(bf16[64,384]{1,0:T(8,128)(2,1)} %constant.7.clone.table) | copy-start | bytes 147460
  21.0 9.5 %copy-start.6 = (f32[4]{0:T(128)S(1)}, f32[4]{0:T(128)}, u32[]{:S(2)}) copy-start(f32[4]{0:T(128)} %saturation.1) | copy-start | bytes 52
  21.0 9.5 %copy-start.7 = (f32[4]{0:T(128)S(1)}, f32[4]{0:T(128)}, u32[]{:S(2)}) copy-start(f32[4]{0:T(128)} %anisotropy.1) | copy-start | bytes 52
  21.0 9.5 %copy-start.8 = (f32[4]{0:T(128)S(1)}, f32[4]{0:T(128)}, u32[]{:S(2)}) copy-start(f32[4]{0:T(128)} %damping.1) | copy-start | bytes 52
  21.0 9.5 %copy-start.9 = (f32[3]{0:T(128)S(1)}, f32[3]{0:T(128)}, u32[]{:S(2)}) copy-start(f32[3]{0:T(128)} %applied.1) | copy-start | bytes 40
  22.7 12.5 %all-to-all-start.1 = ((f32[32,3,4,128]{3,2,1,0:T(4,128)}), f32[32,3,4,128]{3,2,1,0:T(4,128)S(1)}, u32[]{:S(2)}, u32[]{:S(2)}) async-start(f32[32,3,4,128]{3,2,1,0:T(4,128)} %bitcast.5), calls=%async_computation.1 | async-start | bytes 393216 | tf_op jit(solution)/shard_map/all_to_all | solution.py:802
  25.7 4.7 %collective-permute-start.4 = (f32[96,128]{1,0:T(8,128)S(1)}, f32[96,128]{1,0:T(8,128)S(1)}, u32[]{:S(2)}, u32[]{:S(2)}) collective-permute-start(f32[96,128]{1,0:T(8,128)S(1)} %get-tuple-element.28), channel_id=1, source_target_pairs={{2,0},{0,2},{6,4},{4,6},{10,8},{8,10},{14,12},{12,14},{18,16},{16,... | collective-permute-start | bytes 147464 | tf_op jit(solution)/shard_map/ppermute | solution.py:781
  26.0 4.4 %collective-permute-start.5 = (f32[96,128]{1,0:T(8,128)S(1)}, f32[96,128]{1,0:T(8,128)S(1)}, u32[]{:S(2)}, u32[]{:S(2)}) collective-permute-start(f32[96,128]{1,0:T(8,128)S(1)} %get-tuple-element.29), channel_id=1, source_target_pairs={{2,4},{4,2},{6,8},{8,6},{10,12},{12,10},{14,16},{16,14},{18,20},{2... | collective-permute-start | bytes 147464 | tf_op jit(solution)/shard_map/ppermute | solution.py:783
  26.7 3.7 %collective-permute-start.3 = (f32[8,192]{1,0:T(8,128)S(1)}, f32[8,192]{1,0:T(8,128)S(1)}, u32[]{:S(2)}, u32[]{:S(2)}) collective-permute-start(f32[8,192]{1,0:T(8,128)S(1)} %get-tuple-element.27), channel_id=1, source_target_pairs={{0,1},{1,0},{2,3},{3,2},{4,5},{5,4},{6,7},{7,6},{8,9},{9,8},{10,11... | collective-permute-start | bytes 18440 | tf_op jit(solution)/shard_map/ppermute | solution.py:779

commit v8 on v7

--- a/solution.py
+++ b/solution.py
@@ -380,14 +380,14 @@
             (table_at, table), (tensor.at[:, other], held),
         ))
     ]
-    for move in moves:
-        move.start()
     fetch0 = pltpu.make_async_copy(tensor.at[:, 0], held0, sems.at[7])
 
     @pl.when(w == plan.wide // 2)
     def _():
         fetch0.start()
 
+    for move in moves[::-1]:
+        move.start()
     sent = []
 
     def send(source, target):
@@ -412,14 +412,7 @@
         rows = slice(t * count, (t + 1) * count)
         swap[rows, : plan.length_y] = held[t].astype(jnp.float32)
     send(swap, swap_at)
-    moves[4].wait()
-    result = mul(table[...], jnp.concatenate([high, low, high], 0))
-    group, lanes = plan.devices, plan.width_y
-    for c in range(3):
-        for j in range(2 * plan.width_x):
-            out[pl.ds(c * 2 * plan.width_x + j, group, stride=6 * plan.width_x), :] = result[
-                j * group : (j + 1) * group, c * lanes : (c + 1) * lanes]
-    send(out, out_at)
+    far = [pltpu.make_async_copy(lower, lower_at, sems.at[8]), pltpu.make_async_copy(upper, upper_at, sems.at[9])]
 
     @pl.when(w == plan.wide // 2)
     def _():
@@ -439,10 +432,21 @@
             here[at : at + count, half:] = rest
             there[edge : edge + 1, :half] = plus[0:1, :]
             there[edge : edge + 1, half:] = rest[0:1, :]
-        sends = [pltpu.make_async_copy(lower, lower_at, sems.at[8]), pltpu.make_async_copy(upper, upper_at, sems.at[9])]
-        for move in sends:
+        for move in far:
             move.start()
-        for move in sends:
+
+    moves[4].wait()
+    result = mul(table[...], jnp.concatenate([high, low, high], 0))
+    group, lanes = plan.devices, plan.width_y
+    for c in range(3):
+        for j in range(2 * plan.width_x):
+            out[pl.ds(c * 2 * plan.width_x + j, group, stride=6 * plan.width_x), :] = result[
+                j * group : (j + 1) * group, c * lanes : (c + 1) * lanes]
+    send(out, out_at)
+
+    @pl.when(w == plan.wide // 2)
+    def _():
+        for move in far:
             move.wait()
 
     for move in sent:

time: 36.4 us -> 36.4 us (level)
  no operation moved by 1% of the time
where the time goes in v8:
time: 36.4 us; the launch traced here: 36.1 us
  starting transfers between devices  14.8 us (41%)
  waiting for transfers between devices  11.7 us (32%)
  Pallas kernels  6.4 us (18%)
  local copies, waits for them, and re-layouts  2.27 us (6%)
  between operations  0.85 us (2%)
    all_to_all x1, waiting for transfers between devices, plane_shards(): lax.all_to_all(out.reshape(blocks), both, 0, 0, tiled=True)  5.83 us
    all_to_all x1, starting transfers between devices, plane_shards(): lax.all_to_all(out.reshape(blocks), both, 0, 0, tiled=True)  4.92 us
    all_to_all x1, waiting for transfers between devices, plane_shards(): lax.all_to_all(sent.reshape(blocks), both, 0, 0, tiled=True)  3.85 us
    ppermute x1, starting transfers between devices, plane_shards(): swapped = lax.ppermute(swap, 'narrow', [(0, 1), (1, 0)])  3.03 us
    all_to_all x1, starting transfers between devices, plane_shards(): lax.all_to_all(sent.reshape(blocks), both, 0, 0, tiled=True)  2.85 us
    unnamed x20, local copies, waits for them, and re-layouts  2.27 us
    pallas_call x1, Pallas kernels, plane_shards(): call(partial(first_kernel, plan, species), outs, [HBM] * 6, (HBM,) * len(...  2.06 us
    ppermute x1, waiting for transfers between devices, plane_shards(): side = lax.ppermute(side, 'narrow', [(0, 1), (1, 0)])  2.03 us
  transfers between devices with their start and end apart: 8, of which 3 were waited for; matrix products, arithmetic and copies ran while one was open for 0% of the time, Pallas kernels for 5%

profile of v8, /device:TPU:0, one launch (start us, length us, event | category | flops | bytes accessed | tf_op | source)
XLA Modules:
  0.0 36.1 jit_solution(5228560487968078701)
XLA Ops:
  0.6 2.1 %shard_map.122 = (f32[384,128]{1,0:T(8,128)}, f32[192,512]{1,0:T(8,128)}, f32[72,512]{1,0:T(8,128)}, f32[136,512]{1,0:T(8,128)}) custom-call(f32[192,128]{1,0:T(8,128)} %bitcast.9, s32[64,128]{1,0:T(8,128)} %bitcast.15, s32[64,128]{1,0:T(8,128)} %bitcast.13, f32[4]{0:T(128)} %saturation.1, bf16[128,192]{1,0:T(8,128)(2,1)} %constant.6.clone.table_at, ...), custom_call_target="tpu_custom_call" | custom-call | flops 268435456 | bytes 1048576 | tf_op jit(solution)/shard_map/pallas_call | solution.py:759
  2.7 3.0 %collective-permute-start = (f32[192,512]{1,0:T(8,128)}, f32[192,512]{1,0:T(8,128)S(1)}, u32[]{:S(2)}, u32[]{:S(2)}) collective-permute-start(f32[192,512]{1,0:T(8,128)} %get-tuple-element.20), channel_id=1, source_target_pairs={{0,1},{1,0},{2,3},{3,2},{4,5},{5,4},{6,7},{7,6},{8,9},{9,8},{10,11... | collective-permute-start | bytes 1179656 | tf_op jit(solution)/shard_map/ppermute | solution.py:772
  5.7 4.9 %all-to-all-start = ((f32[32,3,4,128]{3,2,1,0:T(4,128)}), f32[32,3,4,128]{3,2,1,0:T(4,128)S(1)}, u32[]{:S(2)}, u32[]{:S(2)}) async-start(f32[32,3,4,128]{3,2,1,0:T(4,128)} %bitcast.17), calls=%async_computation | async-start | bytes 393216 | tf_op jit(solution)/shard_map/all_to_all | solution.py:774
  10.7 0.7 %collective-permute-start.2 = (f32[136,512]{1,0:T(8,128)}, f32[136,512]{1,0:T(8,128)S(1)}, u32[]{:S(2)}, u32[]{:S(2)}) collective-permute-start(f32[136,512]{1,0:T(8,128)} %get-tuple-element.25), channel_id=1, source_target_pairs={{17,1}} | collective-permute-start | bytes 835592 | tf_op jit(solution)/shard_map/ppermute | solution.py:776
  11.3 0.7 %collective-permute-start.1 = (f32[72,512]{1,0:T(8,128)}, f32[72,512]{1,0:T(8,128)S(1)}, u32[]{:S(2)}, u32[]{:S(2)}) collective-permute-start(f32[72,512]{1,0:T(8,128)} %get-tuple-element.24), channel_id=1, source_target_pairs={{16,1}} | collective-permute-start | bytes 442376 | tf_op jit(solution)/shard_map/ppermute | solution.py:775
  12.0 0.0 copy-start
  12.0 1.1 %copy-done = bf16[6,4,32,512]{3,2,1,0:T(8,128)(2,1)S(1)} copy-done((bf16[6,4,32,512]{3,2,1,0:T(8,128)(2,1)S(1)}, bf16[6,4,32,512]{3,2,1,0:T(8,128)(2,1)}, u32[]{:S(2)}) %copy-start) | copy-done | bytes 786456
  13.2 1.1 %copy-done.1 = bf16[640,512]{1,0:T(8,128)(2,1)S(1)} copy-done((bf16[640,512]{1,0:T(8,128)(2,1)S(1)}, bf16[640,512]{1,0:T(8,128)(2,1)}, u32[]{:S(2)}) %copy-start.1) | copy-done | bytes 655384
  14.3 0.2 shard_map.123
  14.5 5.8 %all-to-all-done = f32[32,3,4,128]{3,2,1,0:T(4,128)S(1)} async-done(((f32[32,3,4,128]{3,2,1,0:T(4,128)}), f32[32,3,4,128]{3,2,1,0:T(4,128)S(1)}, u32[]{:S(2)}, u32[]{:S(2)}) %all-to-all-start) | async-done | bytes 196640 | tf_op jit(solution)/shard_map/all_to_all | solution.py:774
  20.3 0.0 collective-permute-done.swapped
  20.3 0.6 %shard_map.124 = (f32[6,128,512]{2,1,0:T(8,128)S(1)}, f32[6,32,512]{2,1,0:T(8,128)S(1)}) custom-call(f32[384,128]{1,0:T(8,128)S(1)} %bitcast.12, bf16[640,512]{1,0:T(8,128)(2,1)S(1)} %get-tuple-element.19.table, f32[192,512]{1,0:T(8,128)S(1)} %collective-permute-done.swapped), custom_call_target="tpu_custom_call" | custom-call | flops 536870912 | bytes 1048576 | tf_op jit(solution)/shard_map/pallas_call | solution.py:794
  20.9 0.0 collective-permute-done.2.upper
  21.0 0.0 copy-start.2
  21.0 0.0 copy-start.4
  21.0 0.0 copy-start.3
  21.0 0.0 copy-start.5
  21.0 0.0 copy-start.6
  21.0 0.0 copy-start.7
  21.0 0.0 copy-start.8
  21.0 0.0 copy-start.9
  21.0 1.6 %shard_map.125 = f32[384,128]{1,0:T(8,128)} custom-call(f32[6,128,512]{2,1,0:T(8,128)S(1)} %get-tuple-element.21.mixed, f32[6,32,512]{2,1,0:T(8,128)S(1)} %get-tuple-element.22.own_part, f32[6,32,512]{2,1,0:T(8,128)S(1)} %get-tuple-element.23.far_part, bf16[640,512]{1,0:T(8,128)(2,1)S(1)} %get-tuple-element.19.table, ...), custom_call_target="tpu_custom_call" | custom-call | flops 536870912 | bytes 1048576 | tf_op jit(solution)/shard_map/pallas_call | solution.py:798
  22.7 2.9 %all-to-all-start.1 = ((f32[32,3,4,128]{3,2,1,0:T(4,128)}), f32[32,3,4,128]{3,2,1,0:T(4,128)S(1)}, u32[]{:S(2)}, u32[]{:S(2)}) async-start(f32[32,3,4,128]{3,2,1,0:T(4,128)} %bitcast.5), calls=%async_computation.1 | async-start | bytes 393216 | tf_op jit(solution)/shard_map/all_to_all | solution.py:806
  25.6 0.1 shard_map.126
  25.7 0.3 collective-permute-start.4
  26.0 0.7 %collective-permute-start.5 = (f32[96,128]{1,0:T(8,128)S(1)}, f32[96,128]{1,0:T(8,128)S(1)}, u32[]{:S(2)}, u32[]{:S(2)}) collective-permute-start(f32[96,128]{1,0:T(8,128)S(1)} %get-tuple-element.29), channel_id=1, source_target_pairs={{2,4},{4,2},{6,8},{8,6},{10,12},{12,10},{14,16},{16,14},{18,20},{2... | collective-permute-start | bytes 147464 | tf_op jit(solution)/shard_map/ppermute | solution.py:787
  26.7 1.7 %collective-permute-start.3 = (f32[8,192]{1,0:T(8,128)S(1)}, f32[8,192]{1,0:T(8,128)S(1)}, u32[]{:S(2)}, u32[]{:S(2)}) collective-permute-start(f32[8,192]{1,0:T(8,128)S(1)} %get-tuple-element.27), channel_id=1, source_target_pairs={{0,1},{1,0},{2,3},{3,2},{4,5},{5,4},{6,7},{7,6},{8,9},{9,8},{10,11... | collective-permute-start | bytes 18440 | tf_op jit(solution)/shard_map/ppermute | solution.py:783
  28.4 2.0 %collective-permute-done.3.side = f32[8,192]{1,0:T(8,128)S(1)} collective-permute-done((f32[8,192]{1,0:T(8,128)S(1)}, f32[8,192]{1,0:T(8,128)S(1)}, u32[]{:S(2)}, u32[]{:S(2)}) %collective-permute-start.3) | collective-permute-done | bytes 6176 | tf_op jit(solution)/shard_map/ppermute | solution.py:783
  30.4 0.0 collective-permute-done.4.near
  30.5 0.8 %shard_map.127 = (f32[192,128]{1,0:T(8,128)S(1)}, f32[64,128]{1,0:T(8,128)S(1)}) custom-call(f32[192,128]{1,0:T(8,128)S(1)} %get-tuple-element.26.turned, f32[8,192]{1,0:T(8,128)S(1)} %collective-permute-done.3.side, f32[96,128]{1,0:T(8,128)S(1)} %collective-permute-done.4.near, f32[96,128]{1,0:T(8,128)S(1)} %collective-permute-done.5.next_, ...), custom_call_target="tpu_custom_call" | custom-call | flops 4194304 | bytes 1048576 | tf_op jit(solution)/shard_map/pallas_call | solution.py:807
  31.3 3.9 %all-to-all-done.1 = f32[32,3,4,128]{3,2,1,0:T(4,128)S(1)} async-done(((f32[32,3,4,128]{3,2,1,0:T(4,128)}), f32[32,3,4,128]{3,2,1,0:T(4,128)S(1)}, u32[]{:S(2)}, u32[]{:S(2)}) %all-to-all-start.1) | async-done | bytes 196640 | tf_op jit(solution)/shard_map/all_to_all | solution.py:806
  35.2 0.9 %shard_map.128 = (f32[192,128]{1,0:T(8,128)}, f32[192,128]{1,0:T(8,128)}) custom-call(f32[384,128]{1,0:T(8,128)S(1)} %bitcast.11, bf16[64,384]{1,0:T(8,128)(2,1)S(1)} %copy-done.5, f32[192,128]{1,0:T(8,128)S(1)} %get-tuple-element.30.base, f32[192,128]{1,0:T(8,128)S(1)} %get-tuple-element.26.turned, f32[64,128]{1,0:T(8,128)S(1)} %get-tuple-element.31.damping), custom_call_target="tpu_custom_call" | custom-call | flops 268435456 | bytes 1048576 | tf_op jit(solution)/shard_map/pallas_call | solution.py:812
  (11 shorter events, 0.0 us)
Async XLA Ops:
  2.7 17.6 %collective-permute-start = (f32[192,512]{1,0:T(8,128)}, f32[192,512]{1,0:T(8,128)S(1)}, u32[]{:S(2)}, u32[]{:S(2)}) collective-permute-start(f32[192,512]{1,0:T(8,128)} %get-tuple-element.20), channel_id=1, source_target_pairs={{0,1},{1,0},{2,3},{3,2},{4,5},{5,4},{6,7},{7,6},{8,9},{9,8},{10,11... | collective-permute-start | bytes 1179656 | tf_op jit(solution)/shard_map/ppermute | solution.py:772
  5.7 14.6 %all-to-all-start = ((f32[32,3,4,128]{3,2,1,0:T(4,128)}), f32[32,3,4,128]{3,2,1,0:T(4,128)S(1)}, u32[]{:S(2)}, u32[]{:S(2)}) async-start(f32[32,3,4,128]{3,2,1,0:T(4,128)} %bitcast.17), calls=%async_computation | async-start | bytes 393216 | tf_op jit(solution)/shard_map/all_to_all | solution.py:774
  10.7 10.3 %collective-permute-start.2 = (f32[136,512]{1,0:T(8,128)}, f32[136,512]{1,0:T(8,128)S(1)}, u32[]{:S(2)}, u32[]{:S(2)}) collective-permute-start(f32[136,512]{1,0:T(8,128)} %get-tuple-element.25), channel_id=1, source_target_pairs={{17,1}} | collective-permute-start | bytes 835592 | tf_op jit(solution)/shard_map/ppermute | solution.py:776
  11.3 9.6 %collective-permute-start.1 = (f32[72,512]{1,0:T(8,128)}, f32[72,512]{1,0:T(8,128)S(1)}, u32[]{:S(2)}, u32[]{:S(2)}) collective-permute-start(f32[72,512]{1,0:T(8,128)} %get-tuple-element.24), channel_id=1, source_target_pairs={{16,1}} | collective-permute-start | bytes 442376 | tf_op jit(solution)/shard_map/ppermute | solution.py:775
  12.0 1.1 %copy-start = (bf16[6,4,32,512]{3,2,1,0:T(8,128)(2,1)S(1)}, bf16[6,4,32,512]{3,2,1,0:T(8,128)(2,1)}, u32[]{:S(2)}) copy-start(bf16[6,4,32,512]{3,2,1,0:T(8,128)(2,1)} %tensor.3) | copy-start | bytes 2359300
  13.2 1.1 %copy-start.1 = (bf16[640,512]{1,0:T(8,128)(2,1)S(1)}, bf16[640,512]{1,0:T(8,128)(2,1)}, u32[]{:S(2)}) copy-start(bf16[640,512]{1,0:T(8,128)(2,1)} %constant.8.clone.table_at) | copy-start | bytes 1966084
  21.0 4.6 %copy-start.2 = (f32[3,32,2,128]{3,2,1,0:T(2,128)S(1)}, f32[3,32,2,128]{3,2,1,0:T(2,128)}, u32[]{:S(2)}) copy-start(f32[3,32,2,128]{3,2,1,0:T(2,128)} %param.11) | copy-start | bytes 294916
  21.0 4.6 %copy-start.4 = (s32[32,2,128]{2,1,0:T(2,128)S(1)}, s32[32,2,128]{2,1,0:T(2,128)}, u32[]{:S(2)}) copy-start(s32[32,2,128]{2,1,0:T(2,128)} %param.12) | copy-start | bytes 98308
  21.0 9.5 %copy-start.3 = (s32[32,2,128]{2,1,0:T(2,128)S(1)}, s32[32,2,128]{2,1,0:T(2,128)}, u32[]{:S(2)}) copy-start(s32[32,2,128]{2,1,0:T(2,128)} %param.13) | copy-start | bytes 98308
  21.0 9.5 %copy-start.5 = (bf16[64,384]{1,0:T(8,128)(2,1)S(1)}, bf16[64,384]{1,0:T(8,128)(2,1)}, u32[]{:S(2)}) copy-start(bf16[64,384]{1,0:T(8,128)(2,1)} %constant.7.clone.table) | copy-start | bytes 147460
  21.0 9.5 %copy-start.6 = (f32[4]{0:T(128)S(1)}, f32[4]{0:T(128)}, u32[]{:S(2)}) copy-start(f32[4]{0:T(128)} %saturation.1) | copy-start | bytes 52
  21.0 9.5 %copy-start.7 = (f32[4]{0:T(128)S(1)}, f32[4]{0:T(128)}, u32[]{:S(2)}) copy-start(f32[4]{0:T(128)} %anisotropy.1) | copy-start | bytes 52
  21.0 9.5 %copy-start.8 = (f32[4]{0:T(128)S(1)}, f32[4]{0:T(128)}, u32[]{:S(2)}) copy-start(f32[4]{0:T(128)} %damping.1) | copy-start | bytes 52
  21.0 9.5 %copy-start.9 = (f32[3]{0:T(128)S(1)}, f32[3]{0:T(128)}, u32[]{:S(2)}) copy-start(f32[3]{0:T(128)} %applied.1) | copy-start | bytes 40
  22.7 12.5 %all-to-all-start.1 = ((f32[32,3,4,128]{3,2,1,0:T(4,128)}), f32[32,3,4,128]{3,2,1,0:T(4,128)S(1)}, u32[]{:S(2)}, u32[]{:S(2)}) async-start(f32[32,3,4,128]{3,2,1,0:T(4,128)} %bitcast.5), calls=%async_computation.1 | async-start | bytes 393216 | tf_op jit(solution)/shard_map/all_to_all | solution.py:806
  25.7 4.7 %collective-permute-start.4 = (f32[96,128]{1,0:T(8,128)S(1)}, f32[96,128]{1,0:T(8,128)S(1)}, u32[]{:S(2)}, u32[]{:S(2)}) collective-permute-start(f32[96,128]{1,0:T(8,128)S(1)} %get-tuple-element.28), channel_id=1, source_target_pairs={{2,0},{0,2},{6,4},{4,6},{10,8},{8,10},{14,12},{12,14},{18,16},{16,... | collective-permute-start | bytes 147464 | tf_op jit(solution)/shard_map/ppermute | solution.py:785
  26.0 4.4 %collective-permute-start.5 = (f32[96,128]{1,0:T(8,128)S(1)}, f32[96,128]{1,0:T(8,128)S(1)}, u32[]{:S(2)}, u32[]{:S(2)}) collective-permute-start(f32[96,128]{1,0:T(8,128)S(1)} %get-tuple-element.29), channel_id=1, source_target_pairs={{2,4},{4,2},{6,8},{8,6},{10,12},{12,10},{14,16},{16,14},{18,20},{2... | collective-permute-start | bytes 147464 | tf_op jit(solution)/shard_map/ppermute | solution.py:787
  26.7 3.7 %collective-permute-start.3 = (f32[8,192]{1,0:T(8,128)S(1)}, f32[8,192]{1,0:T(8,128)S(1)}, u32[]{:S(2)}, u32[]{:S(2)}) collective-permute-start(f32[8,192]{1,0:T(8,128)S(1)} %get-tuple-element.27), channel_id=1, source_target_pairs={{0,1},{1,0},{2,3},{3,2},{4,5},{5,4},{6,7},{7,6},{8,9},{9,8},{10,11... | collective-permute-start | bytes 18440 | tf_op jit(solution)/shard_map/ppermute | solution.py:783
